TPU v7x, 32 devices: a whole 2x2x4 slice. The times are simulated.
32 devices in a mesh: bag: 4 (over x, core), sp: 8 (over z, y).
Axes of the slice: x: 2, y: 2, z: 4, core: 2. Of those that a mesh axis runs over, the one named last changes fastest.
Arguments:
- tokens: bfloat16 [8192, 1152], P(('bag', 'sp')), may hold values from -8 to 8
- row_seq: int32 [8192], P(('bag', 'sp')), may hold values from 0 to 3, as said below
- modulation: float32 [4, 6, 1152], replicated, may hold values from -4 to 4
- w_qkv: bfloat16 [1152, 3456], replicated, may hold values from -1 to 1
- w_out: bfloat16 [1152, 1152], replicated, may hold values from -0.1875 to 0.1875
- w_fc1: bfloat16 [1152, 2304], replicated, may hold values from -0.1875 to 0.1875
- w_fc2: bfloat16 [2304, 1152], replicated, may hold values from -0.125 to 0.125
Outputs:
- output: bfloat16 [8192, 1152], P(('bag', 'sp'))
Inputs may be any that keep to these rules, and one draw needn't show every extreme that they name: `row_seq`: rows 2m and 2m + 1 belong to the same sequence. Sequence s lies in bag s. Of one device's 256 rows at most 80 lie in any one bag, and on every device exactly 80 lie in one bag. Every sequence has rows.
All inputs are finite; a program needn't handle non-finite values.
Results may differ from a plain program's by a relative error of at most 0.0095.
Values may be sent and summed in bfloat16 or wider, within the bound.
No kernel may reach another device: no remote copies, remote signals or barrier semaphores. Data moves between devices by JAX's collectives and lax.ppermute only.
A program may use at most 128 MiB of HBM per device.

v0:
```python
import functools
import math

import jax
import jax.numpy as jnp
from jax import lax
from jax.experimental import pallas as pl
from jax.experimental.pallas import tpu as pltpu
from jax.sharding import PartitionSpec as P


HD = 72
SEQ_BAG = 1
LANE = 128
EPS = 1e-06
HUGE = 1e30
AXES = ("bag", "sp")
BF16, F32 = jnp.bfloat16, jnp.float32


def vmem():
    return pl.BlockSpec(memory_space=pltpu.VMEM)


def smem():
    return pl.BlockSpec(memory_space=pltpu.SMEM)


def hbm():
    return pl.BlockSpec(memory_space=pl.ANY)


def layer_norm(values):
    center = values - jnp.mean(values, axis=-1, keepdims=True)
    spread = jnp.mean(center * center, axis=-1, keepdims=True)
    return center * lax.rsqrt(spread + EPS)


def to_column(row):
    n = row.shape[1]
    diagonal = lax.broadcasted_iota(jnp.int32, (n, n), 0) == lax.broadcasted_iota(jnp.int32, (n, n), 1)
    return jnp.sum(jnp.where(diagonal, jnp.broadcast_to(row, (n, n)), 0.0), axis=1, keepdims=True)


def slot_of_row(bag_row, capacity):
    n = bag_row.shape[1]
    earlier = lax.broadcasted_iota(jnp.int32, (n, n), 0) < lax.broadcasted_iota(jnp.int32, (n, n), 1)
    same = jnp.broadcast_to(to_column(bag_row), (n, n)) == jnp.broadcast_to(bag_row, (n, n))
    rank = jnp.sum(jnp.where(same & earlier, 1.0, 0.0), axis=0, keepdims=True)
    return (bag_row * capacity + rank).astype(jnp.int32)


def slot_kernel(capacity, place_ref, tokens_ref, seq_ref, mod_ref, *out_refs):
    me = place_ref[0]
    row_count, width = tokens_ref.shape
    block_count = len(out_refs)
    bag_row = ((seq_ref[...] // SEQ_BAG) ^ me).astype(F32)
    position = slot_of_row(bag_row, capacity)
    slot_ids = lax.broadcasted_iota(jnp.int32, (block_count * capacity, row_count), 0)
    pick = jnp.where(slot_ids == position, 1.0, 0.0)
    filled = jnp.sum(pick, axis=1, keepdims=True)
    rows = jnp.dot(pick.astype(BF16), tokens_ref[...], preferred_element_type=F32)
    first = lax.broadcasted_iota(jnp.int32, (capacity, width), 1) == 0
    for block, out_ref in enumerate(out_refs):
        part = slice(block * capacity, (block + 1) * capacity)
        mods = mod_ref[block ^ me]
        normed = layer_norm(rows[part]) * (1.0 + mods[1:2]) + mods[0:1]
        normed = jnp.where(first & (filled[part] < 0.5), HUGE, normed)
        out_ref[...] = normed.astype(BF16)


def slot_rows(place, tokens, seq_row, modulation, bag_count, capacity):
    width = tokens.shape[1]
    return pl.pallas_call(
        functools.partial(slot_kernel, capacity),
        in_specs=[smem(), vmem(), vmem(), vmem()],
        out_specs=[vmem()] * bag_count,
        out_shape=[jax.ShapeDtypeStruct((capacity, width), BF16)] * bag_count,
        name="slot_rows",
    )(place, tokens, seq_row, modulation)


def weight_kernel(part, chip_ref, w_ref, out_ref, window, sem):
    total = w_ref.shape[1]
    wide = window.shape[2]
    copies, shifts = [], []
    for kind in range(3):
        start = kind * (total // 3) + chip_ref[0] * part
        base = pl.multiple_of(jnp.minimum(start // LANE * LANE, total - wide), LANE)
        shifts.append(start - base)
        copies.append(
            pltpu.make_async_copy(w_ref.at[:, pl.ds(base, wide)], window.at[kind], sem.at[kind])
        )
    for copy in copies:
        copy.start()
    pieces = []
    for kind, copy in enumerate(copies):
        copy.wait()
        rolled = pltpu.roll(window[kind].astype(F32), wide - shifts[kind], axis=1)
        pieces.append(rolled[:, :part].astype(BF16))
    filler = out_ref.shape[1] - 3 * part
    if filler:
        pieces.append(jnp.zeros((w_ref.shape[0], filler), BF16))
    out_ref[...] = jnp.concatenate(pieces, axis=1)


def round_up(value, unit):
    return -(-value // unit) * unit


def chip_weights(chip, w_qkv, head_count):
    depth, part = w_qkv.shape[0], head_count * HD
    wide = round_up(part + LANE - math.gcd(part, LANE), LANE)
    return pl.pallas_call(
        functools.partial(weight_kernel, part),
        in_specs=[smem(), hbm()],
        out_specs=vmem(),
        out_shape=jax.ShapeDtypeStruct((depth, round_up(3 * part, LANE)), BF16),
        scratch_shapes=[pltpu.VMEM((3, depth, wide), BF16), pltpu.SemaphoreType.DMA((3,))],
        cost_estimate=pl.CostEstimate(flops=10**9, bytes_accessed=10**7, transcendentals=0),
        name="chip_weights",
    )(chip, w_qkv)


def project_kernel(head_count, *refs):
    w_ref, (q_ref, kv_ref) = refs[-3], refs[-2:]
    rows = jnp.concatenate([ref[...] for ref in refs[:-3]], axis=0)
    size = rows.shape[0]
    factor = math.log2(math.e) / math.sqrt(HD)
    empty = rows[:, :1].astype(F32) > 0.5 * HUGE
    start = jnp.where(empty, 0.0, rows[:, :LANE].astype(F32)).astype(BF16)
    rows = jnp.concatenate([start, rows[:, LANE:]], axis=1)
    made = jnp.dot(rows, w_ref[...], preferred_element_type=F32)
    lane = lax.broadcasted_iota(jnp.int32, (size, LANE), 1)
    bias = jnp.where(empty, -HUGE, 0.0)
    for kind in range(3):
        for head in range(head_count):
            column = (kind * head_count + head) * HD
            base, shift = column // LANE * LANE, column % LANE
            wide = LANE if shift + HD <= LANE else 2 * LANE
            value = made[:, base : base + wide]
            if shift:
                value = pltpu.roll(value, wide - shift, axis=1)
            value = value[:, :LANE]
            if kind == 0:
                value, beside = value * factor, 1.0
            else:
                beside = bias if kind == 1 else 1.0
            value = jnp.where(lane < HD, value, jnp.where(lane == HD, beside, 0.0)).astype(BF16)
            if kind == 0:
                q_ref[head] = value
            else:
                kv_ref[kind - 1, head] = value


def project(parts, weights, head_count):
    size, depth = sum(part.shape[0] for part in parts), weights.shape[0]
    return pl.pallas_call(
        functools.partial(project_kernel, head_count),
        in_specs=[vmem()] * (len(parts) + 1),
        out_specs=[vmem(), vmem()],
        out_shape=[
            jax.ShapeDtypeStruct((head_count, size, LANE), BF16),
            jax.ShapeDtypeStruct((2, head_count, size, LANE), BF16),
        ],
        cost_estimate=pl.CostEstimate(
            flops=2 * size * depth * weights.shape[1], bytes_accessed=4 * size * depth, transcendentals=0
        ),
        name="project",
    )(*parts, weights)


def packed_rows(capacity, width):
    whole = width // LANE
    rest = width - whole * LANE
    if rest == 0:
        return whole * capacity, 0, 0
    if capacity % 16:
        return (whole + 1) * capacity, rest, capacity
    groups = LANE // rest
    tiles = -(-(capacity // 16) // groups)
    return whole * capacity + tiles * 16, rest, 16


def pack(block, write):
    capacity, width = block.shape
    whole = width // LANE
    for tile in range(whole):
        write(tile * capacity, block[:, tile * LANE : (tile + 1) * LANE])
    _, rest, size = packed_rows(capacity, width)
    if rest == 0:
        return
    tail = block[:, whole * LANE :]
    groups = 1 if size == capacity else LANE // rest
    for first in range(0, capacity // size, groups):
        pieces = [
            tail[group * size : (group + 1) * size]
            for group in range(first, min(first + groups, capacity // size))
        ]
        filler = LANE - rest * len(pieces)
        if filler:
            pieces.append(jnp.zeros((size, filler), block.dtype))
        write(whole * capacity + first // groups * size, jnp.concatenate(pieces, axis=1))


def unpack(packed, capacity, width):
    whole = width // LANE
    columns = [packed[tile * capacity : (tile + 1) * capacity] for tile in range(whole)]
    _, rest, size = packed_rows(capacity, width)
    if rest:
        groups = 1 if size == capacity else LANE // rest
        pieces = []
        for group in range(capacity // size):
            top = whole * capacity + group // groups * size
            left = group % groups * rest
            pieces.append(packed[top : top + size, left : left + rest])
        columns.append(jnp.concatenate(pieces, axis=0))
    return jnp.concatenate(columns, axis=1)


def attend_kernel(chips, capacity, piece_count, *refs):
    q_ref, pieces, out_ref = refs[0], refs[1 : 1 + piece_count], refs[1 + piece_count]
    if piece_count > 1:
        kv_ref = refs[2 + piece_count]
        at = 0
        for ref in pieces:
            kv_ref[:, :, at : at + ref.shape[2]] = ref[...]
            at += ref.shape[2]
    else:
        kv_ref = pieces[0]
    nt = (((1,), (1,)), ((), ()))
    results = []
    for head in range(q_ref.shape[0]):
        score = lax.dot_general(q_ref[head], kv_ref[0, head], nt, preferred_element_type=F32)
        top = jnp.max(score, axis=1, keepdims=True)
        probs = jnp.exp2(score - top).astype(BF16)
        mixed = jnp.dot(probs, kv_ref[1, head], preferred_element_type=F32)
        results.append(mixed[:, :HD] / mixed[:, HD : HD + 1])
    rows = jnp.concatenate(results, axis=1).astype(BF16)
    for chip in range(chips):
        block = rows[chip * capacity : (chip + 1) * capacity]

        def write(first, value):
            out_ref[chip, first : first + value.shape[0]] = value

        pack(block, write)


def attend(queries, pieces, chips, capacity):
    head_count = queries.shape[0]
    keys = sum(piece.shape[2] for piece in pieces)
    out_rows = packed_rows(capacity, head_count * HD)[0]
    out_shape = [jax.ShapeDtypeStruct((chips, out_rows, LANE), BF16)]
    if len(pieces) > 1:
        out_shape.append(jax.ShapeDtypeStruct((2, head_count, keys, LANE), BF16))
    made = pl.pallas_call(
        functools.partial(attend_kernel, chips, capacity, len(pieces)),
        in_specs=[vmem()] * (1 + len(pieces)),
        out_specs=[vmem()] * len(out_shape),
        out_shape=out_shape,
        cost_estimate=pl.CostEstimate(
            flops=4 * head_count * queries.shape[1] * keys * LANE,
            bytes_accessed=4 * head_count * keys * LANE,
            transcendentals=head_count * queries.shape[1] * keys,
        ),
        name="attend",
    )(queries, *pieces)
    return made[0], (made[1] if len(pieces) > 1 else pieces[0])


def finish_kernel(capacity, chips, place_ref, tokens_ref, seq_ref, mod_ref, w_out, w_fc1, w_fc2, *refs):
    parts, out_ref, whole = refs[:chips], refs[chips], refs[chips + 1]
    row_count, width = tokens_ref.shape
    for index, part in enumerate(parts):
        whole[place_ref[1] ^ index] = part[...]
    bags = parts[0].shape[0]
    seq_row = seq_ref[...]
    position = slot_of_row(((seq_row // SEQ_BAG) ^ place_ref[0]).astype(F32), capacity)
    slot_ids = lax.broadcasted_iota(jnp.int32, (bags * capacity, row_count), 0)
    pick = jnp.where(slot_ids == position, 1.0, 0.0).astype(BF16)
    seq_column = to_column(seq_row.astype(F32))
    slots = jnp.concatenate(
        [
            jnp.concatenate(
                [unpack(whole[chip, bag], capacity, width // chips) for chip in range(chips)], axis=1
            )
            for bag in range(bags)
        ],
        axis=0,
    )
    tn = (((0,), (0,)), ((), ()))
    attended = lax.dot_general(pick, slots, tn, preferred_element_type=F32).astype(BF16)

    def per_row(column):
        value = jnp.broadcast_to(mod_ref[0, column : column + 1], (row_count, width))
        for seq in range(1, mod_ref.shape[0]):
            value = jnp.where(seq_column == seq, mod_ref[seq, column : column + 1], value)
        return value

    branch = jnp.dot(attended, w_out[...], preferred_element_type=F32)
    hidden = (tokens_ref[...].astype(F32) + per_row(2) * branch).astype(BF16)
    normed = (layer_norm(hidden.astype(F32)) * (1.0 + per_row(4)) + per_row(3)).astype(BF16)
    active = jax.nn.gelu(jnp.dot(normed, w_fc1[...], preferred_element_type=F32), approximate=True)
    last = jnp.dot(active.astype(BF16), w_fc2[...], preferred_element_type=F32)
    out_ref[...] = (hidden.astype(F32) + per_row(5) * last).astype(BF16)


def finish(place, tokens, seq_row, modulation, parts, w_out, w_fc1, w_fc2, capacity):
    chips = len(parts)
    return pl.pallas_call(
        functools.partial(finish_kernel, capacity, chips),
        in_specs=[smem()] + [vmem()] * (6 + chips),
        out_specs=vmem(),
        out_shape=jax.ShapeDtypeStruct(tokens.shape, BF16),
        scratch_shapes=[pltpu.VMEM((chips,) + parts[0].shape, BF16)],
        name="finish",
    )(place, tokens, seq_row, modulation, w_out, w_fc1, w_fc2, *parts)


def layer(tokens, row_seq, modulation, w_qkv, w_out, w_fc1, w_fc2):
    bags, sp = lax.axis_size("bag"), lax.axis_size("sp")
    along, across, cores = sp // bags, bags // 2, 2
    chips = across * along
    row_count, width = tokens.shape
    capacity = row_count // bags * 5 // 4
    head_count = width // HD // chips
    my_bag, my_sp = lax.axis_index("bag"), lax.axis_index("sp")
    my_x, my_z, my_y = my_bag // cores, my_sp // along, my_sp % along

    def swap(value, dx=0, core=0, dz=0, dy=0):
        pairs = []
        for b in range(bags):
            for s in range(sp):
                b2 = ((b // cores) ^ dx) * cores + ((b % cores) ^ core)
                s2 = ((s // along) ^ dz) * along + ((s % along) ^ dy)
                pairs.append((b * sp + s, b2 * sp + s2))
        return lax.ppermute(value, AXES, pairs)

    seq_row = row_seq.reshape(1, row_count)
    place = jnp.stack([my_z, my_x * along + my_y]).astype(jnp.int32)
    blocks = slot_rows(place, tokens, seq_row, modulation, bags, capacity)
    weights = chip_weights(place[1:], w_qkv, head_count)
    blocks = [block if k == 0 else swap(block, dz=k) for k, block in enumerate(blocks)]
    half = round_up(capacity, 32) // 2
    queries, pieces = [], []
    for block in blocks:
        if across == 2 and along == 2:
            from_x, from_y = swap(block, dx=1), swap(block, dy=1)
            upper, lower = swap(from_x[:half], dy=1), swap(from_y[half:], dx=1)
            parts = [block, from_y, from_x, upper, lower]
        else:
            parts = [swap(block, dx=j // along, dy=j % along) if j else block for j in range(chips)]
        query, kv = project(parts, weights, head_count)
        queries.append(query)
        pieces += [kv, swap(kv, core=1)]
    mixed = [None] * bags
    for k in reversed(range(bags)):
        part, kv = attend(queries[k], pieces, chips, capacity)
        pieces = [kv]
        mixed[k] = swap(part, dz=k) if k else part
    shares = []
    for j in range(chips):
        share = jnp.stack([part[j] for part in mixed])
        shares.append(swap(share, dx=j // along, dy=j % along) if j else share)
    return finish(place, tokens, seq_row, modulation, shares, w_out, w_fc1, w_fc2, capacity)


def solution(mesh):
    placed = (P(("bag", "sp"), None), P(("bag", "sp")), P(), P(), P(), P(), P())
    return jax.shard_map(
        layer, mesh=mesh, in_specs=placed, out_specs=P(("bag", "sp"), None), check_vma=False
    )
```

profile of v0, /device:TPU:0, one launch (start us, length us, event | category | flops | bytes accessed | tf_op | source)
XLA Modules:
  0.0 145.7 jit_solution(15192434914818692682)
XLA Ops:
  2.2 2.7 %slot_rows.1 = (bf16[80,1152]{1,0:T(8,128)(2,1)}, bf16[80,1152]{1,0:T(8,128)(2,1)}, bf16[80,1152]{1,0:T(8,128)(2,1)}, bf16[80,1152]{1,0:T(8,128)(2,1)}) custom-call(s32[2]{0:T(128)} %pad_add_fusion.place_ref, bf16[256,1152]{1,0:T(8,128)(2,1)} %tokens_ref.3, s32[1,256]{1,0:T(1,128)} %bitcast.3, f32[4,6,1152]{2,1,0:T(8,128)} %copy.9.mod_ref), custom_call_target="tpu_custom_call" | custom-call | tf_op jit(solution)/shard_map/slot_rows/pallas_call | solution.py:74
  4.9 5.1 %collective-permute-start.4 = (bf16[80,1152]{1,0:T(8,128)(2,1)}, bf16[80,1152]{1,0:T(8,128)(2,1)S(1)}, u32[]{:S(2)}, u32[]{:S(2)}) collective-permute-start(bf16[80,1152]{1,0:T(8,128)(2,1)} %get-tuple-element.21), channel_id=1, source_target_pairs={{0,6},{1,7},{2,4},{3,5},{4,2},{5,3},{6,0},{7,1},{8,14},{9,15},{10,... | collective-permute-start | bytes 552968 | tf_op jit(solution)/shard_map/ppermute | solution.py:337
  17.4 2.4 %collective-permute-done.10.refs_0_ = bf16[80,1152]{1,0:T(8,128)(2,1)S(1)} collective-permute-done((bf16[80,1152]{1,0:T(8,128)(2,1)}, bf16[80,1152]{1,0:T(8,128)(2,1)S(1)}, u32[]{:S(2)}, u32[]{:S(2)}) %collective-permute-start.10) | collective-permute-done | bytes 184352 | tf_op jit(solution)/shard_map/ppermute | solution.py:337
  21.3 4.5 %collective-permute-done.16.refs_0_ = bf16[80,1152]{1,0:T(8,128)(2,1)S(1)} collective-permute-done((bf16[80,1152]{1,0:T(8,128)(2,1)}, bf16[80,1152]{1,0:T(8,128)(2,1)S(1)}, u32[]{:S(2)}, u32[]{:S(2)}) %collective-permute-start.16) | collective-permute-done | bytes 184352 | tf_op jit(solution)/shard_map/ppermute | solution.py:337
  29.5 3.8 %collective-permute-done.3.refs_4_ = bf16[32,1152]{1,0:T(8,128)(2,1)S(1)} collective-permute-done((bf16[32,1152]{1,0:T(8,128)(2,1)S(1)}, bf16[32,1152]{1,0:T(8,128)(2,1)S(1)}, u32[]{:S(2)}, u32[]{:S(2)}) %collective-permute-start.3) | collective-permute-done | bytes 73760 | tf_op jit(solution)/shard_map/ppermute | solution.py:337
  39.0 4.5 %chip_weights.1.refs_5_ = bf16[1152,896]{1,0:T(8,128)(2,1)} custom-call(s32[1]{0:T(128)} %bitcast.1.chip_ref, bf16[1152,3456]{1,0:T(8,128)(2,1)} %w_ref.1), custom_call_target="tpu_custom_call" | custom-call | flops 1000000000 | bytes 10000000 | tf_op jit(solution)/shard_map/chip_weights/pallas_call | solution.py:114
  45.6 3.9 %project.4 = (bf16[4,320,128]{2,1,0:T(8,128)(2,1)}, bf16[2,4,320,128]{3,2,1,0:T(8,128)(2,1)}) custom-call(bf16[80,1152]{1,0:T(8,128)(2,1)} %get-tuple-element.19.refs_0_, bf16[80,1152]{1,0:T(8,128)(2,1)} %copy-done.7, bf16[80,1152]{1,0:T(8,128)(2,1)} %copy-done.3, bf16[48,1152]{1,0:T(8,128)(2,1)} %copy-done.17, bf16[32,1152]{1,0:T(8,128)(2,1)} %copy-done.18, ...), custom_call_target="tpu_custom_call" | custom-call | flops 660602880 | bytes 1474560 | tf_op jit(solution)/shard_map/project/pallas_call | solution.py:158
  52.0 3.9 %project.5 = (bf16[4,320,128]{2,1,0:T(8,128)(2,1)}, bf16[2,4,320,128]{3,2,1,0:T(8,128)(2,1)}) custom-call(bf16[80,1152]{1,0:T(8,128)(2,1)} %copy-done.13, bf16[80,1152]{1,0:T(8,128)(2,1)} %copy-done.6, bf16[80,1152]{1,0:T(8,128)(2,1)} %copy-done.2, bf16[48,1152]{1,0:T(8,128)(2,1)} %copy-done.15, bf16[32,1152]{1,0:T(8,128)(2,1)} %copy-done.20, ...), custom_call_target="tpu_custom_call" | custom-call | flops 660602880 | bytes 1474560 | tf_op jit(solution)/shard_map/project/pallas_call | solution.py:158
  57.1 3.9 %project.6 = (bf16[4,320,128]{2,1,0:T(8,128)(2,1)}, bf16[2,4,320,128]{3,2,1,0:T(8,128)(2,1)}) custom-call(bf16[80,1152]{1,0:T(8,128)(2,1)} %copy-done.12, bf16[80,1152]{1,0:T(8,128)(2,1)} %copy-done.4, bf16[80,1152]{1,0:T(8,128)(2,1)} %copy-done, bf16[48,1152]{1,0:T(8,128)(2,1)} %copy-done.14, bf16[32,1152]{1,0:T(8,128)(2,1)} %copy-done.19, ...), custom_call_target="tpu_custom_call" | custom-call | flops 660602880 | bytes 1474560 | tf_op jit(solution)/shard_map/project/pallas_call | solution.py:158
  62.5 4.0 %project.7 = (bf16[4,320,128]{2,1,0:T(8,128)(2,1)}, bf16[2,4,320,128]{3,2,1,0:T(8,128)(2,1)}) custom-call(bf16[80,1152]{1,0:T(8,128)(2,1)} %copy-done.11, bf16[80,1152]{1,0:T(8,128)(2,1)} %copy-done.5, bf16[80,1152]{1,0:T(8,128)(2,1)} %copy-done.1, bf16[48,1152]{1,0:T(8,128)(2,1)} %copy-done.16, bf16[32,1152]{1,0:T(8,128)(2,1)} %copy-done.21, ...), custom_call_target="tpu_custom_call" | custom-call | flops 660602880 | bytes 1474560 | tf_op jit(solution)/shard_map/project/pallas_call | solution.py:158
  66.9 2.1 %collective-permute-done.21.refs_6_ = bf16[2,4,320,128]{3,2,1,0:T(8,128)(2,1)} collective-permute-done((bf16[2,4,320,128]{3,2,1,0:T(8,128)(2,1)}, bf16[2,4,320,128]{3,2,1,0:T(8,128)(2,1)}, u32[]{:S(2)}, u32[]{:S(2)}) %collective-permute-start.21) | collective-permute-done | bytes 655392 | tf_op jit(solution)/shard_map/ppermute | solution.py:337
  69.0 9.5 %attend.4 = (bf16[4,192,128]{2,1,0:T(8,128)(2,1)}, bf16[2,4,2560,128]{3,2,1,0:T(8,128)(2,1)}) custom-call(bf16[4,320,128]{2,1,0:T(8,128)(2,1)} %get-tuple-element.22.refs_0_, bf16[2,4,320,128]{3,2,1,0:T(8,128)(2,1)} %get-tuple-element.23.refs_1_, bf16[2,4,320,128]{3,2,1,0:T(8,128)(2,1)} %copy-done.22, bf16[2,4,320,128]{3,2,1,0:T(8,128)(2,1)} %get-tuple-element.25.refs_3_, ...), custom_call_target="tpu_custom_call" | custom-call | flops 1677721600 | bytes 5242880 | tf_op jit(solution)/shard_map/attend/pallas_call | solution.py:256
  78.5 8.1 %attend.7 = bf16[4,192,128]{2,1,0:T(8,128)(2,1)} custom-call(bf16[4,320,128]{2,1,0:T(8,128)(2,1)} %get-tuple-element.31.refs_0_, bf16[2,4,2560,128]{3,2,1,0:T(8,128)(2,1)} %get-tuple-element.29.refs_1_), custom_call_target="tpu_custom_call" | custom-call | flops 1677721600 | bytes 5242880 | tf_op jit(solution)/shard_map/attend/pallas_call | solution.py:256
  86.6 8.1 %attend.6 = bf16[4,192,128]{2,1,0:T(8,128)(2,1)} custom-call(bf16[4,320,128]{2,1,0:T(8,128)(2,1)} %get-tuple-element.30.refs_0_, bf16[2,4,2560,128]{3,2,1,0:T(8,128)(2,1)} %get-tuple-element.29.refs_1_), custom_call_target="tpu_custom_call" | custom-call | flops 1677721600 | bytes 5242880 | tf_op jit(solution)/shard_map/attend/pallas_call | solution.py:256
  94.7 8.4 %attend.5 = bf16[4,192,128]{2,1,0:T(8,128)(2,1)} custom-call(bf16[4,320,128]{2,1,0:T(8,128)(2,1)} %get-tuple-element.20.refs_0_, bf16[2,4,2560,128]{3,2,1,0:T(8,128)(2,1)} %get-tuple-element.29.refs_1_), custom_call_target="tpu_custom_call" | custom-call | flops 1677721600 | bytes 5242880 | tf_op jit(solution)/shard_map/attend/pallas_call | solution.py:256
  103.1 2.3 %collective-permute-start.25 = (bf16[4,192,128]{2,1,0:T(8,128)(2,1)S(1)}, bf16[4,192,128]{2,1,0:T(8,128)(2,1)S(1)}, u32[]{:S(2)}, u32[]{:S(2)}) collective-permute-start(bf16[4,192,128]{2,1,0:T(8,128)(2,1)S(1)} %copy-done.26), channel_id=1, source_target_pairs={{0,6},{1,7},{2,4},{3,5},{4,2},{5,3},{6,0},{7,1},{8,14},{9,15},{10,... | collective-permute-start | bytes 589832 | tf_op jit(solution)/shard_map/ppermute | solution.py:337
  105.4 2.1 %collective-permute-start.24 = (bf16[4,192,128]{2,1,0:T(8,128)(2,1)S(1)}, bf16[4,192,128]{2,1,0:T(8,128)(2,1)S(1)}, u32[]{:S(2)}, u32[]{:S(2)}) collective-permute-start(bf16[4,192,128]{2,1,0:T(8,128)(2,1)S(1)} %copy-done.25), channel_id=1, source_target_pairs={{0,4},{1,5},{2,6},{3,7},{4,0},{5,1},{6,2},{7,3},{8,12},{9,13},{10,... | collective-permute-start | bytes 589832 | tf_op jit(solution)/shard_map/ppermute | solution.py:337
  108.4 4.4 %collective-permute-done.25 = bf16[4,192,128]{2,1,0:T(8,128)(2,1)S(1)} collective-permute-done((bf16[4,192,128]{2,1,0:T(8,128)(2,1)S(1)}, bf16[4,192,128]{2,1,0:T(8,128)(2,1)S(1)}, u32[]{:S(2)}, u32[]{:S(2)}) %collective-permute-start.25) | collective-permute-done | bytes 196640 | tf_op jit(solution)/shard_map/ppermute | solution.py:337
  112.8 6.7 %collective-permute-done.23 = bf16[4,192,128]{2,1,0:T(8,128)(2,1)S(1)} collective-permute-done((bf16[4,192,128]{2,1,0:T(8,128)(2,1)S(1)}, bf16[4,192,128]{2,1,0:T(8,128)(2,1)S(1)}, u32[]{:S(2)}, u32[]{:S(2)}) %collective-permute-start.23) | collective-permute-done | bytes 196640 | tf_op jit(solution)/shard_map/ppermute | solution.py:337
  119.5 2.3 %collective-permute-done.24 = bf16[4,192,128]{2,1,0:T(8,128)(2,1)S(1)} collective-permute-done((bf16[4,192,128]{2,1,0:T(8,128)(2,1)S(1)}, bf16[4,192,128]{2,1,0:T(8,128)(2,1)S(1)}, u32[]{:S(2)}, u32[]{:S(2)}) %collective-permute-start.24) | collective-permute-done | bytes 196640 | tf_op jit(solution)/shard_map/ppermute | solution.py:337
  126.2 2.4 %collective-permute-done.26.refs_1_ = bf16[4,192,128]{2,1,0:T(8,128)(2,1)S(1)} collective-permute-done((bf16[4,192,128]{2,1,0:T(8,128)(2,1)S(1)}, bf16[4,192,128]{2,1,0:T(8,128)(2,1)S(1)}, u32[]{:S(2)}, u32[]{:S(2)}) %collective-permute-start.26) | collective-permute-done | bytes 196640 | tf_op jit(solution)/shard_map/ppermute | solution.py:337
  128.6 2.0 %collective-permute-done.27.refs_2_ = bf16[4,192,128]{2,1,0:T(8,128)(2,1)S(1)} collective-permute-done((bf16[4,192,128]{2,1,0:T(8,128)(2,1)S(1)}, bf16[4,192,128]{2,1,0:T(8,128)(2,1)S(1)}, u32[]{:S(2)}, u32[]{:S(2)}) %collective-permute-start.27) | collective-permute-done | bytes 196640 | tf_op jit(solution)/shard_map/ppermute | solution.py:337
  130.6 3.0 %collective-permute-done.28.refs_3_ = bf16[4,192,128]{2,1,0:T(8,128)(2,1)S(1)} collective-permute-done((bf16[4,192,128]{2,1,0:T(8,128)(2,1)S(1)}, bf16[4,192,128]{2,1,0:T(8,128)(2,1)S(1)}, u32[]{:S(2)}, u32[]{:S(2)}) %collective-permute-start.28) | collective-permute-done | bytes 196640 | tf_op jit(solution)/shard_map/ppermute | solution.py:337
  134.3 11.4 %finish.1 = bf16[256,1152]{1,0:T(8,128)(2,1)} custom-call(s32[2]{0:T(128)} %pad_add_fusion.place_ref, bf16[256,1152]{1,0:T(8,128)(2,1)} %tokens_ref.3, s32[1,256]{1,0:T(1,128)} %bitcast.4, f32[4,6,1152]{2,1,0:T(8,128)} %copy.9.mod_ref, bf16[1152,1152]{1,0:T(8,128)(2,1)} %w_out.1, bf16[1152,2304]{1,0:T(8,128)(2,1)} %w_fc1.1, bf16[2304,1152]{1,0:T(8,128)(2,1)} %w_fc2.1, ...), custom_call_target="tpu_custom_call" | custom-call | tf_op jit(solution)/shard_map/finish/pallas_call | solution.py:310
  (119 shorter events, 33.9 us)
Async XLA Ops:
  4.9 10.8 %collective-permute-start.4 = (bf16[80,1152]{1,0:T(8,128)(2,1)}, bf16[80,1152]{1,0:T(8,128)(2,1)S(1)}, u32[]{:S(2)}, u32[]{:S(2)}) collective-permute-start(bf16[80,1152]{1,0:T(8,128)(2,1)} %get-tuple-element.21), channel_id=1, source_target_pairs={{0,6},{1,7},{2,4},{3,5},{4,2},{5,3},{6,0},{7,1},{8,14},{9,15},{10,... | collective-permute-start | bytes 552968 | tf_op jit(solution)/shard_map/ppermute | solution.py:337
  10.0 9.9 %collective-permute-start.10 = (bf16[80,1152]{1,0:T(8,128)(2,1)}, bf16[80,1152]{1,0:T(8,128)(2,1)S(1)}, u32[]{:S(2)}, u32[]{:S(2)}) collective-permute-start(bf16[80,1152]{1,0:T(8,128)(2,1)} %get-tuple-element.24), channel_id=1, source_target_pairs={{0,2},{1,3},{2,0},{3,1},{4,6},{5,7},{6,4},{7,5},{8,10},{9,11},{10,... | collective-permute-start | bytes 552968 | tf_op jit(solution)/shard_map/ppermute | solution.py:337
  10.0 15.8 %collective-permute-start.16 = (bf16[80,1152]{1,0:T(8,128)(2,1)}, bf16[80,1152]{1,0:T(8,128)(2,1)S(1)}, u32[]{:S(2)}, u32[]{:S(2)}) collective-permute-start(bf16[80,1152]{1,0:T(8,128)(2,1)} %get-tuple-element.26), channel_id=1, source_target_pairs={{0,4},{1,5},{2,6},{3,7},{4,0},{5,1},{6,2},{7,3},{8,12},{9,13},{10,... | collective-permute-start | bytes 552968 | tf_op jit(solution)/shard_map/ppermute | solution.py:337
  10.6 16.8 %collective-permute-start = (bf16[80,1152]{1,0:T(8,128)(2,1)}, bf16[80,1152]{1,0:T(8,128)(2,1)S(1)}, u32[]{:S(2)}, u32[]{:S(2)}) collective-permute-start(bf16[80,1152]{1,0:T(8,128)(2,1)} %get-tuple-element.19.refs_0_), channel_id=1, source_target_pairs={{0,1},{1,0},{2,3},{3,2},{4,5},{5,4},{6,7},{7,6},{8,9},{9,8},{10,11... | collective-permute-start | bytes 552968 | tf_op jit(solution)/shard_map/ppermute | solution.py:337
  12.3 16.6 %collective-permute-start.1 = (bf16[80,1152]{1,0:T(8,128)(2,1)}, bf16[80,1152]{1,0:T(8,128)(2,1)S(1)}, u32[]{:S(2)}, u32[]{:S(2)}) collective-permute-start(bf16[80,1152]{1,0:T(8,128)(2,1)} %get-tuple-element.19.refs_0_), channel_id=1, source_target_pairs={{0,16},{1,17},{2,18},{3,19},{4,20},{5,21},{6,22},{7,23},{8,24},{9,... | collective-permute-start | bytes 552968 | tf_op jit(solution)/shard_map/ppermute | solution.py:337
  15.8 18.9 %collective-permute-start.6 = (bf16[80,1152]{1,0:T(8,128)(2,1)S(1)}, bf16[80,1152]{1,0:T(8,128)(2,1)S(1)}, u32[]{:S(2)}, u32[]{:S(2)}) collective-permute-start(bf16[80,1152]{1,0:T(8,128)(2,1)S(1)} %collective-permute-done.4.refs_0_), channel_id=1, source_target_pairs={{0,16},{1,17},{2,18},{3,19},{4,20},{5,21},{6,22},{7,23},{8,24},{9,... | collective-permute-start | bytes 552968 | tf_op jit(solution)/shard_map/ppermute | solution.py:337
  19.9 16.3 %collective-permute-start.5 = (bf16[80,1152]{1,0:T(8,128)(2,1)S(1)}, bf16[80,1152]{1,0:T(8,128)(2,1)S(1)}, u32[]{:S(2)}, u32[]{:S(2)}) collective-permute-start(bf16[80,1152]{1,0:T(8,128)(2,1)S(1)} %collective-permute-done.4.refs_0_), channel_id=1, source_target_pairs={{0,1},{1,0},{2,3},{3,2},{4,5},{5,4},{6,7},{7,6},{8,9},{9,8},{10,11... | collective-permute-start | bytes 552968 | tf_op jit(solution)/shard_map/ppermute | solution.py:337
  25.9 10.9 %collective-permute-start.12 = (bf16[80,1152]{1,0:T(8,128)(2,1)S(1)}, bf16[80,1152]{1,0:T(8,128)(2,1)S(1)}, u32[]{:S(2)}, u32[]{:S(2)}) collective-permute-start(bf16[80,1152]{1,0:T(8,128)(2,1)S(1)} %collective-permute-done.10.refs_0_), channel_id=1, source_target_pairs={{0,16},{1,17},{2,18},{3,19},{4,20},{5,21},{6,22},{7,23},{8,24},{9,... | collective-permute-start | bytes 552968 | tf_op jit(solution)/shard_map/ppermute | solution.py:337
  27.4 11.1 %collective-permute-start.11 = (bf16[80,1152]{1,0:T(8,128)(2,1)S(1)}, bf16[80,1152]{1,0:T(8,128)(2,1)S(1)}, u32[]{:S(2)}, u32[]{:S(2)}) collective-permute-start(bf16[80,1152]{1,0:T(8,128)(2,1)S(1)} %collective-permute-done.10.refs_0_), channel_id=1, source_target_pairs={{0,1},{1,0},{2,3},{3,2},{4,5},{5,4},{6,7},{7,6},{8,9},{9,8},{10,11... | collective-permute-start | bytes 552968 | tf_op jit(solution)/shard_map/ppermute | solution.py:337
  33.3 11.2 %collective-permute-start.18 = (bf16[80,1152]{1,0:T(8,128)(2,1)S(1)}, bf16[80,1152]{1,0:T(8,128)(2,1)S(1)}, u32[]{:S(2)}, u32[]{:S(2)}) collective-permute-start(bf16[80,1152]{1,0:T(8,128)(2,1)S(1)} %collective-permute-done.16.refs_0_), channel_id=1, source_target_pairs={{0,16},{1,17},{2,18},{3,19},{4,20},{5,21},{6,22},{7,23},{8,24},{9,... | collective-permute-start | bytes 552968 | tf_op jit(solution)/shard_map/ppermute | solution.py:337
  34.7 14.9 %collective-permute-start.17 = (bf16[80,1152]{1,0:T(8,128)(2,1)S(1)}, bf16[80,1152]{1,0:T(8,128)(2,1)S(1)}, u32[]{:S(2)}, u32[]{:S(2)}) collective-permute-start(bf16[80,1152]{1,0:T(8,128)(2,1)S(1)} %collective-permute-done.16.refs_0_), channel_id=1, source_target_pairs={{0,1},{1,0},{2,3},{3,2},{4,5},{5,4},{6,7},{7,6},{8,9},{9,8},{10,11... | collective-permute-start | bytes 552968 | tf_op jit(solution)/shard_map/ppermute | solution.py:337
  36.8 14.5 %collective-permute-start.7 = (bf16[48,1152]{1,0:T(8,128)(2,1)S(1)}, bf16[48,1152]{1,0:T(8,128)(2,1)S(1)}, u32[]{:S(2)}, u32[]{:S(2)}) collective-permute-start(bf16[48,1152]{1,0:T(8,128)(2,1)S(1)} %slice.98), channel_id=1, source_target_pairs={{0,1},{1,0},{2,3},{3,2},{4,5},{5,4},{6,7},{7,6},{8,9},{9,8},{10,11... | collective-permute-start | bytes 331784 | tf_op jit(solution)/shard_map/ppermute | solution.py:337
  38.4 11.3 %collective-permute-start.8 = (bf16[32,1152]{1,0:T(8,128)(2,1)S(1)}, bf16[32,1152]{1,0:T(8,128)(2,1)S(1)}, u32[]{:S(2)}, u32[]{:S(2)}) collective-permute-start(bf16[32,1152]{1,0:T(8,128)(2,1)S(1)} %slice.99), channel_id=1, source_target_pairs={{0,16},{1,17},{2,18},{3,19},{4,20},{5,21},{6,22},{7,23},{8,24},{9,... | collective-permute-start | bytes 221192 | tf_op jit(solution)/shard_map/ppermute | solution.py:337
  43.6 12.6 %collective-permute-start.13 = (bf16[48,1152]{1,0:T(8,128)(2,1)S(1)}, bf16[48,1152]{1,0:T(8,128)(2,1)S(1)}, u32[]{:S(2)}, u32[]{:S(2)}) collective-permute-start(bf16[48,1152]{1,0:T(8,128)(2,1)S(1)} %slice.100), channel_id=1, source_target_pairs={{0,1},{1,0},{2,3},{3,2},{4,5},{5,4},{6,7},{7,6},{8,9},{9,8},{10,11... | collective-permute-start | bytes 331784 | tf_op jit(solution)/shard_map/ppermute | solution.py:337
  44.6 11.3 %collective-permute-start.14 = (bf16[32,1152]{1,0:T(8,128)(2,1)S(1)}, bf16[32,1152]{1,0:T(8,128)(2,1)S(1)}, u32[]{:S(2)}, u32[]{:S(2)}) collective-permute-start(bf16[32,1152]{1,0:T(8,128)(2,1)S(1)} %slice.101), channel_id=1, source_target_pairs={{0,16},{1,17},{2,18},{3,19},{4,20},{5,21},{6,22},{7,23},{8,24},{9,... | collective-permute-start | bytes 221192 | tf_op jit(solution)/shard_map/ppermute | solution.py:337
  49.6 17.2 %collective-permute-start.9 = (bf16[2,4,320,128]{3,2,1,0:T(8,128)(2,1)}, bf16[2,4,320,128]{3,2,1,0:T(8,128)(2,1)S(1)}, u32[]{:S(2)}, u32[]{:S(2)}) collective-permute-start(bf16[2,4,320,128]{3,2,1,0:T(8,128)(2,1)} %get-tuple-element.23.refs_1_), channel_id=1, source_target_pairs={{0,8},{1,9},{2,10},{3,11},{4,12},{5,13},{6,14},{7,15},{8,0},{9,1},... | collective-permute-start | bytes 1966088 | tf_op jit(solution)/shard_map/ppermute | solution.py:337
  49.7 11.5 %collective-permute-start.19 = (bf16[48,1152]{1,0:T(8,128)(2,1)S(1)}, bf16[48,1152]{1,0:T(8,128)(2,1)S(1)}, u32[]{:S(2)}, u32[]{:S(2)}) collective-permute-start(bf16[48,1152]{1,0:T(8,128)(2,1)S(1)} %slice.102), channel_id=1, source_target_pairs={{0,1},{1,0},{2,3},{3,2},{4,5},{5,4},{6,7},{7,6},{8,9},{9,8},{10,11... | collective-permute-start | bytes 331784 | tf_op jit(solution)/shard_map/ppermute | solution.py:337
  51.3 9.9 %collective-permute-start.20 = (bf16[32,1152]{1,0:T(8,128)(2,1)S(1)}, bf16[32,1152]{1,0:T(8,128)(2,1)S(1)}, u32[]{:S(2)}, u32[]{:S(2)}) collective-permute-start(bf16[32,1152]{1,0:T(8,128)(2,1)S(1)} %slice.103), channel_id=1, source_target_pairs={{0,16},{1,17},{2,18},{3,19},{4,20},{5,21},{6,22},{7,23},{8,24},{9,... | collective-permute-start | bytes 221192 | tf_op jit(solution)/shard_map/ppermute | solution.py:337
  55.9 11.0 %collective-permute-start.22 = (bf16[2,4,320,128]{3,2,1,0:T(8,128)(2,1)}, bf16[2,4,320,128]{3,2,1,0:T(8,128)(2,1)S(1)}, u32[]{:S(2)}, u32[]{:S(2)}) collective-permute-start(bf16[2,4,320,128]{3,2,1,0:T(8,128)(2,1)} %get-tuple-element.28.refs_7_), channel_id=1, source_target_pairs={{0,8},{1,9},{2,10},{3,11},{4,12},{5,13},{6,14},{7,15},{8,0},{9,1},... | collective-permute-start | bytes 1966088 | tf_op jit(solution)/shard_map/ppermute | solution.py:337
  103.1 9.7 %collective-permute-start.25 = (bf16[4,192,128]{2,1,0:T(8,128)(2,1)S(1)}, bf16[4,192,128]{2,1,0:T(8,128)(2,1)S(1)}, u32[]{:S(2)}, u32[]{:S(2)}) collective-permute-start(bf16[4,192,128]{2,1,0:T(8,128)(2,1)S(1)} %copy-done.26), channel_id=1, source_target_pairs={{0,6},{1,7},{2,4},{3,5},{4,2},{5,3},{6,0},{7,1},{8,14},{9,15},{10,... | collective-permute-start | bytes 589832 | tf_op jit(solution)/shard_map/ppermute | solution.py:337
  105.4 14.1 %collective-permute-start.23 = (bf16[4,192,128]{2,1,0:T(8,128)(2,1)S(1)}, bf16[4,192,128]{2,1,0:T(8,128)(2,1)S(1)}, u32[]{:S(2)}, u32[]{:S(2)}) collective-permute-start(bf16[4,192,128]{2,1,0:T(8,128)(2,1)S(1)} %copy-done.27), channel_id=1, source_target_pairs={{0,2},{1,3},{2,0},{3,1},{4,6},{5,7},{6,4},{7,5},{8,10},{9,11},{10,... | collective-permute-start | bytes 589832 | tf_op jit(solution)/shard_map/ppermute | solution.py:337
  105.4 16.3 %collective-permute-start.24 = (bf16[4,192,128]{2,1,0:T(8,128)(2,1)S(1)}, bf16[4,192,128]{2,1,0:T(8,128)(2,1)S(1)}, u32[]{:S(2)}, u32[]{:S(2)}) collective-permute-start(bf16[4,192,128]{2,1,0:T(8,128)(2,1)S(1)} %copy-done.25), channel_id=1, source_target_pairs={{0,4},{1,5},{2,6},{3,7},{4,0},{5,1},{6,2},{7,3},{8,12},{9,13},{10,... | collective-permute-start | bytes 589832 | tf_op jit(solution)/shard_map/ppermute | solution.py:337
  122.8 7.8 %collective-permute-start.27 = (bf16[4,192,128]{2,1,0:T(8,128)(2,1)S(1)}, bf16[4,192,128]{2,1,0:T(8,128)(2,1)S(1)}, u32[]{:S(2)}, u32[]{:S(2)}) collective-permute-start(bf16[4,192,128]{2,1,0:T(8,128)(2,1)S(1)} %pad_maximum_fusion.2), channel_id=1, source_target_pairs={{0,16},{1,17},{2,18},{3,19},{4,20},{5,21},{6,22},{7,23},{8,24},{9,... | collective-permute-start | bytes 589832 | tf_op jit(solution)/shard_map/ppermute | solution.py:337
  123.9 9.7 %collective-permute-start.28 = (bf16[4,192,128]{2,1,0:T(8,128)(2,1)S(1)}, bf16[4,192,128]{2,1,0:T(8,128)(2,1)S(1)}, u32[]{:S(2)}, u32[]{:S(2)}) collective-permute-start(bf16[4,192,128]{2,1,0:T(8,128)(2,1)S(1)} %pad_maximum_fusion.3), channel_id=1, source_target_pairs={{0,17},{1,16},{2,19},{3,18},{4,21},{5,20},{6,23},{7,22},{8,25},{9,... | collective-permute-start | bytes 589832 | tf_op jit(solution)/shard_map/ppermute | solution.py:337
  (33 other events, 273.4 us)
where the time goes:
time: 146 us
  Pallas kernels  68.4 us (47%)
  waiting for transfers between devices  35.5 us (24%)
  starting transfers between devices  34.2 us (23%)
  local copies, waits for them, and re-layouts  5.67 us (4%)
  other arithmetic  1.46 us (1%)
    ppermute x29, waiting for transfers between devices, swap(): return lax.ppermute(value, AXES, pairs)  35.5 us
    ppermute x29, starting transfers between devices, swap(): return lax.ppermute(value, AXES, pairs)  34.2 us
    pallas_call x4, Pallas kernels, attend(): pl.pallas_call(functools.partial(attend_kernel, chips, capacity, len(piec...  34.1 us
    pallas_call x4, Pallas kernels, project(): pl.pallas_call(functools.partial(project_kernel, head_count), in_specs=[v...  15.7 us
    pallas_call x1, Pallas kernels, finish(): pl.pallas_call(functools.partial(finish_kernel, capacity, chips), in_spec...  11.4 us
    unnamed x57, local copies, waits for them, and re-layouts  4.68 us
    pallas_call x1, Pallas kernels, chip_weights(): pl.pallas_call(functools.partial(weight_kernel, part), in_specs=[smem(),...  4.47 us
  transfers between devices with their start and end apart: 29, of which 11 were waited for; matrix products, arithmetic and copies ran while one was open for 1% of the time, Pallas kernels for 14%

commit v1 on v0

--- a/solution.py
+++ b/solution.py
@@ -22,12 +22,18 @@
     return pl.BlockSpec(memory_space=pltpu.VMEM)
 
 
-def smem():
-    return pl.BlockSpec(memory_space=pltpu.SMEM)
-
-
 def hbm():
-    return pl.BlockSpec(memory_space=pl.ANY)
+    return pl.BlockSpec(memory_space=pltpu.HBM)
+
+
+def limit(mebibytes):
+    return pltpu.CompilerParams(vmem_limit_bytes=mebibytes << 20)
+
+
+def coordinates():
+    along = lax.axis_size("sp") // lax.axis_size("bag")
+    bag, sp = lax.axis_index("bag"), lax.axis_index("sp")
+    return lax.div(sp, along), lax.div(bag, 2) * along + lax.rem(sp, along)
 
 
 def layer_norm(values):
@@ -50,8 +56,8 @@
     return (bag_row * capacity + rank).astype(jnp.int32)
 
 
-def slot_kernel(capacity, place_ref, tokens_ref, seq_ref, mod_ref, *out_refs):
-    me = place_ref[0]
+def slot_kernel(capacity, tokens_ref, seq_ref, mod_ref, *out_refs):
+    me, _ = coordinates()
     row_count, width = tokens_ref.shape
     block_count = len(out_refs)
     bag_row = ((seq_ref[...] // SEQ_BAG) ^ me).astype(F32)
@@ -63,29 +69,31 @@
     first = lax.broadcasted_iota(jnp.int32, (capacity, width), 1) == 0
     for block, out_ref in enumerate(out_refs):
         part = slice(block * capacity, (block + 1) * capacity)
-        mods = mod_ref[block ^ me]
-        normed = layer_norm(rows[part]) * (1.0 + mods[1:2]) + mods[0:1]
+        shift, scale = [mod_ref[column, pl.ds(block ^ me, 1)] for column in (0, 1)]
+        normed = layer_norm(rows[part]) * (1.0 + scale) + shift
         normed = jnp.where(first & (filled[part] < 0.5), HUGE, normed)
         out_ref[...] = normed.astype(BF16)
 
 
-def slot_rows(place, tokens, seq_row, modulation, bag_count, capacity):
+def slot_rows(tokens, seq_row, modulation, bag_count, capacity):
     width = tokens.shape[1]
     return pl.pallas_call(
         functools.partial(slot_kernel, capacity),
-        in_specs=[smem(), vmem(), vmem(), vmem()],
+        in_specs=[vmem(), vmem(), vmem()],
         out_specs=[vmem()] * bag_count,
         out_shape=[jax.ShapeDtypeStruct((capacity, width), BF16)] * bag_count,
+        compiler_params=limit(16),
         name="slot_rows",
-    )(place, tokens, seq_row, modulation)
-
-
-def weight_kernel(part, chip_ref, w_ref, out_ref, window, sem):
+    )(tokens, seq_row, modulation)
+
+
+def weight_kernel(part, w_ref, out_ref, window, sem):
     total = w_ref.shape[1]
     wide = window.shape[2]
     copies, shifts = [], []
+    _, chip = coordinates()
     for kind in range(3):
-        start = kind * (total // 3) + chip_ref[0] * part
+        start = kind * (total // 3) + chip * part
         base = pl.multiple_of(jnp.minimum(start // LANE * LANE, total - wide), LANE)
         shifts.append(start - base)
         copies.append(
@@ -108,18 +116,19 @@
     return -(-value // unit) * unit
 
 
-def chip_weights(chip, w_qkv, head_count):
+def chip_weights(w_qkv, head_count):
     depth, part = w_qkv.shape[0], head_count * HD
     wide = round_up(part + LANE - math.gcd(part, LANE), LANE)
     return pl.pallas_call(
         functools.partial(weight_kernel, part),
-        in_specs=[smem(), hbm()],
+        in_specs=[hbm()],
         out_specs=vmem(),
         out_shape=jax.ShapeDtypeStruct((depth, round_up(3 * part, LANE)), BF16),
         scratch_shapes=[pltpu.VMEM((3, depth, wide), BF16), pltpu.SemaphoreType.DMA((3,))],
         cost_estimate=pl.CostEstimate(flops=10**9, bytes_accessed=10**7, transcendentals=0),
+        compiler_params=limit(20),
         name="chip_weights",
-    )(chip, w_qkv)
+    )(w_qkv)
 
 
 def project_kernel(head_count, *refs):
@@ -166,6 +175,7 @@
         cost_estimate=pl.CostEstimate(
             flops=2 * size * depth * weights.shape[1], bytes_accessed=4 * size * depth, transcendentals=0
         ),
+        compiler_params=limit(12),
         name="project",
     )(*parts, weights)
 
@@ -263,19 +273,21 @@
             bytes_accessed=4 * head_count * keys * LANE,
             transcendentals=head_count * queries.shape[1] * keys,
         ),
+        compiler_params=limit(24),
         name="attend",
     )(queries, *pieces)
     return made[0], (made[1] if len(pieces) > 1 else pieces[0])
 
 
-def finish_kernel(capacity, chips, place_ref, tokens_ref, seq_ref, mod_ref, w_out, w_fc1, w_fc2, *refs):
+def finish_kernel(capacity, chips, tokens_ref, seq_ref, mod_ref, w_out, w_fc1, w_fc2, *refs):
     parts, out_ref, whole = refs[:chips], refs[chips], refs[chips + 1]
     row_count, width = tokens_ref.shape
+    plane, here = coordinates()
     for index, part in enumerate(parts):
-        whole[place_ref[1] ^ index] = part[...]
+        whole[here ^ index] = part[...]
     bags = parts[0].shape[0]
     seq_row = seq_ref[...]
-    position = slot_of_row(((seq_row // SEQ_BAG) ^ place_ref[0]).astype(F32), capacity)
+    position = slot_of_row(((seq_row // SEQ_BAG) ^ plane).astype(F32), capacity)
     slot_ids = lax.broadcasted_iota(jnp.int32, (bags * capacity, row_count), 0)
     pick = jnp.where(slot_ids == position, 1.0, 0.0).astype(BF16)
     seq_column = to_column(seq_row.astype(F32))
@@ -292,9 +304,9 @@
     attended = lax.dot_general(pick, slots, tn, preferred_element_type=F32).astype(BF16)
 
     def per_row(column):
-        value = jnp.broadcast_to(mod_ref[0, column : column + 1], (row_count, width))
-        for seq in range(1, mod_ref.shape[0]):
-            value = jnp.where(seq_column == seq, mod_ref[seq, column : column + 1], value)
+        value = jnp.broadcast_to(mod_ref[column, 0:1], (row_count, width))
+        for seq in range(1, mod_ref.shape[1]):
+            value = jnp.where(seq_column == seq, mod_ref[column, seq : seq + 1], value)
         return value
 
     branch = jnp.dot(attended, w_out[...], preferred_element_type=F32)
@@ -305,16 +317,17 @@
     out_ref[...] = (hidden.astype(F32) + per_row(5) * last).astype(BF16)
 
 
-def finish(place, tokens, seq_row, modulation, parts, w_out, w_fc1, w_fc2, capacity):
+def finish(tokens, seq_row, modulation, parts, w_out, w_fc1, w_fc2, capacity):
     chips = len(parts)
     return pl.pallas_call(
         functools.partial(finish_kernel, capacity, chips),
-        in_specs=[smem()] + [vmem()] * (6 + chips),
+        in_specs=[vmem()] * (6 + chips),
         out_specs=vmem(),
         out_shape=jax.ShapeDtypeStruct(tokens.shape, BF16),
         scratch_shapes=[pltpu.VMEM((chips,) + parts[0].shape, BF16)],
+        compiler_params=limit(20),
         name="finish",
-    )(place, tokens, seq_row, modulation, w_out, w_fc1, w_fc2, *parts)
+    )(tokens, seq_row, modulation, w_out, w_fc1, w_fc2, *parts)
 
 
 def layer(tokens, row_seq, modulation, w_qkv, w_out, w_fc1, w_fc2):
@@ -324,8 +337,6 @@
     row_count, width = tokens.shape
     capacity = row_count // bags * 5 // 4
     head_count = width // HD // chips
-    my_bag, my_sp = lax.axis_index("bag"), lax.axis_index("sp")
-    my_x, my_z, my_y = my_bag // cores, my_sp // along, my_sp % along
 
     def swap(value, dx=0, core=0, dz=0, dy=0):
         pairs = []
@@ -337,9 +348,9 @@
         return lax.ppermute(value, AXES, pairs)
 
     seq_row = row_seq.reshape(1, row_count)
-    place = jnp.stack([my_z, my_x * along + my_y]).astype(jnp.int32)
-    blocks = slot_rows(place, tokens, seq_row, modulation, bags, capacity)
-    weights = chip_weights(place[1:], w_qkv, head_count)
+    modulation = jnp.transpose(modulation, (1, 0, 2))
+    blocks = slot_rows(tokens, seq_row, modulation, bags, capacity)
+    weights = chip_weights(w_qkv, head_count)
     blocks = [block if k == 0 else swap(block, dz=k) for k, block in enumerate(blocks)]
     half = round_up(capacity, 32) // 2
     queries, pieces = [], []
@@ -362,7 +373,7 @@
     for j in range(chips):
         share = jnp.stack([part[j] for part in mixed])
         shares.append(swap(share, dx=j // along, dy=j % along) if j else share)
-    return finish(place, tokens, seq_row, modulation, shares, w_out, w_fc1, w_fc2, capacity)
+    return finish(tokens, seq_row, modulation, shares, w_out, w_fc1, w_fc2, capacity)
 
 
 def solution(mesh):

time: 146 us -> 112 us (0.77)
  Pallas kernels: 68.4 us -> 34 us
  waiting for transfers between devices: 35.5 us -> 37.3 us
    pallas_call x4, Pallas kernels: 34.1 us -> 19.8 us  [attend(): pl.pallas_call(functools.partial(attend_kernel, chips, capacity, len(piec...]
    pallas_call x4, Pallas kernels: 15.7 us -> 4.54 us  [project(): pl.pallas_call(functools.partial(project_kernel, head_count), in_specs=[v...]
    pallas_call x1, Pallas kernels: 11.4 us -> 6.23 us  [finish(): pl.pallas_call(functools.partial(finish_kernel, capacity, chips), in_spec...]
    pallas_call x2, Pallas kernels: 7.17 us -> 3.44 us  [the longest x1 2.45 us: chip_weights(): pl.pallas_call(functools.partial(weight_kernel, part), in_specs=[hbm()],...]
    ppermute x29, waiting for transfers between devices: 35.5 us -> 37.3 us  [swap(): return lax.ppermute(value, AXES, pairs)]
    unnamed x57 -> x24, local copies, waits for them, and re-layouts: 4.68 us -> 5.94 us
  transfers between devices with their start and end apart: 29 -> 29, of which waited for: 11 -> 12; matrix products, arithmetic and copies ran while one was open for 1% -> 0% of each run, Pallas kernels for 14% -> 6%
where the time goes in v1:
time: 112 us
  waiting for transfers between devices  37.3 us (33%)
  starting transfers between devices  34.3 us (31%)
  Pallas kernels  34 us (30%)
  local copies, waits for them, and re-layouts  6.06 us (5%)
    ppermute x29, waiting for transfers between devices, swap(): return lax.ppermute(value, AXES, pairs)  37.3 us
    ppermute x29, starting transfers between devices, swap(): return lax.ppermute(value, AXES, pairs)  34.3 us
    pallas_call x4, Pallas kernels, attend(): pl.pallas_call(functools.partial(attend_kernel, chips, capacity, len(piec...  19.8 us
    pallas_call x1, Pallas kernels, finish(): pl.pallas_call(functools.partial(finish_kernel, capacity, chips), in_spec...  6.23 us
    unnamed x24, local copies, waits for them, and re-layouts  5.94 us
    pallas_call x4, Pallas kernels, project(): pl.pallas_call(functools.partial(project_kernel, head_count), in_specs=[v...  4.54 us
    pallas_call x1, Pallas kernels, chip_weights(): pl.pallas_call(functools.partial(weight_kernel, part), in_specs=[hbm()],...  2.45 us
  transfers between devices with their start and end apart: 29, of which 12 were waited for; matrix products, arithmetic and copies ran while one was open for 0% of the time, Pallas kernels for 6%

profile of v1, /device:TPU:0, one launch (start us, length us, event | category | flops | bytes accessed | tf_op | source)
XLA Modules:
  0.0 112.1 jit_solution(14799901448710890460)
XLA Ops:
  3.6 5.1 %collective-permute-start.4 = (bf16[80,1152]{1,0:T(8,128)(2,1)S(1)}, bf16[80,1152]{1,0:T(8,128)(2,1)S(1)}, u32[]{:S(2)}, u32[]{:S(2)}) collective-permute-start(bf16[80,1152]{1,0:T(8,128)(2,1)S(1)} %get-tuple-element.21), channel_id=1, source_target_pairs={{0,6},{1,7},{2,4},{3,5},{4,2},{5,3},{6,0},{7,1},{8,14},{9,15},{10,... | collective-permute-start | bytes 552968 | tf_op jit(solution)/shard_map/ppermute | solution.py:348
  9.4 1.7 %collective-permute-start = (bf16[80,1152]{1,0:T(8,128)(2,1)S(1)}, bf16[80,1152]{1,0:T(8,128)(2,1)S(1)}, u32[]{:S(2)}, u32[]{:S(2)}) collective-permute-start(bf16[80,1152]{1,0:T(8,128)(2,1)S(1)} %get-tuple-element.19.refs_0_), channel_id=1, source_target_pairs={{0,1},{1,0},{2,3},{3,2},{4,5},{5,4},{6,7},{7,6},{8,9},{9,8},{10,11... | collective-permute-start | bytes 552968 | tf_op jit(solution)/shard_map/ppermute | solution.py:348
  12.6 1.7 %collective-permute-done.4.refs_0_ = bf16[80,1152]{1,0:T(8,128)(2,1)S(1)} collective-permute-done((bf16[80,1152]{1,0:T(8,128)(2,1)S(1)}, bf16[80,1152]{1,0:T(8,128)(2,1)S(1)}, u32[]{:S(2)}, u32[]{:S(2)}) %collective-permute-start.4) | collective-permute-done | bytes 184352 | tf_op jit(solution)/shard_map/ppermute | solution.py:348
  14.3 1.7 %collective-permute-start.6 = (bf16[80,1152]{1,0:T(8,128)(2,1)S(1)}, bf16[80,1152]{1,0:T(8,128)(2,1)S(1)}, u32[]{:S(2)}, u32[]{:S(2)}) collective-permute-start(bf16[80,1152]{1,0:T(8,128)(2,1)S(1)} %collective-permute-done.4.refs_0_), channel_id=1, source_target_pairs={{0,16},{1,17},{2,18},{3,19},{4,20},{5,21},{6,22},{7,23},{8,24},{9,... | collective-permute-start | bytes 552968 | tf_op jit(solution)/shard_map/ppermute | solution.py:348
  16.0 2.5 %collective-permute-done.10.refs_0_ = bf16[80,1152]{1,0:T(8,128)(2,1)S(1)} collective-permute-done((bf16[80,1152]{1,0:T(8,128)(2,1)S(1)}, bf16[80,1152]{1,0:T(8,128)(2,1)S(1)}, u32[]{:S(2)}, u32[]{:S(2)}) %collective-permute-start.10) | collective-permute-done | bytes 184352 | tf_op jit(solution)/shard_map/ppermute | solution.py:348
  19.9 4.5 %collective-permute-done.16.refs_0_ = bf16[80,1152]{1,0:T(8,128)(2,1)S(1)} collective-permute-done((bf16[80,1152]{1,0:T(8,128)(2,1)S(1)}, bf16[80,1152]{1,0:T(8,128)(2,1)S(1)}, u32[]{:S(2)}, u32[]{:S(2)}) %collective-permute-start.16) | collective-permute-done | bytes 184352 | tf_op jit(solution)/shard_map/ppermute | solution.py:348
  28.1 3.8 %collective-permute-done.3.refs_4_ = bf16[32,1152]{1,0:T(8,128)(2,1)S(1)} collective-permute-done((bf16[32,1152]{1,0:T(8,128)(2,1)S(1)}, bf16[32,1152]{1,0:T(8,128)(2,1)S(1)}, u32[]{:S(2)}, u32[]{:S(2)}) %collective-permute-start.3) | collective-permute-done | bytes 73760 | tf_op jit(solution)/shard_map/ppermute | solution.py:348
  37.5 3.3 %copy-done = bf16[1152,3456]{1,0:T(8,128)(2,1)S(1)} copy-done((bf16[1152,3456]{1,0:T(8,128)(2,1)S(1)}, bf16[1152,3456]{1,0:T(8,128)(2,1)}, u32[]{:S(2)}) %copy-start) | copy-done | bytes 7962648
  40.7 2.4 %chip_weights.1.refs_5_ = bf16[1152,896]{1,0:T(8,128)(2,1)S(1)} custom-call(bf16[1152,3456]{1,0:T(8,128)(2,1)S(1)} %copy-done), custom_call_target="tpu_custom_call" | custom-call | flops 1000000000 | bytes 10000000 | tf_op jit(solution)/shard_map/chip_weights/pallas_call | solution.py:122
  53.8 2.1 %collective-permute-done.21.refs_6_ = bf16[2,4,320,128]{3,2,1,0:T(8,128)(2,1)S(1)} collective-permute-done((bf16[2,4,320,128]{3,2,1,0:T(8,128)(2,1)S(1)}, bf16[2,4,320,128]{3,2,1,0:T(8,128)(2,1)S(1)}, u32[]{:S(2)}, u32[]{:S(2)}) %collective-permute-start.21) | collective-permute-done | bytes 655392 | tf_op jit(solution)/shard_map/ppermute | solution.py:348
  55.9 4.9 %attend.4 = (bf16[4,192,128]{2,1,0:T(8,128)(2,1)S(1)}, bf16[2,4,2560,128]{3,2,1,0:T(8,128)(2,1)S(1)}) custom-call(bf16[4,320,128]{2,1,0:T(8,128)(2,1)S(1)} %get-tuple-element.22.refs_0_, bf16[2,4,320,128]{3,2,1,0:T(8,128)(2,1)S(1)} %get-tuple-element.23.refs_1_, bf16[2,4,320,128]{3,2,1,0:T(8,128)(2,1)S(1)} %collective-permute-done.9.refs_2_, ...), custom_call_target="tpu_custom_call" | custom-call | flops 1677721600 | bytes 5242880 | tf_op jit(solution)/shard_map/attend/pallas_call | solution.py:266
  60.8 5.0 %attend.7 = bf16[4,192,128]{2,1,0:T(8,128)(2,1)S(1)} custom-call(bf16[4,320,128]{2,1,0:T(8,128)(2,1)S(1)} %get-tuple-element.31.refs_0_, bf16[2,4,2560,128]{3,2,1,0:T(8,128)(2,1)S(1)} %get-tuple-element.29.refs_1_), custom_call_target="tpu_custom_call" | custom-call | flops 1677721600 | bytes 5242880 | tf_op jit(solution)/shard_map/attend/pallas_call | solution.py:266
  65.8 4.8 %attend.6 = bf16[4,192,128]{2,1,0:T(8,128)(2,1)S(1)} custom-call(bf16[4,320,128]{2,1,0:T(8,128)(2,1)S(1)} %get-tuple-element.30.refs_0_, bf16[2,4,2560,128]{3,2,1,0:T(8,128)(2,1)S(1)} %get-tuple-element.29.refs_1_), custom_call_target="tpu_custom_call" | custom-call | flops 1677721600 | bytes 5242880 | tf_op jit(solution)/shard_map/attend/pallas_call | solution.py:266
  70.7 5.1 %attend.5 = bf16[4,192,128]{2,1,0:T(8,128)(2,1)S(1)} custom-call(bf16[4,320,128]{2,1,0:T(8,128)(2,1)S(1)} %get-tuple-element.20.refs_0_, bf16[2,4,2560,128]{3,2,1,0:T(8,128)(2,1)S(1)} %get-tuple-element.29.refs_1_), custom_call_target="tpu_custom_call" | custom-call | flops 1677721600 | bytes 5242880 | tf_op jit(solution)/shard_map/attend/pallas_call | solution.py:266
  75.7 2.3 %collective-permute-start.25 = (bf16[4,192,128]{2,1,0:T(8,128)(2,1)S(1)}, bf16[4,192,128]{2,1,0:T(8,128)(2,1)S(1)}, u32[]{:S(2)}, u32[]{:S(2)}) collective-permute-start(bf16[4,192,128]{2,1,0:T(8,128)(2,1)S(1)} %get-tuple-element.32), channel_id=1, source_target_pairs={{0,6},{1,7},{2,4},{3,5},{4,2},{5,3},{6,0},{7,1},{8,14},{9,15},{10,... | collective-permute-start | bytes 589832 | tf_op jit(solution)/shard_map/ppermute | solution.py:348
  78.1 2.1 %collective-permute-start.24 = (bf16[4,192,128]{2,1,0:T(8,128)(2,1)S(1)}, bf16[4,192,128]{2,1,0:T(8,128)(2,1)S(1)}, u32[]{:S(2)}, u32[]{:S(2)}) collective-permute-start(bf16[4,192,128]{2,1,0:T(8,128)(2,1)S(1)} %attend.7), channel_id=1, source_target_pairs={{0,4},{1,5},{2,6},{3,7},{4,0},{5,1},{6,2},{7,3},{8,12},{9,13},{10,... | collective-permute-start | bytes 589832 | tf_op jit(solution)/shard_map/ppermute | solution.py:348
  80.2 5.3 %collective-permute-done.25 = bf16[4,192,128]{2,1,0:T(8,128)(2,1)S(1)} collective-permute-done((bf16[4,192,128]{2,1,0:T(8,128)(2,1)S(1)}, bf16[4,192,128]{2,1,0:T(8,128)(2,1)S(1)}, u32[]{:S(2)}, u32[]{:S(2)}) %collective-permute-start.25) | collective-permute-done | bytes 196640 | tf_op jit(solution)/shard_map/ppermute | solution.py:348
  85.4 6.6 %collective-permute-done.23 = bf16[4,192,128]{2,1,0:T(8,128)(2,1)S(1)} collective-permute-done((bf16[4,192,128]{2,1,0:T(8,128)(2,1)S(1)}, bf16[4,192,128]{2,1,0:T(8,128)(2,1)S(1)}, u32[]{:S(2)}, u32[]{:S(2)}) %collective-permute-start.23) | collective-permute-done | bytes 196640 | tf_op jit(solution)/shard_map/ppermute | solution.py:348
  92.1 2.1 %collective-permute-done.24 = bf16[4,192,128]{2,1,0:T(8,128)(2,1)S(1)} collective-permute-done((bf16[4,192,128]{2,1,0:T(8,128)(2,1)S(1)}, bf16[4,192,128]{2,1,0:T(8,128)(2,1)S(1)}, u32[]{:S(2)}, u32[]{:S(2)}) %collective-permute-start.24) | collective-permute-done | bytes 196640 | tf_op jit(solution)/shard_map/ppermute | solution.py:348
  96.0 2.0 %collective-permute-start.28 = (bf16[4,192,128]{2,1,0:T(8,128)(2,1)S(1)}, bf16[4,192,128]{2,1,0:T(8,128)(2,1)S(1)}, u32[]{:S(2)}, u32[]{:S(2)}) collective-permute-start(bf16[4,192,128]{2,1,0:T(8,128)(2,1)S(1)} %pad_maximum_fusion.3), channel_id=1, source_target_pairs={{0,17},{1,16},{2,19},{3,18},{4,21},{5,20},{6,23},{7,22},{8,25},{9,... | collective-permute-start | bytes 589832 | tf_op jit(solution)/shard_map/ppermute | solution.py:348
  98.0 3.1 %collective-permute-done.26.refs_1_ = bf16[4,192,128]{2,1,0:T(8,128)(2,1)S(1)} collective-permute-done((bf16[4,192,128]{2,1,0:T(8,128)(2,1)S(1)}, bf16[4,192,128]{2,1,0:T(8,128)(2,1)S(1)}, u32[]{:S(2)}, u32[]{:S(2)}) %collective-permute-start.26) | collective-permute-done | bytes 196640 | tf_op jit(solution)/shard_map/ppermute | solution.py:348
  101.0 2.2 %collective-permute-done.27.refs_2_ = bf16[4,192,128]{2,1,0:T(8,128)(2,1)S(1)} collective-permute-done((bf16[4,192,128]{2,1,0:T(8,128)(2,1)S(1)}, bf16[4,192,128]{2,1,0:T(8,128)(2,1)S(1)}, u32[]{:S(2)}, u32[]{:S(2)}) %collective-permute-start.27) | collective-permute-done | bytes 196640 | tf_op jit(solution)/shard_map/ppermute | solution.py:348
  103.2 2.6 %collective-permute-done.28.refs_3_ = bf16[4,192,128]{2,1,0:T(8,128)(2,1)S(1)} collective-permute-done((bf16[4,192,128]{2,1,0:T(8,128)(2,1)S(1)}, bf16[4,192,128]{2,1,0:T(8,128)(2,1)S(1)}, u32[]{:S(2)}, u32[]{:S(2)}) %collective-permute-start.28) | collective-permute-done | bytes 196640 | tf_op jit(solution)/shard_map/ppermute | solution.py:348
  105.9 6.2 %finish.1 = bf16[256,1152]{1,0:T(8,128)(2,1)} custom-call(bf16[256,1152]{1,0:T(8,128)(2,1)S(1)} %copy-done.3, s32[1,256]{1,0:T(1,128)S(1)} %bitcast.9, f32[6,4,1152]{2,1,0:T(4,128)S(1)} %bitcast.7, bf16[1152,1152]{1,0:T(8,128)(2,1)S(1)} %copy-done.1, bf16[1152,2304]{1,0:T(8,128)(2,1)S(1)} %bitcast.3, bf16[2304,1152]{1,0:T(8,128)(2,1)S(1)} %bitcast.5, ...), custom_call_target="tpu_custom_call" | custom-call | tf_op jit(solution)/shard_map/finish/pallas_call | solution.py:322
  (87 shorter events, 28.8 us)
Async XLA Ops:
  3.6 10.7 %collective-permute-start.4 = (bf16[80,1152]{1,0:T(8,128)(2,1)S(1)}, bf16[80,1152]{1,0:T(8,128)(2,1)S(1)}, u32[]{:S(2)}, u32[]{:S(2)}) collective-permute-start(bf16[80,1152]{1,0:T(8,128)(2,1)S(1)} %get-tuple-element.21), channel_id=1, source_target_pairs={{0,6},{1,7},{2,4},{3,5},{4,2},{5,3},{6,0},{7,1},{8,14},{9,15},{10,... | collective-permute-start | bytes 552968 | tf_op jit(solution)/shard_map/ppermute | solution.py:348
  8.8 9.7 %collective-permute-start.10 = (bf16[80,1152]{1,0:T(8,128)(2,1)S(1)}, bf16[80,1152]{1,0:T(8,128)(2,1)S(1)}, u32[]{:S(2)}, u32[]{:S(2)}) collective-permute-start(bf16[80,1152]{1,0:T(8,128)(2,1)S(1)} %get-tuple-element.24), channel_id=1, source_target_pairs={{0,2},{1,3},{2,0},{3,1},{4,6},{5,7},{6,4},{7,5},{8,10},{9,11},{10,... | collective-permute-start | bytes 552968 | tf_op jit(solution)/shard_map/ppermute | solution.py:348
  8.8 15.6 %collective-permute-start.16 = (bf16[80,1152]{1,0:T(8,128)(2,1)S(1)}, bf16[80,1152]{1,0:T(8,128)(2,1)S(1)}, u32[]{:S(2)}, u32[]{:S(2)}) collective-permute-start(bf16[80,1152]{1,0:T(8,128)(2,1)S(1)} %get-tuple-element.26), channel_id=1, source_target_pairs={{0,4},{1,5},{2,6},{3,7},{4,0},{5,1},{6,2},{7,3},{8,12},{9,13},{10,... | collective-permute-start | bytes 552968 | tf_op jit(solution)/shard_map/ppermute | solution.py:348
  9.4 16.5 %collective-permute-start = (bf16[80,1152]{1,0:T(8,128)(2,1)S(1)}, bf16[80,1152]{1,0:T(8,128)(2,1)S(1)}, u32[]{:S(2)}, u32[]{:S(2)}) collective-permute-start(bf16[80,1152]{1,0:T(8,128)(2,1)S(1)} %get-tuple-element.19.refs_0_), channel_id=1, source_target_pairs={{0,1},{1,0},{2,3},{3,2},{4,5},{5,4},{6,7},{7,6},{8,9},{9,8},{10,11... | collective-permute-start | bytes 552968 | tf_op jit(solution)/shard_map/ppermute | solution.py:348
  11.1 16.4 %collective-permute-start.1 = (bf16[80,1152]{1,0:T(8,128)(2,1)S(1)}, bf16[80,1152]{1,0:T(8,128)(2,1)S(1)}, u32[]{:S(2)}, u32[]{:S(2)}) collective-permute-start(bf16[80,1152]{1,0:T(8,128)(2,1)S(1)} %get-tuple-element.19.refs_0_), channel_id=1, source_target_pairs={{0,16},{1,17},{2,18},{3,19},{4,20},{5,21},{6,22},{7,23},{8,24},{9,... | collective-permute-start | bytes 552968 | tf_op jit(solution)/shard_map/ppermute | solution.py:348
  14.3 18.9 %collective-permute-start.6 = (bf16[80,1152]{1,0:T(8,128)(2,1)S(1)}, bf16[80,1152]{1,0:T(8,128)(2,1)S(1)}, u32[]{:S(2)}, u32[]{:S(2)}) collective-permute-start(bf16[80,1152]{1,0:T(8,128)(2,1)S(1)} %collective-permute-done.4.refs_0_), channel_id=1, source_target_pairs={{0,16},{1,17},{2,18},{3,19},{4,20},{5,21},{6,22},{7,23},{8,24},{9,... | collective-permute-start | bytes 552968 | tf_op jit(solution)/shard_map/ppermute | solution.py:348
  18.4 16.3 %collective-permute-start.5 = (bf16[80,1152]{1,0:T(8,128)(2,1)S(1)}, bf16[80,1152]{1,0:T(8,128)(2,1)S(1)}, u32[]{:S(2)}, u32[]{:S(2)}) collective-permute-start(bf16[80,1152]{1,0:T(8,128)(2,1)S(1)} %collective-permute-done.4.refs_0_), channel_id=1, source_target_pairs={{0,1},{1,0},{2,3},{3,2},{4,5},{5,4},{6,7},{7,6},{8,9},{9,8},{10,11... | collective-permute-start | bytes 552968 | tf_op jit(solution)/shard_map/ppermute | solution.py:348
  24.4 10.9 %collective-permute-start.12 = (bf16[80,1152]{1,0:T(8,128)(2,1)S(1)}, bf16[80,1152]{1,0:T(8,128)(2,1)S(1)}, u32[]{:S(2)}, u32[]{:S(2)}) collective-permute-start(bf16[80,1152]{1,0:T(8,128)(2,1)S(1)} %collective-permute-done.10.refs_0_), channel_id=1, source_target_pairs={{0,16},{1,17},{2,18},{3,19},{4,20},{5,21},{6,22},{7,23},{8,24},{9,... | collective-permute-start | bytes 552968 | tf_op jit(solution)/shard_map/ppermute | solution.py:348
  25.9 11.0 %collective-permute-start.11 = (bf16[80,1152]{1,0:T(8,128)(2,1)S(1)}, bf16[80,1152]{1,0:T(8,128)(2,1)S(1)}, u32[]{:S(2)}, u32[]{:S(2)}) collective-permute-start(bf16[80,1152]{1,0:T(8,128)(2,1)S(1)} %collective-permute-done.10.refs_0_), channel_id=1, source_target_pairs={{0,1},{1,0},{2,3},{3,2},{4,5},{5,4},{6,7},{7,6},{8,9},{9,8},{10,11... | collective-permute-start | bytes 552968 | tf_op jit(solution)/shard_map/ppermute | solution.py:348
  31.9 12.1 %collective-permute-start.18 = (bf16[80,1152]{1,0:T(8,128)(2,1)S(1)}, bf16[80,1152]{1,0:T(8,128)(2,1)S(1)}, u32[]{:S(2)}, u32[]{:S(2)}) collective-permute-start(bf16[80,1152]{1,0:T(8,128)(2,1)S(1)} %collective-permute-done.16.refs_0_), channel_id=1, source_target_pairs={{0,16},{1,17},{2,18},{3,19},{4,20},{5,21},{6,22},{7,23},{8,24},{9,... | collective-permute-start | bytes 552968 | tf_op jit(solution)/shard_map/ppermute | solution.py:348
  33.2 13.3 %collective-permute-start.17 = (bf16[80,1152]{1,0:T(8,128)(2,1)S(1)}, bf16[80,1152]{1,0:T(8,128)(2,1)S(1)}, u32[]{:S(2)}, u32[]{:S(2)}) collective-permute-start(bf16[80,1152]{1,0:T(8,128)(2,1)S(1)} %collective-permute-done.16.refs_0_), channel_id=1, source_target_pairs={{0,1},{1,0},{2,3},{3,2},{4,5},{5,4},{6,7},{7,6},{8,9},{9,8},{10,11... | collective-permute-start | bytes 552968 | tf_op jit(solution)/shard_map/ppermute | solution.py:348
  34.8 8.5 %collective-permute-start.2 = (bf16[48,1152]{1,0:T(8,128)(2,1)S(1)}, bf16[48,1152]{1,0:T(8,128)(2,1)S(1)}, u32[]{:S(2)}, u32[]{:S(2)}) collective-permute-start(bf16[48,1152]{1,0:T(8,128)(2,1)S(1)} %slice.96), channel_id=1, source_target_pairs={{0,1},{1,0},{2,3},{3,2},{4,5},{5,4},{6,7},{7,6},{8,9},{9,8},{10,11... | collective-permute-start | bytes 331784 | tf_op jit(solution)/shard_map/ppermute | solution.py:348
  35.4 12.8 %collective-permute-start.7 = (bf16[48,1152]{1,0:T(8,128)(2,1)S(1)}, bf16[48,1152]{1,0:T(8,128)(2,1)S(1)}, u32[]{:S(2)}, u32[]{:S(2)}) collective-permute-start(bf16[48,1152]{1,0:T(8,128)(2,1)S(1)} %slice.98), channel_id=1, source_target_pairs={{0,1},{1,0},{2,3},{3,2},{4,5},{5,4},{6,7},{7,6},{8,9},{9,8},{10,11... | collective-permute-start | bytes 331784 | tf_op jit(solution)/shard_map/ppermute | solution.py:348
  37.0 9.6 %collective-permute-start.8 = (bf16[32,1152]{1,0:T(8,128)(2,1)S(1)}, bf16[32,1152]{1,0:T(8,128)(2,1)S(1)}, u32[]{:S(2)}, u32[]{:S(2)}) collective-permute-start(bf16[32,1152]{1,0:T(8,128)(2,1)S(1)} %slice.99), channel_id=1, source_target_pairs={{0,16},{1,17},{2,18},{3,19},{4,20},{5,21},{6,22},{7,23},{8,24},{9,... | collective-permute-start | bytes 221192 | tf_op jit(solution)/shard_map/ppermute | solution.py:348
  43.2 6.7 %collective-permute-start.13 = (bf16[48,1152]{1,0:T(8,128)(2,1)S(1)}, bf16[48,1152]{1,0:T(8,128)(2,1)S(1)}, u32[]{:S(2)}, u32[]{:S(2)}) collective-permute-start(bf16[48,1152]{1,0:T(8,128)(2,1)S(1)} %slice.100), channel_id=1, source_target_pairs={{0,1},{1,0},{2,3},{3,2},{4,5},{5,4},{6,7},{7,6},{8,9},{9,8},{10,11... | collective-permute-start | bytes 331784 | tf_op jit(solution)/shard_map/ppermute | solution.py:348
  44.0 5.9 %collective-permute-start.14 = (bf16[32,1152]{1,0:T(8,128)(2,1)S(1)}, bf16[32,1152]{1,0:T(8,128)(2,1)S(1)}, u32[]{:S(2)}, u32[]{:S(2)}) collective-permute-start(bf16[32,1152]{1,0:T(8,128)(2,1)S(1)} %slice.101), channel_id=1, source_target_pairs={{0,16},{1,17},{2,18},{3,19},{4,20},{5,21},{6,22},{7,23},{8,24},{9,... | collective-permute-start | bytes 221192 | tf_op jit(solution)/shard_map/ppermute | solution.py:348
  46.5 7.3 %collective-permute-start.9 = (bf16[2,4,320,128]{3,2,1,0:T(8,128)(2,1)S(1)}, bf16[2,4,320,128]{3,2,1,0:T(8,128)(2,1)S(1)}, u32[]{:S(2)}, u32[]{:S(2)}) collective-permute-start(bf16[2,4,320,128]{3,2,1,0:T(8,128)(2,1)S(1)} %get-tuple-element.23.refs_1_), channel_id=1, source_target_pairs={{0,8},{1,9},{2,10},{3,11},{4,12},{5,13},{6,14},{7,15},{8,0},{9,1},... | collective-permute-start | bytes 1966088 | tf_op jit(solution)/shard_map/ppermute | solution.py:348
  46.6 6.0 %collective-permute-start.19 = (bf16[48,1152]{1,0:T(8,128)(2,1)S(1)}, bf16[48,1152]{1,0:T(8,128)(2,1)S(1)}, u32[]{:S(2)}, u32[]{:S(2)}) collective-permute-start(bf16[48,1152]{1,0:T(8,128)(2,1)S(1)} %slice.102), channel_id=1, source_target_pairs={{0,1},{1,0},{2,3},{3,2},{4,5},{5,4},{6,7},{7,6},{8,9},{9,8},{10,11... | collective-permute-start | bytes 331784 | tf_op jit(solution)/shard_map/ppermute | solution.py:348
  75.7 9.7 %collective-permute-start.25 = (bf16[4,192,128]{2,1,0:T(8,128)(2,1)S(1)}, bf16[4,192,128]{2,1,0:T(8,128)(2,1)S(1)}, u32[]{:S(2)}, u32[]{:S(2)}) collective-permute-start(bf16[4,192,128]{2,1,0:T(8,128)(2,1)S(1)} %get-tuple-element.32), channel_id=1, source_target_pairs={{0,6},{1,7},{2,4},{3,5},{4,2},{5,3},{6,0},{7,1},{8,14},{9,15},{10,... | collective-permute-start | bytes 589832 | tf_op jit(solution)/shard_map/ppermute | solution.py:348
  78.1 14.0 %collective-permute-start.23 = (bf16[4,192,128]{2,1,0:T(8,128)(2,1)S(1)}, bf16[4,192,128]{2,1,0:T(8,128)(2,1)S(1)}, u32[]{:S(2)}, u32[]{:S(2)}) collective-permute-start(bf16[4,192,128]{2,1,0:T(8,128)(2,1)S(1)} %attend.6), channel_id=1, source_target_pairs={{0,2},{1,3},{2,0},{3,1},{4,6},{5,7},{6,4},{7,5},{8,10},{9,11},{10,... | collective-permute-start | bytes 589832 | tf_op jit(solution)/shard_map/ppermute | solution.py:348
  78.1 16.1 %collective-permute-start.24 = (bf16[4,192,128]{2,1,0:T(8,128)(2,1)S(1)}, bf16[4,192,128]{2,1,0:T(8,128)(2,1)S(1)}, u32[]{:S(2)}, u32[]{:S(2)}) collective-permute-start(bf16[4,192,128]{2,1,0:T(8,128)(2,1)S(1)} %attend.7), channel_id=1, source_target_pairs={{0,4},{1,5},{2,6},{3,7},{4,0},{5,1},{6,2},{7,3},{8,12},{9,13},{10,... | collective-permute-start | bytes 589832 | tf_op jit(solution)/shard_map/ppermute | solution.py:348
  94.2 6.8 %collective-permute-start.26 = (bf16[4,192,128]{2,1,0:T(8,128)(2,1)S(1)}, bf16[4,192,128]{2,1,0:T(8,128)(2,1)S(1)}, u32[]{:S(2)}, u32[]{:S(2)}) collective-permute-start(bf16[4,192,128]{2,1,0:T(8,128)(2,1)S(1)} %pad_maximum_fusion.1), channel_id=1, source_target_pairs={{0,1},{1,0},{2,3},{3,2},{4,5},{5,4},{6,7},{7,6},{8,9},{9,8},{10,11... | collective-permute-start | bytes 589832 | tf_op jit(solution)/shard_map/ppermute | solution.py:348
  95.3 7.8 %collective-permute-start.27 = (bf16[4,192,128]{2,1,0:T(8,128)(2,1)S(1)}, bf16[4,192,128]{2,1,0:T(8,128)(2,1)S(1)}, u32[]{:S(2)}, u32[]{:S(2)}) collective-permute-start(bf16[4,192,128]{2,1,0:T(8,128)(2,1)S(1)} %pad_maximum_fusion.2), channel_id=1, source_target_pairs={{0,16},{1,17},{2,18},{3,19},{4,20},{5,21},{6,22},{7,23},{8,24},{9,... | collective-permute-start | bytes 589832 | tf_op jit(solution)/shard_map/ppermute | solution.py:348
  96.0 9.9 %collective-permute-start.28 = (bf16[4,192,128]{2,1,0:T(8,128)(2,1)S(1)}, bf16[4,192,128]{2,1,0:T(8,128)(2,1)S(1)}, u32[]{:S(2)}, u32[]{:S(2)}) collective-permute-start(bf16[4,192,128]{2,1,0:T(8,128)(2,1)S(1)} %pad_maximum_fusion.3), channel_id=1, source_target_pairs={{0,17},{1,16},{2,19},{3,18},{4,21},{5,20},{6,23},{7,22},{8,25},{9,... | collective-permute-start | bytes 589832 | tf_op jit(solution)/shard_map/ppermute | solution.py:348
  (17 other events, 314.8 us)

commit v2 on v1

--- a/solution.py
+++ b/solution.py
@@ -279,13 +279,14 @@
     return made[0], (made[1] if len(pieces) > 1 else pieces[0])
 
 
-def finish_kernel(capacity, chips, tokens_ref, seq_ref, mod_ref, w_out, w_fc1, w_fc2, *refs):
-    parts, out_ref, whole = refs[:chips], refs[chips], refs[chips + 1]
+def finish_kernel(capacity, chips, rounds, tokens_ref, seq_ref, mod_ref, w_out, w_fc1, w_fc2, *refs):
+    parts, out_ref, whole = refs[:-2], refs[-2], refs[-1]
     row_count, width = tokens_ref.shape
     plane, here = coordinates()
     for index, part in enumerate(parts):
-        whole[here ^ index] = part[...]
-    bags = parts[0].shape[0]
+        for at, bag in enumerate(rounds[index // chips]):
+            whole[here ^ (index % chips), bag] = part[at]
+    bags = whole.shape[1]
     seq_row = seq_ref[...]
     position = slot_of_row(((seq_row // SEQ_BAG) ^ plane).astype(F32), capacity)
     slot_ids = lax.broadcasted_iota(jnp.int32, (bags * capacity, row_count), 0)
@@ -317,14 +318,14 @@
     out_ref[...] = (hidden.astype(F32) + per_row(5) * last).astype(BF16)
 
 
-def finish(tokens, seq_row, modulation, parts, w_out, w_fc1, w_fc2, capacity):
-    chips = len(parts)
+def finish(tokens, seq_row, modulation, parts, rounds, w_out, w_fc1, w_fc2, capacity, chips):
+    bags = sum(len(members) for members in rounds)
     return pl.pallas_call(
-        functools.partial(finish_kernel, capacity, chips),
-        in_specs=[vmem()] * (6 + chips),
+        functools.partial(finish_kernel, capacity, chips, rounds),
+        in_specs=[vmem()] * (6 + len(parts)),
         out_specs=vmem(),
         out_shape=jax.ShapeDtypeStruct(tokens.shape, BF16),
-        scratch_shapes=[pltpu.VMEM((chips,) + parts[0].shape, BF16)],
+        scratch_shapes=[pltpu.VMEM((chips, bags) + parts[0].shape[1:], BF16)],
         compiler_params=limit(20),
         name="finish",
     )(tokens, seq_row, modulation, w_out, w_fc1, w_fc2, *parts)
@@ -349,8 +350,12 @@
 
     seq_row = row_seq.reshape(1, row_count)
     modulation = jnp.transpose(modulation, (1, 0, 2))
-    blocks = slot_rows(tokens, seq_row, modulation, bags, capacity)
-    weights = chip_weights(w_qkv, head_count)
+
+    def in_place(value):
+        return pltpu.with_memory_space_constraint(value, pltpu.HBM)
+
+    blocks = slot_rows(in_place(tokens), in_place(seq_row), in_place(modulation), bags, capacity)
+    weights = chip_weights(in_place(w_qkv), head_count)
     blocks = [block if k == 0 else swap(block, dz=k) for k, block in enumerate(blocks)]
     half = round_up(capacity, 32) // 2
     queries, pieces = [], []
@@ -369,11 +374,13 @@
         part, kv = attend(queries[k], pieces, chips, capacity)
         pieces = [kv]
         mixed[k] = swap(part, dz=k) if k else part
+    rounds = [[k for k in range(bags) if k != 2], [2]] if bags > 2 else [list(range(bags))]
     shares = []
-    for j in range(chips):
-        share = jnp.stack([part[j] for part in mixed])
-        shares.append(swap(share, dx=j // along, dy=j % along) if j else share)
-    return finish(tokens, seq_row, modulation, shares, w_out, w_fc1, w_fc2, capacity)
+    for members in rounds:
+        for j in range(chips):
+            share = jnp.stack([mixed[k][j] for k in members])
+            shares.append(swap(share, dx=j // along, dy=j % along) if j else share)
+    return finish(tokens, seq_row, modulation, shares, rounds, w_out, w_fc1, w_fc2, capacity, chips)
 
 
 def solution(mesh):

time: 112 us -> 109 us (0.973)
  local copies, waits for them, and re-layouts: 6.06 us -> 0.16 us
  starting transfers between devices: 34.3 us -> 37.9 us
  waiting for transfers between devices: 37.3 us -> 34.9 us
  Pallas kernels: 34 us -> 35.7 us
    unnamed x24 -> x16, local copies, waits for them, and re-layouts: 5.94 us -> 0.04 us
    ppermute x29 -> x32, starting transfers between devices: 34.3 us -> 37.9 us  [swap(): return lax.ppermute(value, AXES, pairs)]
    ppermute x29 -> x32, waiting for transfers between devices: 37.3 us -> 34.9 us  [swap(): return lax.ppermute(value, AXES, pairs)]
  transfers between devices with their start and end apart: 29 -> 32, of which waited for: 12 -> 12; matrix products, arithmetic and copies ran while one was open for 0% -> 0% of each run, Pallas kernels for 6% -> 7%
where the time goes in v2:
time: 109 us
  starting transfers between devices  37.9 us (35%)
  Pallas kernels  35.7 us (33%)
  waiting for transfers between devices  34.9 us (32%)
    ppermute x32, starting transfers between devices, swap(): return lax.ppermute(value, AXES, pairs)  37.9 us
    ppermute x32, waiting for transfers between devices, swap(): return lax.ppermute(value, AXES, pairs)  34.9 us
    pallas_call x4, Pallas kernels, attend(): pl.pallas_call(functools.partial(attend_kernel, chips, capacity, len(piec...  19.8 us
    pallas_call x1, Pallas kernels, finish(): pl.pallas_call(functools.partial(finish_kernel, capacity, chips, rounds),...  6.23 us
    pallas_call x4, Pallas kernels, project(): pl.pallas_call(functools.partial(project_kernel, head_count), in_specs=[v...  4.54 us
    pallas_call x1, Pallas kernels, chip_weights(): pl.pallas_call(functools.partial(weight_kernel, part), in_specs=[hbm()],...  3.16 us
  transfers between devices with their start and end apart: 32, of which 12 were waited for; matrix products, arithmetic and copies ran while one was open for 0% of the time, Pallas kernels for 7%

profile of v2, /device:TPU:0, one launch (start us, length us, event | category | flops | bytes accessed | tf_op | source)
XLA Modules:
  0.0 109.2 jit_solution(1543211088448612182)
XLA Ops:
  0.0 2.0 %slot_rows.1 = (bf16[80,1152]{1,0:T(8,128)(2,1)S(1)}, bf16[80,1152]{1,0:T(8,128)(2,1)S(1)}, bf16[80,1152]{1,0:T(8,128)(2,1)S(1)}, bf16[80,1152]{1,0:T(8,128)(2,1)S(1)}) custom-call(bf16[256,1152]{1,0:T(8,128)(2,1)} %tokens_ref.3, s32[1,256]{1,0:T(1,128)} %bitcast.8, f32[6,4,1152]{2,1,0:T(4,128)} %bitcast.6), custom_call_target="tpu_custom_call" | custom-call | tf_op jit(solution)/shard_map/slot_rows/pallas_call | solution.py:80
  2.0 5.1 %collective-permute-start.4 = (bf16[80,1152]{1,0:T(8,128)(2,1)S(1)}, bf16[80,1152]{1,0:T(8,128)(2,1)S(1)}, u32[]{:S(2)}, u32[]{:S(2)}) collective-permute-start(bf16[80,1152]{1,0:T(8,128)(2,1)S(1)} %get-tuple-element.21), channel_id=1, source_target_pairs={{0,6},{1,7},{2,4},{3,5},{4,2},{5,3},{6,0},{7,1},{8,14},{9,15},{10,... | collective-permute-start | bytes 552968 | tf_op jit(solution)/shard_map/ppermute | solution.py:349
  7.8 1.7 %collective-permute-start = (bf16[80,1152]{1,0:T(8,128)(2,1)S(1)}, bf16[80,1152]{1,0:T(8,128)(2,1)S(1)}, u32[]{:S(2)}, u32[]{:S(2)}) collective-permute-start(bf16[80,1152]{1,0:T(8,128)(2,1)S(1)} %get-tuple-element.19.refs_0_), channel_id=1, source_target_pairs={{0,1},{1,0},{2,3},{3,2},{4,5},{5,4},{6,7},{7,6},{8,9},{9,8},{10,11... | collective-permute-start | bytes 552968 | tf_op jit(solution)/shard_map/ppermute | solution.py:349
  11.0 1.7 %collective-permute-done.4.refs_0_ = bf16[80,1152]{1,0:T(8,128)(2,1)S(1)} collective-permute-done((bf16[80,1152]{1,0:T(8,128)(2,1)S(1)}, bf16[80,1152]{1,0:T(8,128)(2,1)S(1)}, u32[]{:S(2)}, u32[]{:S(2)}) %collective-permute-start.4) | collective-permute-done | bytes 184352 | tf_op jit(solution)/shard_map/ppermute | solution.py:349
  12.7 1.7 %collective-permute-start.6 = (bf16[80,1152]{1,0:T(8,128)(2,1)S(1)}, bf16[80,1152]{1,0:T(8,128)(2,1)S(1)}, u32[]{:S(2)}, u32[]{:S(2)}) collective-permute-start(bf16[80,1152]{1,0:T(8,128)(2,1)S(1)} %collective-permute-done.4.refs_0_), channel_id=1, source_target_pairs={{0,16},{1,17},{2,18},{3,19},{4,20},{5,21},{6,22},{7,23},{8,24},{9,... | collective-permute-start | bytes 552968 | tf_op jit(solution)/shard_map/ppermute | solution.py:349
  14.4 2.4 %collective-permute-done.10.refs_0_ = bf16[80,1152]{1,0:T(8,128)(2,1)S(1)} collective-permute-done((bf16[80,1152]{1,0:T(8,128)(2,1)S(1)}, bf16[80,1152]{1,0:T(8,128)(2,1)S(1)}, u32[]{:S(2)}, u32[]{:S(2)}) %collective-permute-start.10) | collective-permute-done | bytes 184352 | tf_op jit(solution)/shard_map/ppermute | solution.py:349
  18.3 4.5 %collective-permute-done.16.refs_0_ = bf16[80,1152]{1,0:T(8,128)(2,1)S(1)} collective-permute-done((bf16[80,1152]{1,0:T(8,128)(2,1)S(1)}, bf16[80,1152]{1,0:T(8,128)(2,1)S(1)}, u32[]{:S(2)}, u32[]{:S(2)}) %collective-permute-start.16) | collective-permute-done | bytes 184352 | tf_op jit(solution)/shard_map/ppermute | solution.py:349
  26.4 3.8 %collective-permute-done.3.refs_4_ = bf16[32,1152]{1,0:T(8,128)(2,1)S(1)} collective-permute-done((bf16[32,1152]{1,0:T(8,128)(2,1)S(1)}, bf16[32,1152]{1,0:T(8,128)(2,1)S(1)}, u32[]{:S(2)}, u32[]{:S(2)}) %collective-permute-start.3) | collective-permute-done | bytes 73760 | tf_op jit(solution)/shard_map/ppermute | solution.py:349
  35.9 3.2 %chip_weights.1.refs_5_ = bf16[1152,896]{1,0:T(8,128)(2,1)S(1)} custom-call(bf16[1152,3456]{1,0:T(8,128)(2,1)} %w_ref.1), custom_call_target="tpu_custom_call" | custom-call | flops 1000000000 | bytes 10000000 | tf_op jit(solution)/shard_map/chip_weights/pallas_call | solution.py:122
  39.1 1.7 %collective-permute-done.2.refs_3_ = bf16[48,1152]{1,0:T(8,128)(2,1)S(1)} collective-permute-done((bf16[48,1152]{1,0:T(8,128)(2,1)S(1)}, bf16[48,1152]{1,0:T(8,128)(2,1)S(1)}, u32[]{:S(2)}, u32[]{:S(2)}) %collective-permute-start.2) | collective-permute-done | bytes 110624 | tf_op jit(solution)/shard_map/ppermute | solution.py:349
  40.8 1.7 %collective-permute-start.13 = (bf16[48,1152]{1,0:T(8,128)(2,1)S(1)}, bf16[48,1152]{1,0:T(8,128)(2,1)S(1)}, u32[]{:S(2)}, u32[]{:S(2)}) collective-permute-start(bf16[48,1152]{1,0:T(8,128)(2,1)S(1)} %slice.100), channel_id=1, source_target_pairs={{0,1},{1,0},{2,3},{3,2},{4,5},{5,4},{6,7},{7,6},{8,9},{9,8},{10,11... | collective-permute-start | bytes 331784 | tf_op jit(solution)/shard_map/ppermute | solution.py:349
  44.5 1.7 %collective-permute-start.20 = (bf16[32,1152]{1,0:T(8,128)(2,1)S(1)}, bf16[32,1152]{1,0:T(8,128)(2,1)S(1)}, u32[]{:S(2)}, u32[]{:S(2)}) collective-permute-start(bf16[32,1152]{1,0:T(8,128)(2,1)S(1)} %slice.103), channel_id=1, source_target_pairs={{0,16},{1,17},{2,18},{3,19},{4,20},{5,21},{6,22},{7,23},{8,24},{9,... | collective-permute-start | bytes 221192 | tf_op jit(solution)/shard_map/ppermute | solution.py:349
  50.9 2.1 %collective-permute-done.21.refs_6_ = bf16[2,4,320,128]{3,2,1,0:T(8,128)(2,1)S(1)} collective-permute-done((bf16[2,4,320,128]{3,2,1,0:T(8,128)(2,1)S(1)}, bf16[2,4,320,128]{3,2,1,0:T(8,128)(2,1)S(1)}, u32[]{:S(2)}, u32[]{:S(2)}) %collective-permute-start.21) | collective-permute-done | bytes 655392 | tf_op jit(solution)/shard_map/ppermute | solution.py:349
  53.0 5.1 %attend.4 = (bf16[4,192,128]{2,1,0:T(8,128)(2,1)S(1)}, bf16[2,4,2560,128]{3,2,1,0:T(8,128)(2,1)S(1)}) custom-call(bf16[4,320,128]{2,1,0:T(8,128)(2,1)S(1)} %get-tuple-element.22.refs_0_, bf16[2,4,320,128]{3,2,1,0:T(8,128)(2,1)S(1)} %get-tuple-element.23.refs_1_, bf16[2,4,320,128]{3,2,1,0:T(8,128)(2,1)S(1)} %collective-permute-done.9.refs_2_, ...), custom_call_target="tpu_custom_call" | custom-call | flops 1677721600 | bytes 5242880 | tf_op jit(solution)/shard_map/attend/pallas_call | solution.py:266
  58.1 4.8 %attend.7 = bf16[4,192,128]{2,1,0:T(8,128)(2,1)S(1)} custom-call(bf16[4,320,128]{2,1,0:T(8,128)(2,1)S(1)} %get-tuple-element.32.refs_0_, bf16[2,4,2560,128]{3,2,1,0:T(8,128)(2,1)S(1)} %get-tuple-element.29.refs_1_), custom_call_target="tpu_custom_call" | custom-call | flops 1677721600 | bytes 5242880 | tf_op jit(solution)/shard_map/attend/pallas_call | solution.py:266
  62.9 4.8 %attend.6 = bf16[4,192,128]{2,1,0:T(8,128)(2,1)S(1)} custom-call(bf16[4,320,128]{2,1,0:T(8,128)(2,1)S(1)} %get-tuple-element.30.refs_0_, bf16[2,4,2560,128]{3,2,1,0:T(8,128)(2,1)S(1)} %get-tuple-element.29.refs_1_), custom_call_target="tpu_custom_call" | custom-call | flops 1677721600 | bytes 5242880 | tf_op jit(solution)/shard_map/attend/pallas_call | solution.py:266
  67.8 5.0 %attend.5 = bf16[4,192,128]{2,1,0:T(8,128)(2,1)S(1)} custom-call(bf16[4,320,128]{2,1,0:T(8,128)(2,1)S(1)} %get-tuple-element.20.refs_0_, bf16[2,4,2560,128]{3,2,1,0:T(8,128)(2,1)S(1)} %get-tuple-element.29.refs_1_), custom_call_target="tpu_custom_call" | custom-call | flops 1677721600 | bytes 5242880 | tf_op jit(solution)/shard_map/attend/pallas_call | solution.py:266
  72.8 2.2 %collective-permute-start.24 = (bf16[4,192,128]{2,1,0:T(8,128)(2,1)S(1)}, bf16[4,192,128]{2,1,0:T(8,128)(2,1)S(1)}, u32[]{:S(2)}, u32[]{:S(2)}) collective-permute-start(bf16[4,192,128]{2,1,0:T(8,128)(2,1)S(1)} %get-tuple-element.31), channel_id=1, source_target_pairs={{0,6},{1,7},{2,4},{3,5},{4,2},{5,3},{6,0},{7,1},{8,14},{9,15},{10,... | collective-permute-start | bytes 589832 | tf_op jit(solution)/shard_map/ppermute | solution.py:349
  75.0 2.3 %collective-permute-start.28 = (bf16[4,192,128]{2,1,0:T(8,128)(2,1)S(1)}, bf16[4,192,128]{2,1,0:T(8,128)(2,1)S(1)}, u32[]{:S(2)}, u32[]{:S(2)}) collective-permute-start(bf16[4,192,128]{2,1,0:T(8,128)(2,1)S(1)} %attend.7), channel_id=1, source_target_pairs={{0,4},{1,5},{2,6},{3,7},{4,0},{5,1},{6,2},{7,3},{8,12},{9,13},{10,... | collective-permute-start | bytes 589832 | tf_op jit(solution)/shard_map/ppermute | solution.py:349
  77.2 5.3 %collective-permute-done.24 = bf16[4,192,128]{2,1,0:T(8,128)(2,1)S(1)} collective-permute-done((bf16[4,192,128]{2,1,0:T(8,128)(2,1)S(1)}, bf16[4,192,128]{2,1,0:T(8,128)(2,1)S(1)}, u32[]{:S(2)}, u32[]{:S(2)}) %collective-permute-start.24) | collective-permute-done | bytes 196640 | tf_op jit(solution)/shard_map/ppermute | solution.py:349
  82.5 6.8 %collective-permute-done.23 = bf16[4,192,128]{2,1,0:T(8,128)(2,1)S(1)} collective-permute-done((bf16[4,192,128]{2,1,0:T(8,128)(2,1)S(1)}, bf16[4,192,128]{2,1,0:T(8,128)(2,1)S(1)}, u32[]{:S(2)}, u32[]{:S(2)}) %collective-permute-start.23) | collective-permute-done | bytes 196640 | tf_op jit(solution)/shard_map/ppermute | solution.py:349
  93.1 2.0 %collective-permute-start.27 = (bf16[3,192,128]{2,1,0:T(8,128)(2,1)S(1)}, bf16[3,192,128]{2,1,0:T(8,128)(2,1)S(1)}, u32[]{:S(2)}, u32[]{:S(2)}) collective-permute-start(bf16[3,192,128]{2,1,0:T(8,128)(2,1)S(1)} %pad_maximum_fusion.3), channel_id=1, source_target_pairs={{0,17},{1,16},{2,19},{3,18},{4,21},{5,20},{6,23},{7,22},{8,25},{9,... | collective-permute-start | bytes 442376 | tf_op jit(solution)/shard_map/ppermute | solution.py:349
  95.7 3.0 %collective-permute-done.31.refs_7_ = bf16[1,192,128]{2,1,0:T(8,128)(2,1)S(1)} collective-permute-done((bf16[1,192,128]{2,1,0:T(8,128)(2,1)S(1)}, bf16[1,192,128]{2,1,0:T(8,128)(2,1)S(1)}, u32[]{:S(2)}, u32[]{:S(2)}) %collective-permute-start.31) | collective-permute-done | bytes 49184 | tf_op jit(solution)/shard_map/ppermute | solution.py:349
  103.0 6.2 %finish.1 = bf16[256,1152]{1,0:T(8,128)(2,1)} custom-call(bf16[256,1152]{1,0:T(8,128)(2,1)S(1)} %copy-done.1, s32[1,256]{1,0:T(1,128)S(1)} %bitcast.9, f32[6,4,1152]{2,1,0:T(4,128)S(1)} %bitcast.7, bf16[1152,1152]{1,0:T(8,128)(2,1)S(1)} %copy-done, bf16[1152,2304]{1,0:T(8,128)(2,1)S(1)} %bitcast.3, bf16[2304,1152]{1,0:T(8,128)(2,1)S(1)} %bitcast.5, ...), custom_call_target="tpu_custom_call" | custom-call | tf_op jit(solution)/shard_map/finish/pallas_call | solution.py:323
  (85 shorter events, 28.1 us)
Async XLA Ops:
  2.0 10.7 %collective-permute-start.4 = (bf16[80,1152]{1,0:T(8,128)(2,1)S(1)}, bf16[80,1152]{1,0:T(8,128)(2,1)S(1)}, u32[]{:S(2)}, u32[]{:S(2)}) collective-permute-start(bf16[80,1152]{1,0:T(8,128)(2,1)S(1)} %get-tuple-element.21), channel_id=1, source_target_pairs={{0,6},{1,7},{2,4},{3,5},{4,2},{5,3},{6,0},{7,1},{8,14},{9,15},{10,... | collective-permute-start | bytes 552968 | tf_op jit(solution)/shard_map/ppermute | solution.py:349
  7.2 9.6 %collective-permute-start.10 = (bf16[80,1152]{1,0:T(8,128)(2,1)S(1)}, bf16[80,1152]{1,0:T(8,128)(2,1)S(1)}, u32[]{:S(2)}, u32[]{:S(2)}) collective-permute-start(bf16[80,1152]{1,0:T(8,128)(2,1)S(1)} %get-tuple-element.24), channel_id=1, source_target_pairs={{0,2},{1,3},{2,0},{3,1},{4,6},{5,7},{6,4},{7,5},{8,10},{9,11},{10,... | collective-permute-start | bytes 552968 | tf_op jit(solution)/shard_map/ppermute | solution.py:349
  7.2 15.6 %collective-permute-start.16 = (bf16[80,1152]{1,0:T(8,128)(2,1)S(1)}, bf16[80,1152]{1,0:T(8,128)(2,1)S(1)}, u32[]{:S(2)}, u32[]{:S(2)}) collective-permute-start(bf16[80,1152]{1,0:T(8,128)(2,1)S(1)} %get-tuple-element.26), channel_id=1, source_target_pairs={{0,4},{1,5},{2,6},{3,7},{4,0},{5,1},{6,2},{7,3},{8,12},{9,13},{10,... | collective-permute-start | bytes 552968 | tf_op jit(solution)/shard_map/ppermute | solution.py:349
  7.8 16.5 %collective-permute-start = (bf16[80,1152]{1,0:T(8,128)(2,1)S(1)}, bf16[80,1152]{1,0:T(8,128)(2,1)S(1)}, u32[]{:S(2)}, u32[]{:S(2)}) collective-permute-start(bf16[80,1152]{1,0:T(8,128)(2,1)S(1)} %get-tuple-element.19.refs_0_), channel_id=1, source_target_pairs={{0,1},{1,0},{2,3},{3,2},{4,5},{5,4},{6,7},{7,6},{8,9},{9,8},{10,11... | collective-permute-start | bytes 552968 | tf_op jit(solution)/shard_map/ppermute | solution.py:349
  9.5 16.4 %collective-permute-start.1 = (bf16[80,1152]{1,0:T(8,128)(2,1)S(1)}, bf16[80,1152]{1,0:T(8,128)(2,1)S(1)}, u32[]{:S(2)}, u32[]{:S(2)}) collective-permute-start(bf16[80,1152]{1,0:T(8,128)(2,1)S(1)} %get-tuple-element.19.refs_0_), channel_id=1, source_target_pairs={{0,16},{1,17},{2,18},{3,19},{4,20},{5,21},{6,22},{7,23},{8,24},{9,... | collective-permute-start | bytes 552968 | tf_op jit(solution)/shard_map/ppermute | solution.py:349
  12.7 18.9 %collective-permute-start.6 = (bf16[80,1152]{1,0:T(8,128)(2,1)S(1)}, bf16[80,1152]{1,0:T(8,128)(2,1)S(1)}, u32[]{:S(2)}, u32[]{:S(2)}) collective-permute-start(bf16[80,1152]{1,0:T(8,128)(2,1)S(1)} %collective-permute-done.4.refs_0_), channel_id=1, source_target_pairs={{0,16},{1,17},{2,18},{3,19},{4,20},{5,21},{6,22},{7,23},{8,24},{9,... | collective-permute-start | bytes 552968 | tf_op jit(solution)/shard_map/ppermute | solution.py:349
  16.8 16.3 %collective-permute-start.5 = (bf16[80,1152]{1,0:T(8,128)(2,1)S(1)}, bf16[80,1152]{1,0:T(8,128)(2,1)S(1)}, u32[]{:S(2)}, u32[]{:S(2)}) collective-permute-start(bf16[80,1152]{1,0:T(8,128)(2,1)S(1)} %collective-permute-done.4.refs_0_), channel_id=1, source_target_pairs={{0,1},{1,0},{2,3},{3,2},{4,5},{5,4},{6,7},{7,6},{8,9},{9,8},{10,11... | collective-permute-start | bytes 552968 | tf_op jit(solution)/shard_map/ppermute | solution.py:349
  22.8 10.9 %collective-permute-start.12 = (bf16[80,1152]{1,0:T(8,128)(2,1)S(1)}, bf16[80,1152]{1,0:T(8,128)(2,1)S(1)}, u32[]{:S(2)}, u32[]{:S(2)}) collective-permute-start(bf16[80,1152]{1,0:T(8,128)(2,1)S(1)} %collective-permute-done.10.refs_0_), channel_id=1, source_target_pairs={{0,16},{1,17},{2,18},{3,19},{4,20},{5,21},{6,22},{7,23},{8,24},{9,... | collective-permute-start | bytes 552968 | tf_op jit(solution)/shard_map/ppermute | solution.py:349
  24.3 11.0 %collective-permute-start.11 = (bf16[80,1152]{1,0:T(8,128)(2,1)S(1)}, bf16[80,1152]{1,0:T(8,128)(2,1)S(1)}, u32[]{:S(2)}, u32[]{:S(2)}) collective-permute-start(bf16[80,1152]{1,0:T(8,128)(2,1)S(1)} %collective-permute-done.10.refs_0_), channel_id=1, source_target_pairs={{0,1},{1,0},{2,3},{3,2},{4,5},{5,4},{6,7},{7,6},{8,9},{9,8},{10,11... | collective-permute-start | bytes 552968 | tf_op jit(solution)/shard_map/ppermute | solution.py:349
  30.2 12.2 %collective-permute-start.18 = (bf16[80,1152]{1,0:T(8,128)(2,1)S(1)}, bf16[80,1152]{1,0:T(8,128)(2,1)S(1)}, u32[]{:S(2)}, u32[]{:S(2)}) collective-permute-start(bf16[80,1152]{1,0:T(8,128)(2,1)S(1)} %collective-permute-done.16.refs_0_), channel_id=1, source_target_pairs={{0,16},{1,17},{2,18},{3,19},{4,20},{5,21},{6,22},{7,23},{8,24},{9,... | collective-permute-start | bytes 552968 | tf_op jit(solution)/shard_map/ppermute | solution.py:349
  31.6 12.5 %collective-permute-start.17 = (bf16[80,1152]{1,0:T(8,128)(2,1)S(1)}, bf16[80,1152]{1,0:T(8,128)(2,1)S(1)}, u32[]{:S(2)}, u32[]{:S(2)}) collective-permute-start(bf16[80,1152]{1,0:T(8,128)(2,1)S(1)} %collective-permute-done.16.refs_0_), channel_id=1, source_target_pairs={{0,1},{1,0},{2,3},{3,2},{4,5},{5,4},{6,7},{7,6},{8,9},{9,8},{10,11... | collective-permute-start | bytes 552968 | tf_op jit(solution)/shard_map/ppermute | solution.py:349
  33.1 7.6 %collective-permute-start.2 = (bf16[48,1152]{1,0:T(8,128)(2,1)S(1)}, bf16[48,1152]{1,0:T(8,128)(2,1)S(1)}, u32[]{:S(2)}, u32[]{:S(2)}) collective-permute-start(bf16[48,1152]{1,0:T(8,128)(2,1)S(1)} %slice.96), channel_id=1, source_target_pairs={{0,1},{1,0},{2,3},{3,2},{4,5},{5,4},{6,7},{7,6},{8,9},{9,8},{10,11... | collective-permute-start | bytes 331784 | tf_op jit(solution)/shard_map/ppermute | solution.py:349
  33.7 10.8 %collective-permute-start.7 = (bf16[48,1152]{1,0:T(8,128)(2,1)S(1)}, bf16[48,1152]{1,0:T(8,128)(2,1)S(1)}, u32[]{:S(2)}, u32[]{:S(2)}) collective-permute-start(bf16[48,1152]{1,0:T(8,128)(2,1)S(1)} %slice.98), channel_id=1, source_target_pairs={{0,1},{1,0},{2,3},{3,2},{4,5},{5,4},{6,7},{7,6},{8,9},{9,8},{10,11... | collective-permute-start | bytes 331784 | tf_op jit(solution)/shard_map/ppermute | solution.py:349
  35.3 8.8 %collective-permute-start.8 = (bf16[32,1152]{1,0:T(8,128)(2,1)S(1)}, bf16[32,1152]{1,0:T(8,128)(2,1)S(1)}, u32[]{:S(2)}, u32[]{:S(2)}) collective-permute-start(bf16[32,1152]{1,0:T(8,128)(2,1)S(1)} %slice.99), channel_id=1, source_target_pairs={{0,16},{1,17},{2,18},{3,19},{4,20},{5,21},{6,22},{7,23},{8,24},{9,... | collective-permute-start | bytes 221192 | tf_op jit(solution)/shard_map/ppermute | solution.py:349
  40.8 6.6 %collective-permute-start.13 = (bf16[48,1152]{1,0:T(8,128)(2,1)S(1)}, bf16[48,1152]{1,0:T(8,128)(2,1)S(1)}, u32[]{:S(2)}, u32[]{:S(2)}) collective-permute-start(bf16[48,1152]{1,0:T(8,128)(2,1)S(1)} %slice.100), channel_id=1, source_target_pairs={{0,1},{1,0},{2,3},{3,2},{4,5},{5,4},{6,7},{7,6},{8,9},{9,8},{10,11... | collective-permute-start | bytes 331784 | tf_op jit(solution)/shard_map/ppermute | solution.py:349
  44.1 6.8 %collective-permute-start.9 = (bf16[2,4,320,128]{3,2,1,0:T(8,128)(2,1)S(1)}, bf16[2,4,320,128]{3,2,1,0:T(8,128)(2,1)S(1)}, u32[]{:S(2)}, u32[]{:S(2)}) collective-permute-start(bf16[2,4,320,128]{3,2,1,0:T(8,128)(2,1)S(1)} %get-tuple-element.23.refs_1_), channel_id=1, source_target_pairs={{0,8},{1,9},{2,10},{3,11},{4,12},{5,13},{6,14},{7,15},{8,0},{9,1},... | collective-permute-start | bytes 1966088 | tf_op jit(solution)/shard_map/ppermute | solution.py:349
  72.8 9.7 %collective-permute-start.24 = (bf16[4,192,128]{2,1,0:T(8,128)(2,1)S(1)}, bf16[4,192,128]{2,1,0:T(8,128)(2,1)S(1)}, u32[]{:S(2)}, u32[]{:S(2)}) collective-permute-start(bf16[4,192,128]{2,1,0:T(8,128)(2,1)S(1)} %get-tuple-element.31), channel_id=1, source_target_pairs={{0,6},{1,7},{2,4},{3,5},{4,2},{5,3},{6,0},{7,1},{8,14},{9,15},{10,... | collective-permute-start | bytes 589832 | tf_op jit(solution)/shard_map/ppermute | solution.py:349
  75.0 14.4 %collective-permute-start.23 = (bf16[4,192,128]{2,1,0:T(8,128)(2,1)S(1)}, bf16[4,192,128]{2,1,0:T(8,128)(2,1)S(1)}, u32[]{:S(2)}, u32[]{:S(2)}) collective-permute-start(bf16[4,192,128]{2,1,0:T(8,128)(2,1)S(1)} %attend.6), channel_id=1, source_target_pairs={{0,2},{1,3},{2,0},{3,1},{4,6},{5,7},{6,4},{7,5},{8,10},{9,11},{10,... | collective-permute-start | bytes 589832 | tf_op jit(solution)/shard_map/ppermute | solution.py:349
  75.0 17.1 %collective-permute-start.28 = (bf16[4,192,128]{2,1,0:T(8,128)(2,1)S(1)}, bf16[4,192,128]{2,1,0:T(8,128)(2,1)S(1)}, u32[]{:S(2)}, u32[]{:S(2)}) collective-permute-start(bf16[4,192,128]{2,1,0:T(8,128)(2,1)S(1)} %attend.7), channel_id=1, source_target_pairs={{0,4},{1,5},{2,6},{3,7},{4,0},{5,1},{6,2},{7,3},{8,12},{9,13},{10,... | collective-permute-start | bytes 589832 | tf_op jit(solution)/shard_map/ppermute | solution.py:349
  89.4 13.5 %collective-permute-start.25 = (bf16[3,192,128]{2,1,0:T(8,128)(2,1)S(1)}, bf16[3,192,128]{2,1,0:T(8,128)(2,1)S(1)}, u32[]{:S(2)}, u32[]{:S(2)}) collective-permute-start(bf16[3,192,128]{2,1,0:T(8,128)(2,1)S(1)} %pad_maximum_fusion.1), channel_id=1, source_target_pairs={{0,1},{1,0},{2,3},{3,2},{4,5},{5,4},{6,7},{7,6},{8,9},{9,8},{10,11... | collective-permute-start | bytes 442376 | tf_op jit(solution)/shard_map/ppermute | solution.py:349
  90.5 12.3 %collective-permute-start.26 = (bf16[3,192,128]{2,1,0:T(8,128)(2,1)S(1)}, bf16[3,192,128]{2,1,0:T(8,128)(2,1)S(1)}, u32[]{:S(2)}, u32[]{:S(2)}) collective-permute-start(bf16[3,192,128]{2,1,0:T(8,128)(2,1)S(1)} %pad_maximum_fusion.2), channel_id=1, source_target_pairs={{0,16},{1,17},{2,18},{3,19},{4,20},{5,21},{6,22},{7,23},{8,24},{9,... | collective-permute-start | bytes 442376 | tf_op jit(solution)/shard_map/ppermute | solution.py:349
  92.1 6.7 %collective-permute-start.31 = (bf16[1,192,128]{2,1,0:T(8,128)(2,1)S(1)}, bf16[1,192,128]{2,1,0:T(8,128)(2,1)S(1)}, u32[]{:S(2)}, u32[]{:S(2)}) collective-permute-start(bf16[1,192,128]{2,1,0:T(8,128)(2,1)S(1)} %get-tuple-element.33), channel_id=1, source_target_pairs={{0,17},{1,16},{2,19},{3,18},{4,21},{5,20},{6,23},{7,22},{8,25},{9,... | collective-permute-start | bytes 147464 | tf_op jit(solution)/shard_map/ppermute | solution.py:349
  93.1 9.8 %collective-permute-start.27 = (bf16[3,192,128]{2,1,0:T(8,128)(2,1)S(1)}, bf16[3,192,128]{2,1,0:T(8,128)(2,1)S(1)}, u32[]{:S(2)}, u32[]{:S(2)}) collective-permute-start(bf16[3,192,128]{2,1,0:T(8,128)(2,1)S(1)} %pad_maximum_fusion.3), channel_id=1, source_target_pairs={{0,17},{1,16},{2,19},{3,18},{4,21},{5,20},{6,23},{7,22},{8,25},{9,... | collective-permute-start | bytes 442376 | tf_op jit(solution)/shard_map/ppermute | solution.py:349
  95.2 6.1 %collective-permute-start.30 = (bf16[1,192,128]{2,1,0:T(8,128)(2,1)S(1)}, bf16[1,192,128]{2,1,0:T(8,128)(2,1)S(1)}, u32[]{:S(2)}, u32[]{:S(2)}) collective-permute-start(bf16[1,192,128]{2,1,0:T(8,128)(2,1)S(1)} %get-tuple-element.34), channel_id=1, source_target_pairs={{0,16},{1,17},{2,18},{3,19},{4,20},{5,21},{6,22},{7,23},{8,24},{9,... | collective-permute-start | bytes 147464 | tf_op jit(solution)/shard_map/ppermute | solution.py:349
  (16 other events, 322.8 us)

commit v3 on v2

--- a/solution.py
+++ b/solution.py
@@ -228,10 +228,11 @@
     return jnp.concatenate(columns, axis=1)
 
 
-def attend_kernel(chips, capacity, piece_count, *refs):
-    q_ref, pieces, out_ref = refs[0], refs[1 : 1 + piece_count], refs[1 + piece_count]
+def attend_kernel(chips, capacity, query_count, piece_count, *refs):
+    queries, pieces = refs[:query_count], refs[query_count : query_count + piece_count]
+    out_ref = refs[query_count + piece_count]
     if piece_count > 1:
-        kv_ref = refs[2 + piece_count]
+        kv_ref = refs[-1]
         at = 0
         for ref in pieces:
             kv_ref[:, :, at : at + ref.shape[2]] = ref[...]
@@ -240,8 +241,9 @@
         kv_ref = pieces[0]
     nt = (((1,), (1,)), ((), ()))
     results = []
-    for head in range(q_ref.shape[0]):
-        score = lax.dot_general(q_ref[head], kv_ref[0, head], nt, preferred_element_type=F32)
+    for head in range(kv_ref.shape[1]):
+        query = jnp.concatenate([ref[head] for ref in queries], axis=0)
+        score = lax.dot_general(query, kv_ref[0, head], nt, preferred_element_type=F32)
         top = jnp.max(score, axis=1, keepdims=True)
         probs = jnp.exp2(score - top).astype(BF16)
         mixed = jnp.dot(probs, kv_ref[1, head], preferred_element_type=F32)
@@ -257,25 +259,25 @@
 
 
 def attend(queries, pieces, chips, capacity):
-    head_count = queries.shape[0]
+    head_count, rows = queries[0].shape[0], sum(query.shape[1] for query in queries)
     keys = sum(piece.shape[2] for piece in pieces)
     out_rows = packed_rows(capacity, head_count * HD)[0]
     out_shape = [jax.ShapeDtypeStruct((chips, out_rows, LANE), BF16)]
     if len(pieces) > 1:
         out_shape.append(jax.ShapeDtypeStruct((2, head_count, keys, LANE), BF16))
     made = pl.pallas_call(
-        functools.partial(attend_kernel, chips, capacity, len(pieces)),
-        in_specs=[vmem()] * (1 + len(pieces)),
+        functools.partial(attend_kernel, chips, capacity, len(queries), len(pieces)),
+        in_specs=[vmem()] * (len(queries) + len(pieces)),
         out_specs=[vmem()] * len(out_shape),
         out_shape=out_shape,
         cost_estimate=pl.CostEstimate(
-            flops=4 * head_count * queries.shape[1] * keys * LANE,
+            flops=4 * head_count * rows * keys * LANE,
             bytes_accessed=4 * head_count * keys * LANE,
-            transcendentals=head_count * queries.shape[1] * keys,
+            transcendentals=head_count * rows * keys,
         ),
         compiler_params=limit(24),
         name="attend",
-    )(queries, *pieces)
+    )(*queries, *pieces)
     return made[0], (made[1] if len(pieces) > 1 else pieces[0])
 
 
@@ -359,16 +361,21 @@
     blocks = [block if k == 0 else swap(block, dz=k) for k, block in enumerate(blocks)]
     half = round_up(capacity, 32) // 2
     queries, pieces = [], []
-    for block in blocks:
+    for k, block in enumerate(blocks):
         if across == 2 and along == 2:
             from_x, from_y = swap(block, dx=1), swap(block, dy=1)
             upper, lower = swap(from_x[:half], dy=1), swap(from_y[half:], dx=1)
             parts = [block, from_y, from_x, upper, lower]
         else:
             parts = [swap(block, dx=j // along, dy=j % along) if j else block for j in range(chips)]
-        query, kv = project(parts, weights, head_count)
-        queries.append(query)
-        pieces += [kv, swap(kv, core=1)]
+        groups = [parts]
+        if k == bags - 1 and len(parts) > chips:
+            groups = [parts[: chips - 1], parts[chips - 1 :]]
+        queries.append([])
+        for group in groups:
+            query, kv = project(group, weights, head_count)
+            queries[k].append(query)
+            pieces += [kv, swap(kv, core=1)]
     mixed = [None] * bags
     for k in reversed(range(bags)):
         part, kv = attend(queries[k], pieces, chips, capacity)

time: 109 us -> 109 us (level)
  waiting for transfers between devices: 34.9 us -> 31.9 us
  starting transfers between devices: 37.9 us -> 40.2 us
    ppermute x32 -> x33, waiting for transfers between devices: 34.9 us -> 31.9 us  [swap(): return lax.ppermute(value, AXES, pairs)]
    ppermute x32 -> x33, starting transfers between devices: 37.9 us -> 40.2 us  [swap(): return lax.ppermute(value, AXES, pairs)]
    pallas_call x4 -> x5, Pallas kernels: 4.54 us -> 4.95 us  [project(): pl.pallas_call(functools.partial(project_kernel, head_count), in_specs=[v...]
  transfers between devices with their start and end apart: 32 -> 33, of which waited for: 12 -> 13; matrix products, arithmetic and copies ran while one was open for 0% -> 0% of each run, Pallas kernels for 7% -> 7%
where the time goes in v3:
time: 109 us
  starting transfers between devices  40.2 us (37%)
  Pallas kernels  36.1 us (33%)
  waiting for transfers between devices  31.9 us (29%)
    ppermute x33, starting transfers between devices, swap(): return lax.ppermute(value, AXES, pairs)  40.2 us
    ppermute x33, waiting for transfers between devices, swap(): return lax.ppermute(value, AXES, pairs)  31.9 us
    pallas_call x4, Pallas kernels, attend(): pl.pallas_call(functools.partial(attend_kernel, chips, capacity, len(quer...  19.8 us
    pallas_call x1, Pallas kernels, finish(): pl.pallas_call(functools.partial(finish_kernel, capacity, chips, rounds),...  6.23 us
    pallas_call x5, Pallas kernels, project(): pl.pallas_call(functools.partial(project_kernel, head_count), in_specs=[v...  4.95 us
    pallas_call x1, Pallas kernels, chip_weights(): pl.pallas_call(functools.partial(weight_kernel, part), in_specs=[hbm()],...  3.16 us
  transfers between devices with their start and end apart: 33, of which 13 were waited for; matrix products, arithmetic and copies ran while one was open for 0% of the time, Pallas kernels for 7%

profile of v3, /device:TPU:0, one launch (start us, length us, event | category | flops | bytes accessed | tf_op | source)
XLA Modules:
  0.0 108.9 jit_solution(11368272100580038067)
XLA Ops:
  0.0 2.0 %slot_rows.1 = (bf16[80,1152]{1,0:T(8,128)(2,1)S(1)}, bf16[80,1152]{1,0:T(8,128)(2,1)S(1)}, bf16[80,1152]{1,0:T(8,128)(2,1)S(1)}, bf16[80,1152]{1,0:T(8,128)(2,1)S(1)}) custom-call(bf16[256,1152]{1,0:T(8,128)(2,1)} %tokens_ref.3, s32[1,256]{1,0:T(1,128)} %bitcast.8, f32[6,4,1152]{2,1,0:T(4,128)} %bitcast.6), custom_call_target="tpu_custom_call" | custom-call | tf_op jit(solution)/shard_map/slot_rows/pallas_call | solution.py:80
  2.0 3.1 %collective-permute-start.10 = (bf16[80,1152]{1,0:T(8,128)(2,1)S(1)}, bf16[80,1152]{1,0:T(8,128)(2,1)S(1)}, u32[]{:S(2)}, u32[]{:S(2)}) collective-permute-start(bf16[80,1152]{1,0:T(8,128)(2,1)S(1)} %get-tuple-element.27), channel_id=1, source_target_pairs={{0,2},{1,3},{2,0},{3,1},{4,6},{5,7},{6,4},{7,5},{8,10},{9,11},{10,... | collective-permute-start | bytes 552968 | tf_op jit(solution)/shard_map/ppermute | solution.py:351
  5.1 2.6 %collective-permute-start.16 = (bf16[80,1152]{1,0:T(8,128)(2,1)S(1)}, bf16[80,1152]{1,0:T(8,128)(2,1)S(1)}, u32[]{:S(2)}, u32[]{:S(2)}) collective-permute-start(bf16[80,1152]{1,0:T(8,128)(2,1)S(1)} %get-tuple-element.29), channel_id=1, source_target_pairs={{0,4},{1,5},{2,6},{3,7},{4,0},{5,1},{6,2},{7,3},{8,12},{9,13},{10,... | collective-permute-start | bytes 552968 | tf_op jit(solution)/shard_map/ppermute | solution.py:351
  10.7 2.9 %collective-permute-done.10.refs_0_ = bf16[80,1152]{1,0:T(8,128)(2,1)S(1)} collective-permute-done((bf16[80,1152]{1,0:T(8,128)(2,1)S(1)}, bf16[80,1152]{1,0:T(8,128)(2,1)S(1)}, u32[]{:S(2)}, u32[]{:S(2)}) %collective-permute-start.10) | collective-permute-done | bytes 184352 | tf_op jit(solution)/shard_map/ppermute | solution.py:351
  13.6 1.7 %collective-permute-start.12 = (bf16[80,1152]{1,0:T(8,128)(2,1)S(1)}, bf16[80,1152]{1,0:T(8,128)(2,1)S(1)}, u32[]{:S(2)}, u32[]{:S(2)}) collective-permute-start(bf16[80,1152]{1,0:T(8,128)(2,1)S(1)} %collective-permute-done.10.refs_0_), channel_id=1, source_target_pairs={{0,16},{1,17},{2,18},{3,19},{4,20},{5,21},{6,22},{7,23},{8,24},{9,... | collective-permute-start | bytes 552968 | tf_op jit(solution)/shard_map/ppermute | solution.py:351
  15.3 1.5 %collective-permute-start.11 = (bf16[80,1152]{1,0:T(8,128)(2,1)S(1)}, bf16[80,1152]{1,0:T(8,128)(2,1)S(1)}, u32[]{:S(2)}, u32[]{:S(2)}) collective-permute-start(bf16[80,1152]{1,0:T(8,128)(2,1)S(1)} %collective-permute-done.10.refs_0_), channel_id=1, source_target_pairs={{0,1},{1,0},{2,3},{3,2},{4,5},{5,4},{6,7},{7,6},{8,9},{9,8},{10,11... | collective-permute-start | bytes 552968 | tf_op jit(solution)/shard_map/ppermute | solution.py:351
  16.8 2.5 %collective-permute-start.4 = (bf16[80,1152]{1,0:T(8,128)(2,1)S(1)}, bf16[80,1152]{1,0:T(8,128)(2,1)S(1)}, u32[]{:S(2)}, u32[]{:S(2)}) collective-permute-start(bf16[80,1152]{1,0:T(8,128)(2,1)S(1)} %get-tuple-element.23), channel_id=1, source_target_pairs={{0,6},{1,7},{2,4},{3,5},{4,2},{5,3},{6,0},{7,1},{8,14},{9,15},{10,... | collective-permute-start | bytes 552968 | tf_op jit(solution)/shard_map/ppermute | solution.py:351
  25.2 1.8 %collective-permute-start.14 = (bf16[32,1152]{1,0:T(8,128)(2,1)S(1)}, bf16[32,1152]{1,0:T(8,128)(2,1)S(1)}, u32[]{:S(2)}, u32[]{:S(2)}) collective-permute-start(bf16[32,1152]{1,0:T(8,128)(2,1)S(1)} %slice.101), channel_id=1, source_target_pairs={{0,16},{1,17},{2,18},{3,19},{4,20},{5,21},{6,22},{7,23},{8,24},{9,... | collective-permute-start | bytes 221192 | tf_op jit(solution)/shard_map/ppermute | solution.py:351
  27.0 3.2 %chip_weights.1.refs_5_.refs_3_.refs_2_ = bf16[1152,896]{1,0:T(8,128)(2,1)S(1)} custom-call(bf16[1152,3456]{1,0:T(8,128)(2,1)} %w_ref.1), custom_call_target="tpu_custom_call" | custom-call | flops 1000000000 | bytes 10000000 | tf_op jit(solution)/shard_map/chip_weights/pallas_call | solution.py:122
  41.6 3.9 %collective-permute-done.8.refs_1_ = bf16[32,1152]{1,0:T(8,128)(2,1)S(1)} collective-permute-done((bf16[32,1152]{1,0:T(8,128)(2,1)S(1)}, bf16[32,1152]{1,0:T(8,128)(2,1)S(1)}, u32[]{:S(2)}, u32[]{:S(2)}) %collective-permute-start.8) | collective-permute-done | bytes 73760 | tf_op jit(solution)/shard_map/ppermute | solution.py:351
  46.9 3.3 %collective-permute-done.7.refs_0_ = bf16[48,1152]{1,0:T(8,128)(2,1)S(1)} collective-permute-done((bf16[48,1152]{1,0:T(8,128)(2,1)S(1)}, bf16[48,1152]{1,0:T(8,128)(2,1)S(1)}, u32[]{:S(2)}, u32[]{:S(2)}) %collective-permute-start.7) | collective-permute-done | bytes 110624 | tf_op jit(solution)/shard_map/ppermute | solution.py:351
  52.3 5.1 %attend.4 = (bf16[4,192,128]{2,1,0:T(8,128)(2,1)S(1)}, bf16[2,4,2560,128]{3,2,1,0:T(8,128)(2,1)S(1)}) custom-call(bf16[4,240,128]{2,1,0:T(8,128)(2,1)S(1)} %get-tuple-element.24.refs_0_, bf16[4,80,128]{2,1,0:T(8,128)(2,1)S(1)} %get-tuple-element.25.refs_1_, bf16[2,4,320,128]{3,2,1,0:T(8,128)(2,1)S(1)} %get-tuple-element.26.refs_2_, ...), custom_call_target="tpu_custom_call" | custom-call | flops 1677721600 | bytes 5242880 | tf_op jit(solution)/shard_map/attend/pallas_call | solution.py:268
  57.4 4.8 %attend.7 = bf16[4,192,128]{2,1,0:T(8,128)(2,1)S(1)} custom-call(bf16[4,320,128]{2,1,0:T(8,128)(2,1)S(1)} %get-tuple-element.36.refs_0_, bf16[2,4,2560,128]{3,2,1,0:T(8,128)(2,1)S(1)} %get-tuple-element.33.refs_1_), custom_call_target="tpu_custom_call" | custom-call | flops 1677721600 | bytes 5242880 | tf_op jit(solution)/shard_map/attend/pallas_call | solution.py:268
  62.2 4.8 %attend.6 = bf16[4,192,128]{2,1,0:T(8,128)(2,1)S(1)} custom-call(bf16[4,320,128]{2,1,0:T(8,128)(2,1)S(1)} %get-tuple-element.34.refs_0_, bf16[2,4,2560,128]{3,2,1,0:T(8,128)(2,1)S(1)} %get-tuple-element.33.refs_1_), custom_call_target="tpu_custom_call" | custom-call | flops 1677721600 | bytes 5242880 | tf_op jit(solution)/shard_map/attend/pallas_call | solution.py:268
  67.1 5.1 %attend.5 = bf16[4,192,128]{2,1,0:T(8,128)(2,1)S(1)} custom-call(bf16[4,320,128]{2,1,0:T(8,128)(2,1)S(1)} %get-tuple-element.22.refs_0_, bf16[2,4,2560,128]{3,2,1,0:T(8,128)(2,1)S(1)} %get-tuple-element.33.refs_1_), custom_call_target="tpu_custom_call" | custom-call | flops 1677721600 | bytes 5242880 | tf_op jit(solution)/shard_map/attend/pallas_call | solution.py:268
  72.1 2.0 %collective-permute-start.25 = (bf16[4,192,128]{2,1,0:T(8,128)(2,1)S(1)}, bf16[4,192,128]{2,1,0:T(8,128)(2,1)S(1)}, u32[]{:S(2)}, u32[]{:S(2)}) collective-permute-start(bf16[4,192,128]{2,1,0:T(8,128)(2,1)S(1)} %get-tuple-element.35), channel_id=1, source_target_pairs={{0,6},{1,7},{2,4},{3,5},{4,2},{5,3},{6,0},{7,1},{8,14},{9,15},{10,... | collective-permute-start | bytes 589832 | tf_op jit(solution)/shard_map/ppermute | solution.py:351
  74.6 1.9 %collective-permute-start.29 = (bf16[4,192,128]{2,1,0:T(8,128)(2,1)S(1)}, bf16[4,192,128]{2,1,0:T(8,128)(2,1)S(1)}, u32[]{:S(2)}, u32[]{:S(2)}) collective-permute-start(bf16[4,192,128]{2,1,0:T(8,128)(2,1)S(1)} %attend.7), channel_id=1, source_target_pairs={{0,4},{1,5},{2,6},{3,7},{4,0},{5,1},{6,2},{7,3},{8,12},{9,13},{10,... | collective-permute-start | bytes 589832 | tf_op jit(solution)/shard_map/ppermute | solution.py:351
  76.6 5.2 %collective-permute-done.25 = bf16[4,192,128]{2,1,0:T(8,128)(2,1)S(1)} collective-permute-done((bf16[4,192,128]{2,1,0:T(8,128)(2,1)S(1)}, bf16[4,192,128]{2,1,0:T(8,128)(2,1)S(1)}, u32[]{:S(2)}, u32[]{:S(2)}) %collective-permute-start.25) | collective-permute-done | bytes 196640 | tf_op jit(solution)/shard_map/ppermute | solution.py:351
  81.8 3.6 %collective-permute-done.24 = bf16[4,192,128]{2,1,0:T(8,128)(2,1)S(1)} collective-permute-done((bf16[4,192,128]{2,1,0:T(8,128)(2,1)S(1)}, bf16[4,192,128]{2,1,0:T(8,128)(2,1)S(1)}, u32[]{:S(2)}, u32[]{:S(2)}) %collective-permute-start.24) | collective-permute-done | bytes 196640 | tf_op jit(solution)/shard_map/ppermute | solution.py:351
  85.5 1.9 %collective-permute-start.26 = (bf16[3,192,128]{2,1,0:T(8,128)(2,1)S(1)}, bf16[3,192,128]{2,1,0:T(8,128)(2,1)S(1)}, u32[]{:S(2)}, u32[]{:S(2)}) collective-permute-start(bf16[3,192,128]{2,1,0:T(8,128)(2,1)S(1)} %pad_maximum_fusion.1), channel_id=1, source_target_pairs={{0,1},{1,0},{2,3},{3,2},{4,5},{5,4},{6,7},{7,6},{8,9},{9,8},{10,11... | collective-permute-start | bytes 442376 | tf_op jit(solution)/shard_map/ppermute | solution.py:351
  87.4 5.7 %collective-permute-done.29 = bf16[4,192,128]{2,1,0:T(8,128)(2,1)S(1)} collective-permute-done((bf16[4,192,128]{2,1,0:T(8,128)(2,1)S(1)}, bf16[4,192,128]{2,1,0:T(8,128)(2,1)S(1)}, u32[]{:S(2)}, u32[]{:S(2)}) %collective-permute-start.29) | collective-permute-done | bytes 196640 | tf_op jit(solution)/shard_map/ppermute | solution.py:351
  93.1 1.5 %collective-permute-start.32 = (bf16[1,192,128]{2,1,0:T(8,128)(2,1)S(1)}, bf16[1,192,128]{2,1,0:T(8,128)(2,1)S(1)}, u32[]{:S(2)}, u32[]{:S(2)}) collective-permute-start(bf16[1,192,128]{2,1,0:T(8,128)(2,1)S(1)} %get-tuple-element.37), channel_id=1, source_target_pairs={{0,17},{1,16},{2,19},{3,18},{4,21},{5,20},{6,23},{7,22},{8,25},{9,... | collective-permute-start | bytes 147464 | tf_op jit(solution)/shard_map/ppermute | solution.py:351
  99.9 1.8 %collective-permute-done.31.refs_6_ = bf16[1,192,128]{2,1,0:T(8,128)(2,1)S(1)} collective-permute-done((bf16[1,192,128]{2,1,0:T(8,128)(2,1)S(1)}, bf16[1,192,128]{2,1,0:T(8,128)(2,1)S(1)}, u32[]{:S(2)}, u32[]{:S(2)}) %collective-permute-start.31) | collective-permute-done | bytes 49184 | tf_op jit(solution)/shard_map/ppermute | solution.py:351
  102.7 6.2 %finish.1 = bf16[256,1152]{1,0:T(8,128)(2,1)} custom-call(bf16[256,1152]{1,0:T(8,128)(2,1)S(1)} %copy-done.1, s32[1,256]{1,0:T(1,128)S(1)} %bitcast.9, f32[6,4,1152]{2,1,0:T(4,128)S(1)} %bitcast.7, bf16[1152,1152]{1,0:T(8,128)(2,1)S(1)} %copy-done, bf16[1152,2304]{1,0:T(8,128)(2,1)S(1)} %bitcast.3, bf16[2304,1152]{1,0:T(8,128)(2,1)S(1)} %bitcast.5, ...), custom_call_target="tpu_custom_call" | custom-call | tf_op jit(solution)/shard_map/finish/pallas_call | solution.py:325
  (88 shorter events, 30.4 us)
Async XLA Ops:
  2.0 11.6 %collective-permute-start.10 = (bf16[80,1152]{1,0:T(8,128)(2,1)S(1)}, bf16[80,1152]{1,0:T(8,128)(2,1)S(1)}, u32[]{:S(2)}, u32[]{:S(2)}) collective-permute-start(bf16[80,1152]{1,0:T(8,128)(2,1)S(1)} %get-tuple-element.27), channel_id=1, source_target_pairs={{0,2},{1,3},{2,0},{3,1},{4,6},{5,7},{6,4},{7,5},{8,10},{9,11},{10,... | collective-permute-start | bytes 552968 | tf_op jit(solution)/shard_map/ppermute | solution.py:351
  5.1 11.7 %collective-permute-start.16 = (bf16[80,1152]{1,0:T(8,128)(2,1)S(1)}, bf16[80,1152]{1,0:T(8,128)(2,1)S(1)}, u32[]{:S(2)}, u32[]{:S(2)}) collective-permute-start(bf16[80,1152]{1,0:T(8,128)(2,1)S(1)} %get-tuple-element.29), channel_id=1, source_target_pairs={{0,4},{1,5},{2,6},{3,7},{4,0},{5,1},{6,2},{7,3},{8,12},{9,13},{10,... | collective-permute-start | bytes 552968 | tf_op jit(solution)/shard_map/ppermute | solution.py:351
  7.7 11.5 %collective-permute-start.1 = (bf16[80,1152]{1,0:T(8,128)(2,1)S(1)}, bf16[80,1152]{1,0:T(8,128)(2,1)S(1)}, u32[]{:S(2)}, u32[]{:S(2)}) collective-permute-start(bf16[80,1152]{1,0:T(8,128)(2,1)S(1)} %get-tuple-element.21.refs_0_), channel_id=1, source_target_pairs={{0,16},{1,17},{2,18},{3,19},{4,20},{5,21},{6,22},{7,23},{8,24},{9,... | collective-permute-start | bytes 552968 | tf_op jit(solution)/shard_map/ppermute | solution.py:351
  9.2 10.9 %collective-permute-start = (bf16[80,1152]{1,0:T(8,128)(2,1)S(1)}, bf16[80,1152]{1,0:T(8,128)(2,1)S(1)}, u32[]{:S(2)}, u32[]{:S(2)}) collective-permute-start(bf16[80,1152]{1,0:T(8,128)(2,1)S(1)} %get-tuple-element.21.refs_0_), channel_id=1, source_target_pairs={{0,1},{1,0},{2,3},{3,2},{4,5},{5,4},{6,7},{7,6},{8,9},{9,8},{10,11... | collective-permute-start | bytes 552968 | tf_op jit(solution)/shard_map/ppermute | solution.py:351
  13.6 8.0 %collective-permute-start.12 = (bf16[80,1152]{1,0:T(8,128)(2,1)S(1)}, bf16[80,1152]{1,0:T(8,128)(2,1)S(1)}, u32[]{:S(2)}, u32[]{:S(2)}) collective-permute-start(bf16[80,1152]{1,0:T(8,128)(2,1)S(1)} %collective-permute-done.10.refs_0_), channel_id=1, source_target_pairs={{0,16},{1,17},{2,18},{3,19},{4,20},{5,21},{6,22},{7,23},{8,24},{9,... | collective-permute-start | bytes 552968 | tf_op jit(solution)/shard_map/ppermute | solution.py:351
  15.3 7.0 %collective-permute-start.11 = (bf16[80,1152]{1,0:T(8,128)(2,1)S(1)}, bf16[80,1152]{1,0:T(8,128)(2,1)S(1)}, u32[]{:S(2)}, u32[]{:S(2)}) collective-permute-start(bf16[80,1152]{1,0:T(8,128)(2,1)S(1)} %collective-permute-done.10.refs_0_), channel_id=1, source_target_pairs={{0,1},{1,0},{2,3},{3,2},{4,5},{5,4},{6,7},{7,6},{8,9},{9,8},{10,11... | collective-permute-start | bytes 552968 | tf_op jit(solution)/shard_map/ppermute | solution.py:351
  16.8 7.4 %collective-permute-start.4 = (bf16[80,1152]{1,0:T(8,128)(2,1)S(1)}, bf16[80,1152]{1,0:T(8,128)(2,1)S(1)}, u32[]{:S(2)}, u32[]{:S(2)}) collective-permute-start(bf16[80,1152]{1,0:T(8,128)(2,1)S(1)} %get-tuple-element.23), channel_id=1, source_target_pairs={{0,6},{1,7},{2,4},{3,5},{4,2},{5,3},{6,0},{7,1},{8,14},{9,15},{10,... | collective-permute-start | bytes 552968 | tf_op jit(solution)/shard_map/ppermute | solution.py:351
  20.1 10.1 %collective-permute-start.17 = (bf16[80,1152]{1,0:T(8,128)(2,1)S(1)}, bf16[80,1152]{1,0:T(8,128)(2,1)S(1)}, u32[]{:S(2)}, u32[]{:S(2)}) collective-permute-start(bf16[80,1152]{1,0:T(8,128)(2,1)S(1)} %collective-permute-done.16.refs_0_), channel_id=1, source_target_pairs={{0,1},{1,0},{2,3},{3,2},{4,5},{5,4},{6,7},{7,6},{8,9},{9,8},{10,11... | collective-permute-start | bytes 552968 | tf_op jit(solution)/shard_map/ppermute | solution.py:351
  21.6 10.0 %collective-permute-start.2 = (bf16[48,1152]{1,0:T(8,128)(2,1)S(1)}, bf16[48,1152]{1,0:T(8,128)(2,1)S(1)}, u32[]{:S(2)}, u32[]{:S(2)}) collective-permute-start(bf16[48,1152]{1,0:T(8,128)(2,1)S(1)} %slice.96), channel_id=1, source_target_pairs={{0,1},{1,0},{2,3},{3,2},{4,5},{5,4},{6,7},{7,6},{8,9},{9,8},{10,11... | collective-permute-start | bytes 331784 | tf_op jit(solution)/shard_map/ppermute | solution.py:351
  22.2 8.3 %collective-permute-start.3 = (bf16[32,1152]{1,0:T(8,128)(2,1)S(1)}, bf16[32,1152]{1,0:T(8,128)(2,1)S(1)}, u32[]{:S(2)}, u32[]{:S(2)}) collective-permute-start(bf16[32,1152]{1,0:T(8,128)(2,1)S(1)} %slice.97), channel_id=1, source_target_pairs={{0,16},{1,17},{2,18},{3,19},{4,20},{5,21},{6,22},{7,23},{8,24},{9,... | collective-permute-start | bytes 221192 | tf_op jit(solution)/shard_map/ppermute | solution.py:351
  24.2 11.4 %collective-permute-start.13 = (bf16[48,1152]{1,0:T(8,128)(2,1)S(1)}, bf16[48,1152]{1,0:T(8,128)(2,1)S(1)}, u32[]{:S(2)}, u32[]{:S(2)}) collective-permute-start(bf16[48,1152]{1,0:T(8,128)(2,1)S(1)} %slice.100), channel_id=1, source_target_pairs={{0,1},{1,0},{2,3},{3,2},{4,5},{5,4},{6,7},{7,6},{8,9},{9,8},{10,11... | collective-permute-start | bytes 331784 | tf_op jit(solution)/shard_map/ppermute | solution.py:351
  25.2 8.9 %collective-permute-start.14 = (bf16[32,1152]{1,0:T(8,128)(2,1)S(1)}, bf16[32,1152]{1,0:T(8,128)(2,1)S(1)}, u32[]{:S(2)}, u32[]{:S(2)}) collective-permute-start(bf16[32,1152]{1,0:T(8,128)(2,1)S(1)} %slice.101), channel_id=1, source_target_pairs={{0,16},{1,17},{2,18},{3,19},{4,20},{5,21},{6,22},{7,23},{8,24},{9,... | collective-permute-start | bytes 221192 | tf_op jit(solution)/shard_map/ppermute | solution.py:351
  30.2 8.4 %collective-permute-start.6 = (bf16[80,1152]{1,0:T(8,128)(2,1)S(1)}, bf16[80,1152]{1,0:T(8,128)(2,1)S(1)}, u32[]{:S(2)}, u32[]{:S(2)}) collective-permute-start(bf16[80,1152]{1,0:T(8,128)(2,1)S(1)} %collective-permute-done.4.refs_0_), channel_id=1, source_target_pairs={{0,16},{1,17},{2,18},{3,19},{4,20},{5,21},{6,22},{7,23},{8,24},{9,... | collective-permute-start | bytes 552968 | tf_op jit(solution)/shard_map/ppermute | solution.py:351
  30.5 6.8 %collective-permute-start.19 = (bf16[48,1152]{1,0:T(8,128)(2,1)S(1)}, bf16[48,1152]{1,0:T(8,128)(2,1)S(1)}, u32[]{:S(2)}, u32[]{:S(2)}) collective-permute-start(bf16[48,1152]{1,0:T(8,128)(2,1)S(1)} %slice.102), channel_id=1, source_target_pairs={{0,1},{1,0},{2,3},{3,2},{4,5},{5,4},{6,7},{7,6},{8,9},{9,8},{10,11... | collective-permute-start | bytes 331784 | tf_op jit(solution)/shard_map/ppermute | solution.py:351
  35.6 16.7 %collective-permute-start.9 = (bf16[2,4,320,128]{3,2,1,0:T(8,128)(2,1)S(1)}, bf16[2,4,320,128]{3,2,1,0:T(8,128)(2,1)S(1)}, u32[]{:S(2)}, u32[]{:S(2)}) collective-permute-start(bf16[2,4,320,128]{3,2,1,0:T(8,128)(2,1)S(1)} %get-tuple-element.26.refs_2_), channel_id=1, source_target_pairs={{0,8},{1,9},{2,10},{3,11},{4,12},{5,13},{6,14},{7,15},{8,0},{9,1},... | collective-permute-start | bytes 1966088 | tf_op jit(solution)/shard_map/ppermute | solution.py:351
  36.7 15.5 %collective-permute-start.15 = (bf16[2,4,320,128]{3,2,1,0:T(8,128)(2,1)S(1)}, bf16[2,4,320,128]{3,2,1,0:T(8,128)(2,1)S(1)}, u32[]{:S(2)}, u32[]{:S(2)}) collective-permute-start(bf16[2,4,320,128]{3,2,1,0:T(8,128)(2,1)S(1)} %get-tuple-element.28.refs_4_), channel_id=1, source_target_pairs={{0,8},{1,9},{2,10},{3,11},{4,12},{5,13},{6,14},{7,15},{8,0},{9,1},... | collective-permute-start | bytes 1966088 | tf_op jit(solution)/shard_map/ppermute | solution.py:351
  38.5 13.8 %collective-permute-start.21 = (bf16[2,4,320,128]{3,2,1,0:T(8,128)(2,1)S(1)}, bf16[2,4,320,128]{3,2,1,0:T(8,128)(2,1)S(1)}, u32[]{:S(2)}, u32[]{:S(2)}) collective-permute-start(bf16[2,4,320,128]{3,2,1,0:T(8,128)(2,1)S(1)} %get-tuple-element.30.refs_6_), channel_id=1, source_target_pairs={{0,8},{1,9},{2,10},{3,11},{4,12},{5,13},{6,14},{7,15},{8,0},{9,1},... | collective-permute-start | bytes 1966088 | tf_op jit(solution)/shard_map/ppermute | solution.py:351
  40.7 11.6 %collective-permute-start.22 = (bf16[2,4,240,128]{3,2,1,0:T(8,128)(2,1)S(1)}, bf16[2,4,240,128]{3,2,1,0:T(8,128)(2,1)S(1)}, u32[]{:S(2)}, u32[]{:S(2)}) collective-permute-start(bf16[2,4,240,128]{3,2,1,0:T(8,128)(2,1)S(1)} %get-tuple-element.31.refs_8_), channel_id=1, source_target_pairs={{0,8},{1,9},{2,10},{3,11},{4,12},{5,13},{6,14},{7,15},{8,0},{9,1},... | collective-permute-start | bytes 1474568 | tf_op jit(solution)/shard_map/ppermute | solution.py:351
  72.1 9.7 %collective-permute-start.25 = (bf16[4,192,128]{2,1,0:T(8,128)(2,1)S(1)}, bf16[4,192,128]{2,1,0:T(8,128)(2,1)S(1)}, u32[]{:S(2)}, u32[]{:S(2)}) collective-permute-start(bf16[4,192,128]{2,1,0:T(8,128)(2,1)S(1)} %get-tuple-element.35), channel_id=1, source_target_pairs={{0,6},{1,7},{2,4},{3,5},{4,2},{5,3},{6,0},{7,1},{8,14},{9,15},{10,... | collective-permute-start | bytes 589832 | tf_op jit(solution)/shard_map/ppermute | solution.py:351
  74.2 11.2 %collective-permute-start.24 = (bf16[4,192,128]{2,1,0:T(8,128)(2,1)S(1)}, bf16[4,192,128]{2,1,0:T(8,128)(2,1)S(1)}, u32[]{:S(2)}, u32[]{:S(2)}) collective-permute-start(bf16[4,192,128]{2,1,0:T(8,128)(2,1)S(1)} %attend.6), channel_id=1, source_target_pairs={{0,2},{1,3},{2,0},{3,1},{4,6},{5,7},{6,4},{7,5},{8,10},{9,11},{10,... | collective-permute-start | bytes 589832 | tf_op jit(solution)/shard_map/ppermute | solution.py:351
  74.6 18.5 %collective-permute-start.29 = (bf16[4,192,128]{2,1,0:T(8,128)(2,1)S(1)}, bf16[4,192,128]{2,1,0:T(8,128)(2,1)S(1)}, u32[]{:S(2)}, u32[]{:S(2)}) collective-permute-start(bf16[4,192,128]{2,1,0:T(8,128)(2,1)S(1)} %attend.7), channel_id=1, source_target_pairs={{0,4},{1,5},{2,6},{3,7},{4,0},{5,1},{6,2},{7,3},{8,12},{9,13},{10,... | collective-permute-start | bytes 589832 | tf_op jit(solution)/shard_map/ppermute | solution.py:351
  85.5 17.1 %collective-permute-start.26 = (bf16[3,192,128]{2,1,0:T(8,128)(2,1)S(1)}, bf16[3,192,128]{2,1,0:T(8,128)(2,1)S(1)}, u32[]{:S(2)}, u32[]{:S(2)}) collective-permute-start(bf16[3,192,128]{2,1,0:T(8,128)(2,1)S(1)} %pad_maximum_fusion.1), channel_id=1, source_target_pairs={{0,1},{1,0},{2,3},{3,2},{4,5},{5,4},{6,7},{7,6},{8,9},{9,8},{10,11... | collective-permute-start | bytes 442376 | tf_op jit(solution)/shard_map/ppermute | solution.py:351
  87.4 15.2 %collective-permute-start.27 = (bf16[3,192,128]{2,1,0:T(8,128)(2,1)S(1)}, bf16[3,192,128]{2,1,0:T(8,128)(2,1)S(1)}, u32[]{:S(2)}, u32[]{:S(2)}) collective-permute-start(bf16[3,192,128]{2,1,0:T(8,128)(2,1)S(1)} %pad_maximum_fusion.2), channel_id=1, source_target_pairs={{0,16},{1,17},{2,18},{3,19},{4,20},{5,21},{6,22},{7,23},{8,24},{9,... | collective-permute-start | bytes 442376 | tf_op jit(solution)/shard_map/ppermute | solution.py:351
  94.7 7.9 %collective-permute-start.28 = (bf16[3,192,128]{2,1,0:T(8,128)(2,1)S(1)}, bf16[3,192,128]{2,1,0:T(8,128)(2,1)S(1)}, u32[]{:S(2)}, u32[]{:S(2)}) collective-permute-start(bf16[3,192,128]{2,1,0:T(8,128)(2,1)S(1)} %pad_maximum_fusion.3), channel_id=1, source_target_pairs={{0,17},{1,16},{2,19},{3,18},{4,21},{5,20},{6,23},{7,22},{8,25},{9,... | collective-permute-start | bytes 442376 | tf_op jit(solution)/shard_map/ppermute | solution.py:351
  (17 other events, 336.6 us)

commit v4 on v3

--- a/solution.py
+++ b/solution.py
@@ -228,7 +228,7 @@
     return jnp.concatenate(columns, axis=1)
 
 
-def attend_kernel(chips, capacity, query_count, piece_count, *refs):
+def attend_kernel(chips, capacity, first_row, query_count, piece_count, *refs):
     queries, pieces = refs[:query_count], refs[query_count : query_count + piece_count]
     out_ref = refs[query_count + piece_count]
     if piece_count > 1:
@@ -243,6 +243,7 @@
     results = []
     for head in range(kv_ref.shape[1]):
         query = jnp.concatenate([ref[head] for ref in queries], axis=0)
+        query = query[first_row : first_row + chips * capacity]
         score = lax.dot_general(query, kv_ref[0, head], nt, preferred_element_type=F32)
         top = jnp.max(score, axis=1, keepdims=True)
         probs = jnp.exp2(score - top).astype(BF16)
@@ -258,15 +259,16 @@
         pack(block, write)
 
 
-def attend(queries, pieces, chips, capacity):
-    head_count, rows = queries[0].shape[0], sum(query.shape[1] for query in queries)
+def attend(queries, pieces, chips, capacity, index, halves):
+    chips //= halves
+    head_count, rows = queries[0].shape[0], chips * capacity
     keys = sum(piece.shape[2] for piece in pieces)
     out_rows = packed_rows(capacity, head_count * HD)[0]
     out_shape = [jax.ShapeDtypeStruct((chips, out_rows, LANE), BF16)]
     if len(pieces) > 1:
         out_shape.append(jax.ShapeDtypeStruct((2, head_count, keys, LANE), BF16))
     made = pl.pallas_call(
-        functools.partial(attend_kernel, chips, capacity, len(queries), len(pieces)),
+        functools.partial(attend_kernel, chips, capacity, index * rows, len(queries), len(pieces)),
         in_specs=[vmem()] * (len(queries) + len(pieces)),
         out_specs=[vmem()] * len(out_shape),
         out_shape=out_shape,
@@ -377,21 +379,29 @@
             queries[k].append(query)
             pieces += [kv, swap(kv, core=1)]
     mixed = [None] * bags
+    rounds = [[bags - 1], [k for k in range(bags - 1) if k != 2], [2]] if bags > 3 else [list(range(bags))]
+    shares = []
+
+    def exchange(index):
+        for j in range(chips):
+            share = jnp.stack([mixed[k][j] for k in rounds[index]])
+            shares.append(swap(share, dx=j // along, dy=j % along) if j else share)
+
     for k in reversed(range(bags)):
-        part, kv = attend(queries[k], pieces, chips, capacity)
-        pieces = [kv]
-        mixed[k] = swap(part, dz=k) if k else part
-    rounds = [[k for k in range(bags) if k != 2], [2]] if bags > 2 else [list(range(bags))]
-    shares = []
-    for members in rounds:
-        for j in range(chips):
-            share = jnp.stack([mixed[k][j] for k in members])
-            shares.append(swap(share, dx=j // along, dy=j % along) if j else share)
-    return finish(tokens, seq_row, modulation, shares, rounds, w_out, w_fc1, w_fc2, capacity, chips)
+        halves = 2 if k == bags - 1 and chips % 2 == 0 else 1
+        mixed[k] = []
+        for index in range(halves):
+            part, kv = attend(queries[k], pieces, chips, capacity, index, halves)
+            pieces = [kv]
+            part = swap(part, dz=k) if k else part
+            mixed[k] += [part[j] for j in range(part.shape[0])]
+    for index in range(len(rounds)):
+        exchange(index)
+    return finish(
+        tokens, seq_row, modulation, shares, rounds, w_out, w_fc1, w_fc2, capacity, chips
+    )
 
 
 def solution(mesh):
     placed = (P(("bag", "sp"), None), P(("bag", "sp")), P(), P(), P(), P(), P())
-    return jax.shard_map(
-        layer, mesh=mesh, in_specs=placed, out_specs=P(("bag", "sp"), None), check_vma=False
-    )
+    return jax.shard_map(layer, mesh=mesh, in_specs=placed, out_specs=P(("bag", "sp"), None), check_vma=False)

time: 109 us -> 105 us (0.963)
  waiting for transfers between devices: 31.9 us -> 20.8 us
  starting transfers between devices: 40.2 us -> 46.5 us
    ppermute x33 -> x37, waiting for transfers between devices: 31.9 us -> 20.8 us  [swap(): return lax.ppermute(value, AXES, pairs)]
    ppermute x33 -> x37, starting transfers between devices: 40.2 us -> 46.5 us  [swap(): return lax.ppermute(value, AXES, pairs)]
    pallas_call x4 -> x5, Pallas kernels: 19.8 us -> 20.7 us  [attend(): pl.pallas_call(functools.partial(attend_kernel, chips, capacity, index *...]
  transfers between devices with their start and end apart: 33 -> 37, of which waited for: 13 -> 11; matrix products, arithmetic and copies ran while one was open for 0% -> 0% of each run, Pallas kernels for 7% -> 13%
where the time goes in v4:
time: 105 us
  starting transfers between devices  46.5 us (44%)
  Pallas kernels  37 us (35%)
  waiting for transfers between devices  20.8 us (20%)
    ppermute x37, starting transfers between devices, swap(): return lax.ppermute(value, AXES, pairs)  46.5 us
    ppermute x37, waiting for transfers between devices, swap(): return lax.ppermute(value, AXES, pairs)  20.8 us
    pallas_call x5, Pallas kernels, attend(): pl.pallas_call(functools.partial(attend_kernel, chips, capacity, index *...  20.7 us
    pallas_call x1, Pallas kernels, finish(): pl.pallas_call(functools.partial(finish_kernel, capacity, chips, rounds),...  6.23 us
    pallas_call x5, Pallas kernels, project(): pl.pallas_call(functools.partial(project_kernel, head_count), in_specs=[v...  4.96 us
    pallas_call x1, Pallas kernels, chip_weights(): pl.pallas_call(functools.partial(weight_kernel, part), in_specs=[hbm()],...  3.16 us
  transfers between devices with their start and end apart: 37, of which 11 were waited for; matrix products, arithmetic and copies ran while one was open for 0% of the time, Pallas kernels for 13%

profile of v4, /device:TPU:0, one launch (start us, length us, event | category | flops | bytes accessed | tf_op | source)
XLA Modules:
  0.0 104.9 jit_solution(9709739959994503676)
XLA Ops:
  0.0 2.0 %slot_rows.1 = (bf16[80,1152]{1,0:T(8,128)(2,1)S(1)}, bf16[80,1152]{1,0:T(8,128)(2,1)S(1)}, bf16[80,1152]{1,0:T(8,128)(2,1)S(1)}, bf16[80,1152]{1,0:T(8,128)(2,1)S(1)}) custom-call(bf16[256,1152]{1,0:T(8,128)(2,1)} %tokens_ref.3, s32[1,256]{1,0:T(1,128)} %bitcast.8, f32[6,4,1152]{2,1,0:T(4,128)} %bitcast.6), custom_call_target="tpu_custom_call" | custom-call | tf_op jit(solution)/shard_map/slot_rows/pallas_call | solution.py:80
  2.0 3.1 %collective-permute-start.10 = (bf16[80,1152]{1,0:T(8,128)(2,1)S(1)}, bf16[80,1152]{1,0:T(8,128)(2,1)S(1)}, u32[]{:S(2)}, u32[]{:S(2)}) collective-permute-start(bf16[80,1152]{1,0:T(8,128)(2,1)S(1)} %get-tuple-element.26), channel_id=1, source_target_pairs={{0,2},{1,3},{2,0},{3,1},{4,6},{5,7},{6,4},{7,5},{8,10},{9,11},{10,... | collective-permute-start | bytes 552968 | tf_op jit(solution)/shard_map/ppermute | solution.py:353
  5.1 2.6 %collective-permute-start.16 = (bf16[80,1152]{1,0:T(8,128)(2,1)S(1)}, bf16[80,1152]{1,0:T(8,128)(2,1)S(1)}, u32[]{:S(2)}, u32[]{:S(2)}) collective-permute-start(bf16[80,1152]{1,0:T(8,128)(2,1)S(1)} %get-tuple-element.28), channel_id=1, source_target_pairs={{0,4},{1,5},{2,6},{3,7},{4,0},{5,1},{6,2},{7,3},{8,12},{9,13},{10,... | collective-permute-start | bytes 552968 | tf_op jit(solution)/shard_map/ppermute | solution.py:353
  10.7 2.9 %collective-permute-done.10.refs_0_ = bf16[80,1152]{1,0:T(8,128)(2,1)S(1)} collective-permute-done((bf16[80,1152]{1,0:T(8,128)(2,1)S(1)}, bf16[80,1152]{1,0:T(8,128)(2,1)S(1)}, u32[]{:S(2)}, u32[]{:S(2)}) %collective-permute-start.10) | collective-permute-done | bytes 184352 | tf_op jit(solution)/shard_map/ppermute | solution.py:353
  13.6 1.7 %collective-permute-start.12 = (bf16[80,1152]{1,0:T(8,128)(2,1)S(1)}, bf16[80,1152]{1,0:T(8,128)(2,1)S(1)}, u32[]{:S(2)}, u32[]{:S(2)}) collective-permute-start(bf16[80,1152]{1,0:T(8,128)(2,1)S(1)} %collective-permute-done.10.refs_0_), channel_id=1, source_target_pairs={{0,16},{1,17},{2,18},{3,19},{4,20},{5,21},{6,22},{7,23},{8,24},{9,... | collective-permute-start | bytes 552968 | tf_op jit(solution)/shard_map/ppermute | solution.py:353
  16.8 2.5 %collective-permute-start = (bf16[80,1152]{1,0:T(8,128)(2,1)S(1)}, bf16[80,1152]{1,0:T(8,128)(2,1)S(1)}, u32[]{:S(2)}, u32[]{:S(2)}) collective-permute-start(bf16[80,1152]{1,0:T(8,128)(2,1)S(1)} %get-tuple-element.21), channel_id=1, source_target_pairs={{0,6},{1,7},{2,4},{3,5},{4,2},{5,3},{6,0},{7,1},{8,14},{9,15},{10,... | collective-permute-start | bytes 552968 | tf_op jit(solution)/shard_map/ppermute | solution.py:353
  25.2 1.8 %collective-permute-start.14 = (bf16[32,1152]{1,0:T(8,128)(2,1)S(1)}, bf16[32,1152]{1,0:T(8,128)(2,1)S(1)}, u32[]{:S(2)}, u32[]{:S(2)}) collective-permute-start(bf16[32,1152]{1,0:T(8,128)(2,1)S(1)} %slice.101), channel_id=1, source_target_pairs={{0,16},{1,17},{2,18},{3,19},{4,20},{5,21},{6,22},{7,23},{8,24},{9,... | collective-permute-start | bytes 221192 | tf_op jit(solution)/shard_map/ppermute | solution.py:353
  27.0 3.2 %chip_weights.1.refs_3_.refs_2_.refs_5_ = bf16[1152,896]{1,0:T(8,128)(2,1)S(1)} custom-call(bf16[1152,3456]{1,0:T(8,128)(2,1)} %w_ref.1), custom_call_target="tpu_custom_call" | custom-call | flops 1000000000 | bytes 10000000 | tf_op jit(solution)/shard_map/chip_weights/pallas_call | solution.py:122
  41.6 3.9 %collective-permute-done.4.refs_1_ = bf16[32,1152]{1,0:T(8,128)(2,1)S(1)} collective-permute-done((bf16[32,1152]{1,0:T(8,128)(2,1)S(1)}, bf16[32,1152]{1,0:T(8,128)(2,1)S(1)}, u32[]{:S(2)}, u32[]{:S(2)}) %collective-permute-start.4) | collective-permute-done | bytes 73760 | tf_op jit(solution)/shard_map/ppermute | solution.py:353
  46.9 3.4 %collective-permute-done.3.refs_0_ = bf16[48,1152]{1,0:T(8,128)(2,1)S(1)} collective-permute-done((bf16[48,1152]{1,0:T(8,128)(2,1)S(1)}, bf16[48,1152]{1,0:T(8,128)(2,1)S(1)}, u32[]{:S(2)}, u32[]{:S(2)}) %collective-permute-start.3) | collective-permute-done | bytes 110624 | tf_op jit(solution)/shard_map/ppermute | solution.py:353
  52.3 2.9 %attend.5 = (bf16[2,192,128]{2,1,0:T(8,128)(2,1)S(1)}, bf16[2,4,2560,128]{3,2,1,0:T(8,128)(2,1)S(1)}) custom-call(bf16[4,240,128]{2,1,0:T(8,128)(2,1)S(1)} %get-tuple-element.22.refs_0_, bf16[4,80,128]{2,1,0:T(8,128)(2,1)S(1)} %get-tuple-element.23.refs_1_, bf16[2,4,320,128]{3,2,1,0:T(8,128)(2,1)S(1)} %get-tuple-element.25.refs_2_, ...), custom_call_target="tpu_custom_call" | custom-call | flops 838860800 | bytes 5242880 | tf_op jit(solution)/shard_map/attend/pallas_call | solution.py:270
  55.2 3.0 %attend.6 = bf16[2,192,128]{2,1,0:T(8,128)(2,1)S(1)} custom-call(bf16[4,240,128]{2,1,0:T(8,128)(2,1)S(1)} %get-tuple-element.22.refs_0_, bf16[4,80,128]{2,1,0:T(8,128)(2,1)S(1)} %get-tuple-element.23.refs_1_, bf16[2,4,2560,128]{3,2,1,0:T(8,128)(2,1)S(1)} %get-tuple-element.33.refs_2_.refs_1_), custom_call_target="tpu_custom_call" | custom-call | flops 838860800 | bytes 5242880 | tf_op jit(solution)/shard_map/attend/pallas_call | solution.py:270
  58.2 4.8 %attend.8 = bf16[4,192,128]{2,1,0:T(8,128)(2,1)S(1)} custom-call(bf16[4,320,128]{2,1,0:T(8,128)(2,1)S(1)} %get-tuple-element.35.refs_0_, bf16[2,4,2560,128]{3,2,1,0:T(8,128)(2,1)S(1)} %get-tuple-element.33.refs_2_.refs_1_), custom_call_target="tpu_custom_call" | custom-call | flops 1677721600 | bytes 5242880 | tf_op jit(solution)/shard_map/attend/pallas_call | solution.py:270
  63.1 4.8 %attend.7 = bf16[4,192,128]{2,1,0:T(8,128)(2,1)S(1)} custom-call(bf16[4,320,128]{2,1,0:T(8,128)(2,1)S(1)} %get-tuple-element.34.refs_0_, bf16[2,4,2560,128]{3,2,1,0:T(8,128)(2,1)S(1)} %get-tuple-element.33.refs_2_.refs_1_), custom_call_target="tpu_custom_call" | custom-call | flops 1677721600 | bytes 5242880 | tf_op jit(solution)/shard_map/attend/pallas_call | solution.py:270
  67.9 2.1 %collective-permute-start.24 = (bf16[2,192,128]{2,1,0:T(8,128)(2,1)S(1)}, bf16[2,192,128]{2,1,0:T(8,128)(2,1)S(1)}, u32[]{:S(2)}, u32[]{:S(2)}) collective-permute-start(bf16[2,192,128]{2,1,0:T(8,128)(2,1)S(1)} %get-tuple-element.32), channel_id=1, source_target_pairs={{0,6},{1,7},{2,4},{3,5},{4,2},{5,3},{6,0},{7,1},{8,14},{9,15},{10,... | collective-permute-start | bytes 294920 | tf_op jit(solution)/shard_map/ppermute | solution.py:353
  70.0 1.8 %collective-permute-start.26 = (bf16[2,192,128]{2,1,0:T(8,128)(2,1)S(1)}, bf16[2,192,128]{2,1,0:T(8,128)(2,1)S(1)}, u32[]{:S(2)}, u32[]{:S(2)}) collective-permute-start(bf16[2,192,128]{2,1,0:T(8,128)(2,1)S(1)} %attend.6), channel_id=1, source_target_pairs={{0,6},{1,7},{2,4},{3,5},{4,2},{5,3},{6,0},{7,1},{8,14},{9,15},{10,... | collective-permute-start | bytes 294920 | tf_op jit(solution)/shard_map/ppermute | solution.py:353
  71.9 5.1 %attend.9 = bf16[4,192,128]{2,1,0:T(8,128)(2,1)S(1)} custom-call(bf16[4,320,128]{2,1,0:T(8,128)(2,1)S(1)} %get-tuple-element.36.refs_0_, bf16[2,4,2560,128]{3,2,1,0:T(8,128)(2,1)S(1)} %get-tuple-element.33.refs_2_.refs_1_), custom_call_target="tpu_custom_call" | custom-call | flops 1677721600 | bytes 5242880 | tf_op jit(solution)/shard_map/attend/pallas_call | solution.py:270
  77.0 2.5 %collective-permute-start.33 = (bf16[4,192,128]{2,1,0:T(8,128)(2,1)S(1)}, bf16[4,192,128]{2,1,0:T(8,128)(2,1)S(1)}, u32[]{:S(2)}, u32[]{:S(2)}) collective-permute-start(bf16[4,192,128]{2,1,0:T(8,128)(2,1)S(1)} %attend.9), channel_id=1, source_target_pairs={{0,4},{1,5},{2,6},{3,7},{4,0},{5,1},{6,2},{7,3},{8,12},{9,13},{10,... | collective-permute-start | bytes 589832 | tf_op jit(solution)/shard_map/ppermute | solution.py:353
  79.5 1.6 %collective-permute-start.25 = (bf16[1,192,128]{2,1,0:T(8,128)(2,1)S(1)}, bf16[1,192,128]{2,1,0:T(8,128)(2,1)S(1)}, u32[]{:S(2)}, u32[]{:S(2)}) collective-permute-start(bf16[1,192,128]{2,1,0:T(8,128)(2,1)S(1)} %get-tuple-element.51), channel_id=1, source_target_pairs={{0,1},{1,0},{2,3},{3,2},{4,5},{5,4},{6,7},{7,6},{8,9},{9,8},{10,11... | collective-permute-start | bytes 147464 | tf_op jit(solution)/shard_map/ppermute | solution.py:353
  83.2 1.6 %collective-permute-start.30 = (bf16[2,192,128]{2,1,0:T(8,128)(2,1)S(1)}, bf16[2,192,128]{2,1,0:T(8,128)(2,1)S(1)}, u32[]{:S(2)}, u32[]{:S(2)}) collective-permute-start(bf16[2,192,128]{2,1,0:T(8,128)(2,1)S(1)} %pad_maximum_fusion.1), channel_id=1, source_target_pairs={{0,1},{1,0},{2,3},{3,2},{4,5},{5,4},{6,7},{7,6},{8,9},{9,8},{10,11... | collective-permute-start | bytes 294920 | tf_op jit(solution)/shard_map/ppermute | solution.py:353
  84.7 4.2 %collective-permute-done.33 = bf16[4,192,128]{2,1,0:T(8,128)(2,1)S(1)} collective-permute-done((bf16[4,192,128]{2,1,0:T(8,128)(2,1)S(1)}, bf16[4,192,128]{2,1,0:T(8,128)(2,1)S(1)}, u32[]{:S(2)}, u32[]{:S(2)}) %collective-permute-start.33) | collective-permute-done | bytes 196640 | tf_op jit(solution)/shard_map/ppermute | solution.py:353
  88.9 1.5 %collective-permute-start.36 = (bf16[1,192,128]{2,1,0:T(8,128)(2,1)S(1)}, bf16[1,192,128]{2,1,0:T(8,128)(2,1)S(1)}, u32[]{:S(2)}, u32[]{:S(2)}) collective-permute-start(bf16[1,192,128]{2,1,0:T(8,128)(2,1)S(1)} %get-tuple-element.37), channel_id=1, source_target_pairs={{0,17},{1,16},{2,19},{3,18},{4,21},{5,20},{6,23},{7,22},{8,25},{9,... | collective-permute-start | bytes 147464 | tf_op jit(solution)/shard_map/ppermute | solution.py:353
  95.7 2.7 %collective-permute-done.35.refs_10_ = bf16[1,192,128]{2,1,0:T(8,128)(2,1)S(1)} collective-permute-done((bf16[1,192,128]{2,1,0:T(8,128)(2,1)S(1)}, bf16[1,192,128]{2,1,0:T(8,128)(2,1)S(1)}, u32[]{:S(2)}, u32[]{:S(2)}) %collective-permute-start.35) | collective-permute-done | bytes 49184 | tf_op jit(solution)/shard_map/ppermute | solution.py:353
  98.6 6.2 %finish.1 = bf16[256,1152]{1,0:T(8,128)(2,1)} custom-call(bf16[256,1152]{1,0:T(8,128)(2,1)S(1)} %copy-done.1, s32[1,256]{1,0:T(1,128)S(1)} %bitcast.9, f32[6,4,1152]{2,1,0:T(4,128)S(1)} %bitcast.7, bf16[1152,1152]{1,0:T(8,128)(2,1)S(1)} %copy-done, bf16[1152,2304]{1,0:T(8,128)(2,1)S(1)} %bitcast.3, bf16[2304,1152]{1,0:T(8,128)(2,1)S(1)} %bitcast.5, ...), custom_call_target="tpu_custom_call" | custom-call | tf_op jit(solution)/shard_map/finish/pallas_call | solution.py:327
  (98 shorter events, 32.9 us)
Async XLA Ops:
  2.0 11.6 %collective-permute-start.10 = (bf16[80,1152]{1,0:T(8,128)(2,1)S(1)}, bf16[80,1152]{1,0:T(8,128)(2,1)S(1)}, u32[]{:S(2)}, u32[]{:S(2)}) collective-permute-start(bf16[80,1152]{1,0:T(8,128)(2,1)S(1)} %get-tuple-element.26), channel_id=1, source_target_pairs={{0,2},{1,3},{2,0},{3,1},{4,6},{5,7},{6,4},{7,5},{8,10},{9,11},{10,... | collective-permute-start | bytes 552968 | tf_op jit(solution)/shard_map/ppermute | solution.py:353
  5.1 11.7 %collective-permute-start.16 = (bf16[80,1152]{1,0:T(8,128)(2,1)S(1)}, bf16[80,1152]{1,0:T(8,128)(2,1)S(1)}, u32[]{:S(2)}, u32[]{:S(2)}) collective-permute-start(bf16[80,1152]{1,0:T(8,128)(2,1)S(1)} %get-tuple-element.28), channel_id=1, source_target_pairs={{0,4},{1,5},{2,6},{3,7},{4,0},{5,1},{6,2},{7,3},{8,12},{9,13},{10,... | collective-permute-start | bytes 552968 | tf_op jit(solution)/shard_map/ppermute | solution.py:353
  7.7 11.5 %collective-permute-start.6 = (bf16[80,1152]{1,0:T(8,128)(2,1)S(1)}, bf16[80,1152]{1,0:T(8,128)(2,1)S(1)}, u32[]{:S(2)}, u32[]{:S(2)}) collective-permute-start(bf16[80,1152]{1,0:T(8,128)(2,1)S(1)} %get-tuple-element.24.refs_0_), channel_id=1, source_target_pairs={{0,16},{1,17},{2,18},{3,19},{4,20},{5,21},{6,22},{7,23},{8,24},{9,... | collective-permute-start | bytes 552968 | tf_op jit(solution)/shard_map/ppermute | solution.py:353
  9.2 10.9 %collective-permute-start.5 = (bf16[80,1152]{1,0:T(8,128)(2,1)S(1)}, bf16[80,1152]{1,0:T(8,128)(2,1)S(1)}, u32[]{:S(2)}, u32[]{:S(2)}) collective-permute-start(bf16[80,1152]{1,0:T(8,128)(2,1)S(1)} %get-tuple-element.24.refs_0_), channel_id=1, source_target_pairs={{0,1},{1,0},{2,3},{3,2},{4,5},{5,4},{6,7},{7,6},{8,9},{9,8},{10,11... | collective-permute-start | bytes 552968 | tf_op jit(solution)/shard_map/ppermute | solution.py:353
  13.6 8.0 %collective-permute-start.12 = (bf16[80,1152]{1,0:T(8,128)(2,1)S(1)}, bf16[80,1152]{1,0:T(8,128)(2,1)S(1)}, u32[]{:S(2)}, u32[]{:S(2)}) collective-permute-start(bf16[80,1152]{1,0:T(8,128)(2,1)S(1)} %collective-permute-done.10.refs_0_), channel_id=1, source_target_pairs={{0,16},{1,17},{2,18},{3,19},{4,20},{5,21},{6,22},{7,23},{8,24},{9,... | collective-permute-start | bytes 552968 | tf_op jit(solution)/shard_map/ppermute | solution.py:353
  20.1 10.1 %collective-permute-start.17 = (bf16[80,1152]{1,0:T(8,128)(2,1)S(1)}, bf16[80,1152]{1,0:T(8,128)(2,1)S(1)}, u32[]{:S(2)}, u32[]{:S(2)}) collective-permute-start(bf16[80,1152]{1,0:T(8,128)(2,1)S(1)} %collective-permute-done.16.refs_0_), channel_id=1, source_target_pairs={{0,1},{1,0},{2,3},{3,2},{4,5},{5,4},{6,7},{7,6},{8,9},{9,8},{10,11... | collective-permute-start | bytes 552968 | tf_op jit(solution)/shard_map/ppermute | solution.py:353
  21.6 10.0 %collective-permute-start.7 = (bf16[48,1152]{1,0:T(8,128)(2,1)S(1)}, bf16[48,1152]{1,0:T(8,128)(2,1)S(1)}, u32[]{:S(2)}, u32[]{:S(2)}) collective-permute-start(bf16[48,1152]{1,0:T(8,128)(2,1)S(1)} %slice.98), channel_id=1, source_target_pairs={{0,1},{1,0},{2,3},{3,2},{4,5},{5,4},{6,7},{7,6},{8,9},{9,8},{10,11... | collective-permute-start | bytes 331784 | tf_op jit(solution)/shard_map/ppermute | solution.py:353
  22.2 8.3 %collective-permute-start.8 = (bf16[32,1152]{1,0:T(8,128)(2,1)S(1)}, bf16[32,1152]{1,0:T(8,128)(2,1)S(1)}, u32[]{:S(2)}, u32[]{:S(2)}) collective-permute-start(bf16[32,1152]{1,0:T(8,128)(2,1)S(1)} %slice.99), channel_id=1, source_target_pairs={{0,16},{1,17},{2,18},{3,19},{4,20},{5,21},{6,22},{7,23},{8,24},{9,... | collective-permute-start | bytes 221192 | tf_op jit(solution)/shard_map/ppermute | solution.py:353
  24.2 11.4 %collective-permute-start.13 = (bf16[48,1152]{1,0:T(8,128)(2,1)S(1)}, bf16[48,1152]{1,0:T(8,128)(2,1)S(1)}, u32[]{:S(2)}, u32[]{:S(2)}) collective-permute-start(bf16[48,1152]{1,0:T(8,128)(2,1)S(1)} %slice.100), channel_id=1, source_target_pairs={{0,1},{1,0},{2,3},{3,2},{4,5},{5,4},{6,7},{7,6},{8,9},{9,8},{10,11... | collective-permute-start | bytes 331784 | tf_op jit(solution)/shard_map/ppermute | solution.py:353
  25.2 8.9 %collective-permute-start.14 = (bf16[32,1152]{1,0:T(8,128)(2,1)S(1)}, bf16[32,1152]{1,0:T(8,128)(2,1)S(1)}, u32[]{:S(2)}, u32[]{:S(2)}) collective-permute-start(bf16[32,1152]{1,0:T(8,128)(2,1)S(1)} %slice.101), channel_id=1, source_target_pairs={{0,16},{1,17},{2,18},{3,19},{4,20},{5,21},{6,22},{7,23},{8,24},{9,... | collective-permute-start | bytes 221192 | tf_op jit(solution)/shard_map/ppermute | solution.py:353
  30.2 8.4 %collective-permute-start.2 = (bf16[80,1152]{1,0:T(8,128)(2,1)S(1)}, bf16[80,1152]{1,0:T(8,128)(2,1)S(1)}, u32[]{:S(2)}, u32[]{:S(2)}) collective-permute-start(bf16[80,1152]{1,0:T(8,128)(2,1)S(1)} %collective-permute-done.refs_0_), channel_id=1, source_target_pairs={{0,16},{1,17},{2,18},{3,19},{4,20},{5,21},{6,22},{7,23},{8,24},{9,... | collective-permute-start | bytes 552968 | tf_op jit(solution)/shard_map/ppermute | solution.py:353
  35.6 16.7 %collective-permute-start.9 = (bf16[2,4,320,128]{3,2,1,0:T(8,128)(2,1)S(1)}, bf16[2,4,320,128]{3,2,1,0:T(8,128)(2,1)S(1)}, u32[]{:S(2)}, u32[]{:S(2)}) collective-permute-start(bf16[2,4,320,128]{3,2,1,0:T(8,128)(2,1)S(1)} %get-tuple-element.25.refs_2_), channel_id=1, source_target_pairs={{0,8},{1,9},{2,10},{3,11},{4,12},{5,13},{6,14},{7,15},{8,0},{9,1},... | collective-permute-start | bytes 1966088 | tf_op jit(solution)/shard_map/ppermute | solution.py:353
  36.7 15.5 %collective-permute-start.15 = (bf16[2,4,320,128]{3,2,1,0:T(8,128)(2,1)S(1)}, bf16[2,4,320,128]{3,2,1,0:T(8,128)(2,1)S(1)}, u32[]{:S(2)}, u32[]{:S(2)}) collective-permute-start(bf16[2,4,320,128]{3,2,1,0:T(8,128)(2,1)S(1)} %get-tuple-element.27.refs_4_), channel_id=1, source_target_pairs={{0,8},{1,9},{2,10},{3,11},{4,12},{5,13},{6,14},{7,15},{8,0},{9,1},... | collective-permute-start | bytes 1966088 | tf_op jit(solution)/shard_map/ppermute | solution.py:353
  38.5 13.8 %collective-permute-start.21 = (bf16[2,4,320,128]{3,2,1,0:T(8,128)(2,1)S(1)}, bf16[2,4,320,128]{3,2,1,0:T(8,128)(2,1)S(1)}, u32[]{:S(2)}, u32[]{:S(2)}) collective-permute-start(bf16[2,4,320,128]{3,2,1,0:T(8,128)(2,1)S(1)} %get-tuple-element.29.refs_6_), channel_id=1, source_target_pairs={{0,8},{1,9},{2,10},{3,11},{4,12},{5,13},{6,14},{7,15},{8,0},{9,1},... | collective-permute-start | bytes 1966088 | tf_op jit(solution)/shard_map/ppermute | solution.py:353
  40.7 11.6 %collective-permute-start.22 = (bf16[2,4,240,128]{3,2,1,0:T(8,128)(2,1)S(1)}, bf16[2,4,240,128]{3,2,1,0:T(8,128)(2,1)S(1)}, u32[]{:S(2)}, u32[]{:S(2)}) collective-permute-start(bf16[2,4,240,128]{3,2,1,0:T(8,128)(2,1)S(1)} %get-tuple-element.30.refs_8_), channel_id=1, source_target_pairs={{0,8},{1,9},{2,10},{3,11},{4,12},{5,13},{6,14},{7,15},{8,0},{9,1},... | collective-permute-start | bytes 1474568 | tf_op jit(solution)/shard_map/ppermute | solution.py:353
  67.9 11.6 %collective-permute-start.24 = (bf16[2,192,128]{2,1,0:T(8,128)(2,1)S(1)}, bf16[2,192,128]{2,1,0:T(8,128)(2,1)S(1)}, u32[]{:S(2)}, u32[]{:S(2)}) collective-permute-start(bf16[2,192,128]{2,1,0:T(8,128)(2,1)S(1)} %get-tuple-element.32), channel_id=1, source_target_pairs={{0,6},{1,7},{2,4},{3,5},{4,2},{5,3},{6,0},{7,1},{8,14},{9,15},{10,... | collective-permute-start | bytes 294920 | tf_op jit(solution)/shard_map/ppermute | solution.py:353
  70.0 11.1 %collective-permute-start.26 = (bf16[2,192,128]{2,1,0:T(8,128)(2,1)S(1)}, bf16[2,192,128]{2,1,0:T(8,128)(2,1)S(1)}, u32[]{:S(2)}, u32[]{:S(2)}) collective-permute-start(bf16[2,192,128]{2,1,0:T(8,128)(2,1)S(1)} %attend.6), channel_id=1, source_target_pairs={{0,6},{1,7},{2,4},{3,5},{4,2},{5,3},{6,0},{7,1},{8,14},{9,15},{10,... | collective-permute-start | bytes 294920 | tf_op jit(solution)/shard_map/ppermute | solution.py:353
  71.8 11.3 %collective-permute-start.29 = (bf16[4,192,128]{2,1,0:T(8,128)(2,1)S(1)}, bf16[4,192,128]{2,1,0:T(8,128)(2,1)S(1)}, u32[]{:S(2)}, u32[]{:S(2)}) collective-permute-start(bf16[4,192,128]{2,1,0:T(8,128)(2,1)S(1)} %attend.8), channel_id=1, source_target_pairs={{0,2},{1,3},{2,0},{3,1},{4,6},{5,7},{6,4},{7,5},{8,10},{9,11},{10,... | collective-permute-start | bytes 589832 | tf_op jit(solution)/shard_map/ppermute | solution.py:353
  77.0 11.9 %collective-permute-start.33 = (bf16[4,192,128]{2,1,0:T(8,128)(2,1)S(1)}, bf16[4,192,128]{2,1,0:T(8,128)(2,1)S(1)}, u32[]{:S(2)}, u32[]{:S(2)}) collective-permute-start(bf16[4,192,128]{2,1,0:T(8,128)(2,1)S(1)} %attend.9), channel_id=1, source_target_pairs={{0,4},{1,5},{2,6},{3,7},{4,0},{5,1},{6,2},{7,3},{8,12},{9,13},{10,... | collective-permute-start | bytes 589832 | tf_op jit(solution)/shard_map/ppermute | solution.py:353
  79.5 11.0 %collective-permute-start.25 = (bf16[1,192,128]{2,1,0:T(8,128)(2,1)S(1)}, bf16[1,192,128]{2,1,0:T(8,128)(2,1)S(1)}, u32[]{:S(2)}, u32[]{:S(2)}) collective-permute-start(bf16[1,192,128]{2,1,0:T(8,128)(2,1)S(1)} %get-tuple-element.51), channel_id=1, source_target_pairs={{0,1},{1,0},{2,3},{3,2},{4,5},{5,4},{6,7},{7,6},{8,9},{9,8},{10,11... | collective-permute-start | bytes 147464 | tf_op jit(solution)/shard_map/ppermute | solution.py:353
  81.1 10.7 %collective-permute-start.28 = (bf16[1,192,128]{2,1,0:T(8,128)(2,1)S(1)}, bf16[1,192,128]{2,1,0:T(8,128)(2,1)S(1)}, u32[]{:S(2)}, u32[]{:S(2)}) collective-permute-start(bf16[1,192,128]{2,1,0:T(8,128)(2,1)S(1)} %get-tuple-element.49), channel_id=1, source_target_pairs={{0,17},{1,16},{2,19},{3,18},{4,21},{5,20},{6,23},{7,22},{8,25},{9,... | collective-permute-start | bytes 147464 | tf_op jit(solution)/shard_map/ppermute | solution.py:353
  82.5 10.4 %collective-permute-start.27 = (bf16[1,192,128]{2,1,0:T(8,128)(2,1)S(1)}, bf16[1,192,128]{2,1,0:T(8,128)(2,1)S(1)}, u32[]{:S(2)}, u32[]{:S(2)}) collective-permute-start(bf16[1,192,128]{2,1,0:T(8,128)(2,1)S(1)} %get-tuple-element.50), channel_id=1, source_target_pairs={{0,16},{1,17},{2,18},{3,19},{4,20},{5,21},{6,22},{7,23},{8,24},{9,... | collective-permute-start | bytes 147464 | tf_op jit(solution)/shard_map/ppermute | solution.py:353
  83.2 15.3 %collective-permute-start.30 = (bf16[2,192,128]{2,1,0:T(8,128)(2,1)S(1)}, bf16[2,192,128]{2,1,0:T(8,128)(2,1)S(1)}, u32[]{:S(2)}, u32[]{:S(2)}) collective-permute-start(bf16[2,192,128]{2,1,0:T(8,128)(2,1)S(1)} %pad_maximum_fusion.1), channel_id=1, source_target_pairs={{0,1},{1,0},{2,3},{3,2},{4,5},{5,4},{6,7},{7,6},{8,9},{9,8},{10,11... | collective-permute-start | bytes 294920 | tf_op jit(solution)/shard_map/ppermute | solution.py:353
  90.5 8.0 %collective-permute-start.31 = (bf16[2,192,128]{2,1,0:T(8,128)(2,1)S(1)}, bf16[2,192,128]{2,1,0:T(8,128)(2,1)S(1)}, u32[]{:S(2)}, u32[]{:S(2)}) collective-permute-start(bf16[2,192,128]{2,1,0:T(8,128)(2,1)S(1)} %pad_maximum_fusion.2), channel_id=1, source_target_pairs={{0,16},{1,17},{2,18},{3,19},{4,20},{5,21},{6,22},{7,23},{8,24},{9,... | collective-permute-start | bytes 294920 | tf_op jit(solution)/shard_map/ppermute | solution.py:353
  (21 other events, 331.4 us)

commit v5 on v4

--- a/solution.py
+++ b/solution.py
@@ -56,8 +56,27 @@
     return (bag_row * capacity + rank).astype(jnp.int32)
 
 
-def slot_kernel(capacity, tokens_ref, seq_ref, mod_ref, *out_refs):
-    me, _ = coordinates()
+def round_up(value, unit):
+    return -(-value // unit) * unit
+
+
+def window_base(start, total, wide):
+    aligned, last = start // LANE * LANE, total - wide
+    return min(aligned, last) if isinstance(start, int) else jnp.minimum(aligned, last)
+
+
+def slot_kernel(capacity, part, tokens_ref, seq_ref, mod_ref, w_ref, window_ref, *refs):
+    out_refs, sem = refs[:-1], refs[-1]
+    me, chip = coordinates()
+    total, wide = w_ref.shape[1], window_ref.shape[2]
+    copies = []
+    for kind in range(3):
+        base = pl.multiple_of(window_base(kind * (total // 3) + chip * part, total, wide), LANE)
+        copies.append(
+            pltpu.make_async_copy(w_ref.at[:, pl.ds(base, wide)], window_ref.at[kind], sem.at[kind])
+        )
+    for copy in copies:
+        copy.start()
     row_count, width = tokens_ref.shape
     block_count = len(out_refs)
     bag_row = ((seq_ref[...] // SEQ_BAG) ^ me).astype(F32)
@@ -68,67 +87,60 @@
     rows = jnp.dot(pick.astype(BF16), tokens_ref[...], preferred_element_type=F32)
     first = lax.broadcasted_iota(jnp.int32, (capacity, width), 1) == 0
     for block, out_ref in enumerate(out_refs):
-        part = slice(block * capacity, (block + 1) * capacity)
+        rows_of = slice(block * capacity, (block + 1) * capacity)
         shift, scale = [mod_ref[column, pl.ds(block ^ me, 1)] for column in (0, 1)]
-        normed = layer_norm(rows[part]) * (1.0 + scale) + shift
-        normed = jnp.where(first & (filled[part] < 0.5), HUGE, normed)
+        normed = layer_norm(rows[rows_of]) * (1.0 + scale) + shift
+        normed = jnp.where(first & (filled[rows_of] < 0.5), HUGE, normed)
         out_ref[...] = normed.astype(BF16)
-
-
-def slot_rows(tokens, seq_row, modulation, bag_count, capacity):
+    for copy in copies:
+        copy.wait()
+
+
+def slot_rows(tokens, seq_row, modulation, w_qkv, bag_count, capacity, part):
     width = tokens.shape[1]
-    return pl.pallas_call(
-        functools.partial(slot_kernel, capacity),
-        in_specs=[vmem(), vmem(), vmem()],
-        out_specs=[vmem()] * bag_count,
-        out_shape=[jax.ShapeDtypeStruct((capacity, width), BF16)] * bag_count,
+    wide = round_up(part + LANE - math.gcd(part, LANE), LANE)
+    made = pl.pallas_call(
+        functools.partial(slot_kernel, capacity, part),
+        in_specs=[vmem(), vmem(), vmem(), hbm()],
+        out_specs=[vmem()] * (1 + bag_count),
+        out_shape=[jax.ShapeDtypeStruct((3, w_qkv.shape[0], wide), BF16)]
+        + [jax.ShapeDtypeStruct((capacity, width), BF16)] * bag_count,
+        scratch_shapes=[pltpu.SemaphoreType.DMA((3,))],
         compiler_params=limit(16),
         name="slot_rows",
-    )(tokens, seq_row, modulation)
-
-
-def weight_kernel(part, w_ref, out_ref, window, sem):
-    total = w_ref.shape[1]
-    wide = window.shape[2]
-    copies, shifts = [], []
-    _, chip = coordinates()
-    for kind in range(3):
-        start = kind * (total // 3) + chip * part
-        base = pl.multiple_of(jnp.minimum(start // LANE * LANE, total - wide), LANE)
-        shifts.append(start - base)
-        copies.append(
-            pltpu.make_async_copy(w_ref.at[:, pl.ds(base, wide)], window.at[kind], sem.at[kind])
-        )
-    for copy in copies:
-        copy.start()
-    pieces = []
-    for kind, copy in enumerate(copies):
-        copy.wait()
-        rolled = pltpu.roll(window[kind].astype(F32), wide - shifts[kind], axis=1)
-        pieces.append(rolled[:, :part].astype(BF16))
-    filler = out_ref.shape[1] - 3 * part
-    if filler:
-        pieces.append(jnp.zeros((w_ref.shape[0], filler), BF16))
-    out_ref[...] = jnp.concatenate(pieces, axis=1)
-
-
-def round_up(value, unit):
-    return -(-value // unit) * unit
-
-
-def chip_weights(w_qkv, head_count):
-    depth, part = w_qkv.shape[0], head_count * HD
-    wide = round_up(part + LANE - math.gcd(part, LANE), LANE)
+    )(tokens, seq_row, modulation, w_qkv)
+    return made[0], made[1:]
+
+
+def weight_kernel(part, total, chips, window_ref, out_ref):
+    _, here = coordinates()
+    depth, wide = window_ref.shape[1:]
+    for chip in range(chips):
+
+        @pl.when(here == chip)
+        def _():
+            pieces = []
+            for kind in range(3):
+                start = kind * (total // 3) + chip * part
+                shift = start - window_base(start, total, wide)
+                pieces.append(window_ref[kind][:, shift : shift + part])
+            filler = out_ref.shape[1] - 3 * part
+            if filler:
+                pieces.append(jnp.zeros((depth, filler), BF16))
+            out_ref[...] = jnp.concatenate(pieces, axis=1)
+
+
+def chip_weights(windows, total, part):
+    depth = windows.shape[1]
     return pl.pallas_call(
-        functools.partial(weight_kernel, part),
-        in_specs=[hbm()],
+        functools.partial(weight_kernel, part, total, total // 3 // part),
+        in_specs=[vmem()],
         out_specs=vmem(),
         out_shape=jax.ShapeDtypeStruct((depth, round_up(3 * part, LANE)), BF16),
-        scratch_shapes=[pltpu.VMEM((3, depth, wide), BF16), pltpu.SemaphoreType.DMA((3,))],
         cost_estimate=pl.CostEstimate(flops=10**9, bytes_accessed=10**7, transcendentals=0),
-        compiler_params=limit(20),
+        compiler_params=limit(16),
         name="chip_weights",
-    )(w_qkv)
+    )(windows)
 
 
 def project_kernel(head_count, *refs):
@@ -358,8 +370,9 @@
     def in_place(value):
         return pltpu.with_memory_space_constraint(value, pltpu.HBM)
 
-    blocks = slot_rows(in_place(tokens), in_place(seq_row), in_place(modulation), bags, capacity)
-    weights = chip_weights(in_place(w_qkv), head_count)
+    inputs = [in_place(value) for value in (tokens, seq_row, modulation, w_qkv)]
+    windows, blocks = slot_rows(*inputs, bags, capacity, head_count * HD)
+    weights = chip_weights(windows, w_qkv.shape[1], head_count * HD)
     blocks = [block if k == 0 else swap(block, dz=k) for k, block in enumerate(blocks)]
     half = round_up(capacity, 32) // 2
     queries, pieces = [], []
@@ -379,7 +392,7 @@
             queries[k].append(query)
             pieces += [kv, swap(kv, core=1)]
     mixed = [None] * bags
-    rounds = [[bags - 1], [k for k in range(bags - 1) if k != 2], [2]] if bags > 3 else [list(range(bags))]
+    rounds = [[bags - 1, 0], list(range(1, bags - 1))] if bags > 2 else [list(range(bags))]
     shares = []
 
     def exchange(index):
@@ -388,7 +401,7 @@
             shares.append(swap(share, dx=j // along, dy=j % along) if j else share)
 
     for k in reversed(range(bags)):
-        halves = 2 if k == bags - 1 and chips % 2 == 0 else 1
+        halves = 1
         mixed[k] = []
         for index in range(halves):
             part, kv = attend(queries[k], pieces, chips, capacity, index, halves)
@@ -397,11 +410,11 @@
             mixed[k] += [part[j] for j in range(part.shape[0])]
     for index in range(len(rounds)):
         exchange(index)
-    return finish(
-        tokens, seq_row, modulation, shares, rounds, w_out, w_fc1, w_fc2, capacity, chips
-    )
+    return finish(tokens, seq_row, modulation, shares, rounds, w_out, w_fc1, w_fc2, capacity, chips)
 
 
 def solution(mesh):
     placed = (P(("bag", "sp"), None), P(("bag", "sp")), P(), P(), P(), P(), P())
-    return jax.shard_map(layer, mesh=mesh, in_specs=placed, out_specs=P(("bag", "sp"), None), check_vma=False)
+    return jax.shard_map(
+        layer, mesh=mesh, in_specs=placed, out_specs=P(("bag", "sp"), None), check_vma=False
+    )

time: 105 us -> 107 us (1.019)
  waiting for transfers between devices: 20.8 us -> 31.4 us
  starting transfers between devices: 46.5 us -> 39.1 us
  Pallas kernels: 37 us -> 35.1 us
    ppermute x37 -> x33, waiting for transfers between devices: 20.8 us -> 31.4 us  [swap(): return lax.ppermute(value, AXES, pairs)]
    ppermute x37 -> x33, starting transfers between devices: 46.5 us -> 39.1 us  [swap(): return lax.ppermute(value, AXES, pairs)]
    pallas_call x5 -> x4, Pallas kernels: 20.7 us -> 19.6 us  [attend(): pl.pallas_call(functools.partial(attend_kernel, chips, capacity, index *...]
  transfers between devices with their start and end apart: 37 -> 33, of which waited for: 11 -> 14; matrix products, arithmetic and copies ran while one was open for 0% -> 0% of each run, Pallas kernels for 13% -> 5%
where the time goes in v5:
time: 107 us
  starting transfers between devices  39.1 us (37%)
  Pallas kernels  35.1 us (33%)
  waiting for transfers between devices  31.4 us (29%)
    ppermute x33, starting transfers between devices, swap(): return lax.ppermute(value, AXES, pairs)  39.1 us
    ppermute x33, waiting for transfers between devices, swap(): return lax.ppermute(value, AXES, pairs)  31.4 us
    pallas_call x4, Pallas kernels, attend(): pl.pallas_call(functools.partial(attend_kernel, chips, capacity, index *...  19.6 us
    pallas_call x1, Pallas kernels, finish(): pl.pallas_call(functools.partial(finish_kernel, capacity, chips, rounds),...  6.22 us
    pallas_call x5, Pallas kernels, project(): pl.pallas_call(functools.partial(project_kernel, head_count), in_specs=[v...  4.95 us
    pallas_call x1, Pallas kernels, slot_rows(): pl.pallas_call(functools.partial(slot_kernel, capacity, part), in_specs=[...  3.67 us
  transfers between devices with their start and end apart: 33, of which 14 were waited for; matrix products, arithmetic and copies ran while one was open for 0% of the time, Pallas kernels for 5%

profile of v5, /device:TPU:0, one launch (start us, length us, event | category | flops | bytes accessed | tf_op | source)
XLA Modules:
  0.0 106.5 jit_solution(7172234653836019560)
XLA Ops:
  0.0 3.7 %slot_rows.1 = (bf16[3,1152,384]{2,1,0:T(8,128)(2,1)S(1)}, bf16[80,1152]{1,0:T(8,128)(2,1)S(1)}, bf16[80,1152]{1,0:T(8,128)(2,1)S(1)}, bf16[80,1152]{1,0:T(8,128)(2,1)S(1)}, bf16[80,1152]{1,0:T(8,128)(2,1)S(1)}) custom-call(bf16[256,1152]{1,0:T(8,128)(2,1)} %tokens_ref.3, s32[1,256]{1,0:T(1,128)} %bitcast.8, f32[6,4,1152]{2,1,0:T(4,128)} %bitcast.6, ...), custom_call_target="tpu_custom_call" | custom-call | tf_op jit(solution)/shard_map/slot_rows/pallas_call | solution.py:102
  3.7 3.1 %collective-permute-start.10 = (bf16[80,1152]{1,0:T(8,128)(2,1)S(1)}, bf16[80,1152]{1,0:T(8,128)(2,1)S(1)}, u32[]{:S(2)}, u32[]{:S(2)}) collective-permute-start(bf16[80,1152]{1,0:T(8,128)(2,1)S(1)} %get-tuple-element.28), channel_id=1, source_target_pairs={{0,2},{1,3},{2,0},{3,1},{4,6},{5,7},{6,4},{7,5},{8,10},{9,11},{10,... | collective-permute-start | bytes 552968 | tf_op jit(solution)/shard_map/ppermute | solution.py:365
  6.8 2.6 %collective-permute-start.16 = (bf16[80,1152]{1,0:T(8,128)(2,1)S(1)}, bf16[80,1152]{1,0:T(8,128)(2,1)S(1)}, u32[]{:S(2)}, u32[]{:S(2)}) collective-permute-start(bf16[80,1152]{1,0:T(8,128)(2,1)S(1)} %get-tuple-element.30), channel_id=1, source_target_pairs={{0,4},{1,5},{2,6},{3,7},{4,0},{5,1},{6,2},{7,3},{8,12},{9,13},{10,... | collective-permute-start | bytes 552968 | tf_op jit(solution)/shard_map/ppermute | solution.py:365
  12.4 2.9 %collective-permute-done.10.refs_0_ = bf16[80,1152]{1,0:T(8,128)(2,1)S(1)} collective-permute-done((bf16[80,1152]{1,0:T(8,128)(2,1)S(1)}, bf16[80,1152]{1,0:T(8,128)(2,1)S(1)}, u32[]{:S(2)}, u32[]{:S(2)}) %collective-permute-start.10) | collective-permute-done | bytes 184352 | tf_op jit(solution)/shard_map/ppermute | solution.py:365
  15.3 1.7 %collective-permute-start.12 = (bf16[80,1152]{1,0:T(8,128)(2,1)S(1)}, bf16[80,1152]{1,0:T(8,128)(2,1)S(1)}, u32[]{:S(2)}, u32[]{:S(2)}) collective-permute-start(bf16[80,1152]{1,0:T(8,128)(2,1)S(1)} %collective-permute-done.10.refs_0_), channel_id=1, source_target_pairs={{0,16},{1,17},{2,18},{3,19},{4,20},{5,21},{6,22},{7,23},{8,24},{9,... | collective-permute-start | bytes 552968 | tf_op jit(solution)/shard_map/ppermute | solution.py:365
  16.9 1.5 %collective-permute-start.11 = (bf16[80,1152]{1,0:T(8,128)(2,1)S(1)}, bf16[80,1152]{1,0:T(8,128)(2,1)S(1)}, u32[]{:S(2)}, u32[]{:S(2)}) collective-permute-start(bf16[80,1152]{1,0:T(8,128)(2,1)S(1)} %collective-permute-done.10.refs_0_), channel_id=1, source_target_pairs={{0,1},{1,0},{2,3},{3,2},{4,5},{5,4},{6,7},{7,6},{8,9},{9,8},{10,11... | collective-permute-start | bytes 552968 | tf_op jit(solution)/shard_map/ppermute | solution.py:365
  18.4 2.5 %collective-permute-start = (bf16[80,1152]{1,0:T(8,128)(2,1)S(1)}, bf16[80,1152]{1,0:T(8,128)(2,1)S(1)}, u32[]{:S(2)}, u32[]{:S(2)}) collective-permute-start(bf16[80,1152]{1,0:T(8,128)(2,1)S(1)} %get-tuple-element.22), channel_id=1, source_target_pairs={{0,6},{1,7},{2,4},{3,5},{4,2},{5,3},{6,0},{7,1},{8,14},{9,15},{10,... | collective-permute-start | bytes 552968 | tf_op jit(solution)/shard_map/ppermute | solution.py:365
  26.9 1.8 %collective-permute-start.14 = (bf16[32,1152]{1,0:T(8,128)(2,1)S(1)}, bf16[32,1152]{1,0:T(8,128)(2,1)S(1)}, u32[]{:S(2)}, u32[]{:S(2)}) collective-permute-start(bf16[32,1152]{1,0:T(8,128)(2,1)S(1)} %slice.101), channel_id=1, source_target_pairs={{0,16},{1,17},{2,18},{3,19},{4,20},{5,21},{6,22},{7,23},{8,24},{9,... | collective-permute-start | bytes 221192 | tf_op jit(solution)/shard_map/ppermute | solution.py:365
  31.1 1.7 %collective-permute-start.20 = (bf16[32,1152]{1,0:T(8,128)(2,1)S(1)}, bf16[32,1152]{1,0:T(8,128)(2,1)S(1)}, u32[]{:S(2)}, u32[]{:S(2)}) collective-permute-start(bf16[32,1152]{1,0:T(8,128)(2,1)S(1)} %slice.103), channel_id=1, source_target_pairs={{0,16},{1,17},{2,18},{3,19},{4,20},{5,21},{6,22},{7,23},{8,24},{9,... | collective-permute-start | bytes 221192 | tf_op jit(solution)/shard_map/ppermute | solution.py:365
  37.8 1.9 %collective-permute-done.1.refs_1_ = bf16[80,1152]{1,0:T(8,128)(2,1)S(1)} collective-permute-done((bf16[80,1152]{1,0:T(8,128)(2,1)S(1)}, bf16[80,1152]{1,0:T(8,128)(2,1)S(1)}, u32[]{:S(2)}, u32[]{:S(2)}) %collective-permute-start.1) | collective-permute-done | bytes 184352 | tf_op jit(solution)/shard_map/ppermute | solution.py:365
  41.1 4.3 %collective-permute-done.4.refs_1_ = bf16[32,1152]{1,0:T(8,128)(2,1)S(1)} collective-permute-done((bf16[32,1152]{1,0:T(8,128)(2,1)S(1)}, bf16[32,1152]{1,0:T(8,128)(2,1)S(1)}, u32[]{:S(2)}, u32[]{:S(2)}) %collective-permute-start.4) | collective-permute-done | bytes 73760 | tf_op jit(solution)/shard_map/ppermute | solution.py:365
  46.1 4.1 %collective-permute-done.3.refs_0_ = bf16[48,1152]{1,0:T(8,128)(2,1)S(1)} collective-permute-done((bf16[48,1152]{1,0:T(8,128)(2,1)S(1)}, bf16[48,1152]{1,0:T(8,128)(2,1)S(1)}, u32[]{:S(2)}, u32[]{:S(2)}) %collective-permute-start.3) | collective-permute-done | bytes 110624 | tf_op jit(solution)/shard_map/ppermute | solution.py:365
  52.2 4.9 %attend.4 = (bf16[4,192,128]{2,1,0:T(8,128)(2,1)S(1)}, bf16[2,4,2560,128]{3,2,1,0:T(8,128)(2,1)S(1)}) custom-call(bf16[4,240,128]{2,1,0:T(8,128)(2,1)S(1)} %get-tuple-element.24.refs_0_, bf16[4,80,128]{2,1,0:T(8,128)(2,1)S(1)} %get-tuple-element.25.refs_1_, bf16[2,4,320,128]{3,2,1,0:T(8,128)(2,1)S(1)} %get-tuple-element.27.refs_2_, ...), custom_call_target="tpu_custom_call" | custom-call | flops 1677721600 | bytes 5242880 | tf_op jit(solution)/shard_map/attend/pallas_call | solution.py:282
  57.1 5.1 %attend.7 = bf16[4,192,128]{2,1,0:T(8,128)(2,1)S(1)} custom-call(bf16[4,320,128]{2,1,0:T(8,128)(2,1)S(1)} %get-tuple-element.38.refs_0_, bf16[2,4,2560,128]{3,2,1,0:T(8,128)(2,1)S(1)} %get-tuple-element.36.refs_1_), custom_call_target="tpu_custom_call" | custom-call | flops 1677721600 | bytes 5242880 | tf_op jit(solution)/shard_map/attend/pallas_call | solution.py:282
  62.2 4.8 %attend.6 = bf16[4,192,128]{2,1,0:T(8,128)(2,1)S(1)} custom-call(bf16[4,320,128]{2,1,0:T(8,128)(2,1)S(1)} %get-tuple-element.37.refs_0_, bf16[2,4,2560,128]{3,2,1,0:T(8,128)(2,1)S(1)} %get-tuple-element.36.refs_1_), custom_call_target="tpu_custom_call" | custom-call | flops 1677721600 | bytes 5242880 | tf_op jit(solution)/shard_map/attend/pallas_call | solution.py:282
  67.0 4.8 %attend.5 = bf16[4,192,128]{2,1,0:T(8,128)(2,1)S(1)} custom-call(bf16[4,320,128]{2,1,0:T(8,128)(2,1)S(1)} %get-tuple-element.35.refs_0_, bf16[2,4,2560,128]{3,2,1,0:T(8,128)(2,1)S(1)} %get-tuple-element.36.refs_1_), custom_call_target="tpu_custom_call" | custom-call | flops 1677721600 | bytes 5242880 | tf_op jit(solution)/shard_map/attend/pallas_call | solution.py:282
  71.8 1.6 %collective-permute-start.24 = (bf16[4,192,128]{2,1,0:T(8,128)(2,1)S(1)}, bf16[4,192,128]{2,1,0:T(8,128)(2,1)S(1)}, u32[]{:S(2)}, u32[]{:S(2)}) collective-permute-start(bf16[4,192,128]{2,1,0:T(8,128)(2,1)S(1)} %get-tuple-element.34), channel_id=1, source_target_pairs={{0,6},{1,7},{2,4},{3,5},{4,2},{5,3},{6,0},{7,1},{8,14},{9,15},{10,... | collective-permute-start | bytes 589832 | tf_op jit(solution)/shard_map/ppermute | solution.py:365
  73.6 2.7 %collective-permute-start.29 = (bf16[4,192,128]{2,1,0:T(8,128)(2,1)S(1)}, bf16[4,192,128]{2,1,0:T(8,128)(2,1)S(1)}, u32[]{:S(2)}, u32[]{:S(2)}) collective-permute-start(bf16[4,192,128]{2,1,0:T(8,128)(2,1)S(1)} %attend.7), channel_id=1, source_target_pairs={{0,4},{1,5},{2,6},{3,7},{4,0},{5,1},{6,2},{7,3},{8,12},{9,13},{10,... | collective-permute-start | bytes 589832 | tf_op jit(solution)/shard_map/ppermute | solution.py:365
  76.3 5.2 %collective-permute-done.24 = bf16[4,192,128]{2,1,0:T(8,128)(2,1)S(1)} collective-permute-done((bf16[4,192,128]{2,1,0:T(8,128)(2,1)S(1)}, bf16[4,192,128]{2,1,0:T(8,128)(2,1)S(1)}, u32[]{:S(2)}, u32[]{:S(2)}) %collective-permute-start.24) | collective-permute-done | bytes 196640 | tf_op jit(solution)/shard_map/ppermute | solution.py:365
  82.3 1.6 %collective-permute-start.26 = (bf16[2,192,128]{2,1,0:T(8,128)(2,1)S(1)}, bf16[2,192,128]{2,1,0:T(8,128)(2,1)S(1)}, u32[]{:S(2)}, u32[]{:S(2)}) collective-permute-start(bf16[2,192,128]{2,1,0:T(8,128)(2,1)S(1)} %pad_maximum_fusion.2), channel_id=1, source_target_pairs={{0,16},{1,17},{2,18},{3,19},{4,20},{5,21},{6,22},{7,23},{8,24},{9,... | collective-permute-start | bytes 294920 | tf_op jit(solution)/shard_map/ppermute | solution.py:365
  85.4 6.7 %collective-permute-done.29 = bf16[4,192,128]{2,1,0:T(8,128)(2,1)S(1)} collective-permute-done((bf16[4,192,128]{2,1,0:T(8,128)(2,1)S(1)}, bf16[4,192,128]{2,1,0:T(8,128)(2,1)S(1)}, u32[]{:S(2)}, u32[]{:S(2)}) %collective-permute-start.29) | collective-permute-done | bytes 196640 | tf_op jit(solution)/shard_map/ppermute | solution.py:365
  96.2 1.7 %collective-permute-done.30.refs_5_ = bf16[2,192,128]{2,1,0:T(8,128)(2,1)S(1)} collective-permute-done((bf16[2,192,128]{2,1,0:T(8,128)(2,1)S(1)}, bf16[2,192,128]{2,1,0:T(8,128)(2,1)S(1)}, u32[]{:S(2)}, u32[]{:S(2)}) %collective-permute-start.30) | collective-permute-done | bytes 98336 | tf_op jit(solution)/shard_map/ppermute | solution.py:365
  98.7 1.6 %collective-permute-done.32.refs_7_ = bf16[2,192,128]{2,1,0:T(8,128)(2,1)S(1)} collective-permute-done((bf16[2,192,128]{2,1,0:T(8,128)(2,1)S(1)}, bf16[2,192,128]{2,1,0:T(8,128)(2,1)S(1)}, u32[]{:S(2)}, u32[]{:S(2)}) %collective-permute-start.32) | collective-permute-done | bytes 98336 | tf_op jit(solution)/shard_map/ppermute | solution.py:365
  100.3 6.2 %finish.1 = bf16[256,1152]{1,0:T(8,128)(2,1)} custom-call(bf16[256,1152]{1,0:T(8,128)(2,1)S(1)} %copy-done.1, s32[1,256]{1,0:T(1,128)S(1)} %bitcast.9, f32[6,4,1152]{2,1,0:T(4,128)S(1)} %bitcast.7, bf16[1152,1152]{1,0:T(8,128)(2,1)S(1)} %copy-done, bf16[1152,2304]{1,0:T(8,128)(2,1)S(1)} %bitcast.3, bf16[2304,1152]{1,0:T(8,128)(2,1)S(1)} %bitcast.5, ...), custom_call_target="tpu_custom_call" | custom-call | tf_op jit(solution)/shard_map/finish/pallas_call | solution.py:339
  (92 shorter events, 27.4 us)
Async XLA Ops:
  3.7 11.6 %collective-permute-start.10 = (bf16[80,1152]{1,0:T(8,128)(2,1)S(1)}, bf16[80,1152]{1,0:T(8,128)(2,1)S(1)}, u32[]{:S(2)}, u32[]{:S(2)}) collective-permute-start(bf16[80,1152]{1,0:T(8,128)(2,1)S(1)} %get-tuple-element.28), channel_id=1, source_target_pairs={{0,2},{1,3},{2,0},{3,1},{4,6},{5,7},{6,4},{7,5},{8,10},{9,11},{10,... | collective-permute-start | bytes 552968 | tf_op jit(solution)/shard_map/ppermute | solution.py:365
  6.8 11.7 %collective-permute-start.16 = (bf16[80,1152]{1,0:T(8,128)(2,1)S(1)}, bf16[80,1152]{1,0:T(8,128)(2,1)S(1)}, u32[]{:S(2)}, u32[]{:S(2)}) collective-permute-start(bf16[80,1152]{1,0:T(8,128)(2,1)S(1)} %get-tuple-element.30), channel_id=1, source_target_pairs={{0,4},{1,5},{2,6},{3,7},{4,0},{5,1},{6,2},{7,3},{8,12},{9,13},{10,... | collective-permute-start | bytes 552968 | tf_op jit(solution)/shard_map/ppermute | solution.py:365
  9.4 11.5 %collective-permute-start.6 = (bf16[80,1152]{1,0:T(8,128)(2,1)S(1)}, bf16[80,1152]{1,0:T(8,128)(2,1)S(1)}, u32[]{:S(2)}, u32[]{:S(2)}) collective-permute-start(bf16[80,1152]{1,0:T(8,128)(2,1)S(1)} %get-tuple-element.26.refs_0_), channel_id=1, source_target_pairs={{0,16},{1,17},{2,18},{3,19},{4,20},{5,21},{6,22},{7,23},{8,24},{9,... | collective-permute-start | bytes 552968 | tf_op jit(solution)/shard_map/ppermute | solution.py:365
  10.9 10.9 %collective-permute-start.5 = (bf16[80,1152]{1,0:T(8,128)(2,1)S(1)}, bf16[80,1152]{1,0:T(8,128)(2,1)S(1)}, u32[]{:S(2)}, u32[]{:S(2)}) collective-permute-start(bf16[80,1152]{1,0:T(8,128)(2,1)S(1)} %get-tuple-element.26.refs_0_), channel_id=1, source_target_pairs={{0,1},{1,0},{2,3},{3,2},{4,5},{5,4},{6,7},{7,6},{8,9},{9,8},{10,11... | collective-permute-start | bytes 552968 | tf_op jit(solution)/shard_map/ppermute | solution.py:365
  15.3 8.0 %collective-permute-start.12 = (bf16[80,1152]{1,0:T(8,128)(2,1)S(1)}, bf16[80,1152]{1,0:T(8,128)(2,1)S(1)}, u32[]{:S(2)}, u32[]{:S(2)}) collective-permute-start(bf16[80,1152]{1,0:T(8,128)(2,1)S(1)} %collective-permute-done.10.refs_0_), channel_id=1, source_target_pairs={{0,16},{1,17},{2,18},{3,19},{4,20},{5,21},{6,22},{7,23},{8,24},{9,... | collective-permute-start | bytes 552968 | tf_op jit(solution)/shard_map/ppermute | solution.py:365
  16.9 7.0 %collective-permute-start.11 = (bf16[80,1152]{1,0:T(8,128)(2,1)S(1)}, bf16[80,1152]{1,0:T(8,128)(2,1)S(1)}, u32[]{:S(2)}, u32[]{:S(2)}) collective-permute-start(bf16[80,1152]{1,0:T(8,128)(2,1)S(1)} %collective-permute-done.10.refs_0_), channel_id=1, source_target_pairs={{0,1},{1,0},{2,3},{3,2},{4,5},{5,4},{6,7},{7,6},{8,9},{9,8},{10,11... | collective-permute-start | bytes 552968 | tf_op jit(solution)/shard_map/ppermute | solution.py:365
  18.4 7.4 %collective-permute-start = (bf16[80,1152]{1,0:T(8,128)(2,1)S(1)}, bf16[80,1152]{1,0:T(8,128)(2,1)S(1)}, u32[]{:S(2)}, u32[]{:S(2)}) collective-permute-start(bf16[80,1152]{1,0:T(8,128)(2,1)S(1)} %get-tuple-element.22), channel_id=1, source_target_pairs={{0,6},{1,7},{2,4},{3,5},{4,2},{5,3},{6,0},{7,1},{8,14},{9,15},{10,... | collective-permute-start | bytes 552968 | tf_op jit(solution)/shard_map/ppermute | solution.py:365
  21.8 7.6 %collective-permute-start.17 = (bf16[80,1152]{1,0:T(8,128)(2,1)S(1)}, bf16[80,1152]{1,0:T(8,128)(2,1)S(1)}, u32[]{:S(2)}, u32[]{:S(2)}) collective-permute-start(bf16[80,1152]{1,0:T(8,128)(2,1)S(1)} %collective-permute-done.16.refs_0_), channel_id=1, source_target_pairs={{0,1},{1,0},{2,3},{3,2},{4,5},{5,4},{6,7},{7,6},{8,9},{9,8},{10,11... | collective-permute-start | bytes 552968 | tf_op jit(solution)/shard_map/ppermute | solution.py:365
  23.3 7.8 %collective-permute-start.7 = (bf16[48,1152]{1,0:T(8,128)(2,1)S(1)}, bf16[48,1152]{1,0:T(8,128)(2,1)S(1)}, u32[]{:S(2)}, u32[]{:S(2)}) collective-permute-start(bf16[48,1152]{1,0:T(8,128)(2,1)S(1)} %slice.98), channel_id=1, source_target_pairs={{0,1},{1,0},{2,3},{3,2},{4,5},{5,4},{6,7},{7,6},{8,9},{9,8},{10,11... | collective-permute-start | bytes 331784 | tf_op jit(solution)/shard_map/ppermute | solution.py:365
  23.9 6.4 %collective-permute-start.8 = (bf16[32,1152]{1,0:T(8,128)(2,1)S(1)}, bf16[32,1152]{1,0:T(8,128)(2,1)S(1)}, u32[]{:S(2)}, u32[]{:S(2)}) collective-permute-start(bf16[32,1152]{1,0:T(8,128)(2,1)S(1)} %slice.99), channel_id=1, source_target_pairs={{0,16},{1,17},{2,18},{3,19},{4,20},{5,21},{6,22},{7,23},{8,24},{9,... | collective-permute-start | bytes 221192 | tf_op jit(solution)/shard_map/ppermute | solution.py:365
  25.9 8.9 %collective-permute-start.13 = (bf16[48,1152]{1,0:T(8,128)(2,1)S(1)}, bf16[48,1152]{1,0:T(8,128)(2,1)S(1)}, u32[]{:S(2)}, u32[]{:S(2)}) collective-permute-start(bf16[48,1152]{1,0:T(8,128)(2,1)S(1)} %slice.100), channel_id=1, source_target_pairs={{0,1},{1,0},{2,3},{3,2},{4,5},{5,4},{6,7},{7,6},{8,9},{9,8},{10,11... | collective-permute-start | bytes 331784 | tf_op jit(solution)/shard_map/ppermute | solution.py:365
  26.9 7.2 %collective-permute-start.14 = (bf16[32,1152]{1,0:T(8,128)(2,1)S(1)}, bf16[32,1152]{1,0:T(8,128)(2,1)S(1)}, u32[]{:S(2)}, u32[]{:S(2)}) collective-permute-start(bf16[32,1152]{1,0:T(8,128)(2,1)S(1)} %slice.101), channel_id=1, source_target_pairs={{0,16},{1,17},{2,18},{3,19},{4,20},{5,21},{6,22},{7,23},{8,24},{9,... | collective-permute-start | bytes 221192 | tf_op jit(solution)/shard_map/ppermute | solution.py:365
  29.4 8.4 %collective-permute-start.2 = (bf16[80,1152]{1,0:T(8,128)(2,1)S(1)}, bf16[80,1152]{1,0:T(8,128)(2,1)S(1)}, u32[]{:S(2)}, u32[]{:S(2)}) collective-permute-start(bf16[80,1152]{1,0:T(8,128)(2,1)S(1)} %collective-permute-done.refs_0_), channel_id=1, source_target_pairs={{0,16},{1,17},{2,18},{3,19},{4,20},{5,21},{6,22},{7,23},{8,24},{9,... | collective-permute-start | bytes 552968 | tf_op jit(solution)/shard_map/ppermute | solution.py:365
  30.3 6.2 %collective-permute-start.19 = (bf16[48,1152]{1,0:T(8,128)(2,1)S(1)}, bf16[48,1152]{1,0:T(8,128)(2,1)S(1)}, u32[]{:S(2)}, u32[]{:S(2)}) collective-permute-start(bf16[48,1152]{1,0:T(8,128)(2,1)S(1)} %slice.102), channel_id=1, source_target_pairs={{0,1},{1,0},{2,3},{3,2},{4,5},{5,4},{6,7},{7,6},{8,9},{9,8},{10,11... | collective-permute-start | bytes 331784 | tf_op jit(solution)/shard_map/ppermute | solution.py:365
  34.8 17.4 %collective-permute-start.9 = (bf16[2,4,320,128]{3,2,1,0:T(8,128)(2,1)S(1)}, bf16[2,4,320,128]{3,2,1,0:T(8,128)(2,1)S(1)}, u32[]{:S(2)}, u32[]{:S(2)}) collective-permute-start(bf16[2,4,320,128]{3,2,1,0:T(8,128)(2,1)S(1)} %get-tuple-element.27.refs_2_), channel_id=1, source_target_pairs={{0,8},{1,9},{2,10},{3,11},{4,12},{5,13},{6,14},{7,15},{8,0},{9,1},... | collective-permute-start | bytes 1966088 | tf_op jit(solution)/shard_map/ppermute | solution.py:365
  35.9 16.2 %collective-permute-start.15 = (bf16[2,4,320,128]{3,2,1,0:T(8,128)(2,1)S(1)}, bf16[2,4,320,128]{3,2,1,0:T(8,128)(2,1)S(1)}, u32[]{:S(2)}, u32[]{:S(2)}) collective-permute-start(bf16[2,4,320,128]{3,2,1,0:T(8,128)(2,1)S(1)} %get-tuple-element.29.refs_4_), channel_id=1, source_target_pairs={{0,8},{1,9},{2,10},{3,11},{4,12},{5,13},{6,14},{7,15},{8,0},{9,1},... | collective-permute-start | bytes 1966088 | tf_op jit(solution)/shard_map/ppermute | solution.py:365
  37.7 14.5 %collective-permute-start.21 = (bf16[2,4,320,128]{3,2,1,0:T(8,128)(2,1)S(1)}, bf16[2,4,320,128]{3,2,1,0:T(8,128)(2,1)S(1)}, u32[]{:S(2)}, u32[]{:S(2)}) collective-permute-start(bf16[2,4,320,128]{3,2,1,0:T(8,128)(2,1)S(1)} %get-tuple-element.31.refs_6_), channel_id=1, source_target_pairs={{0,8},{1,9},{2,10},{3,11},{4,12},{5,13},{6,14},{7,15},{8,0},{9,1},... | collective-permute-start | bytes 1966088 | tf_op jit(solution)/shard_map/ppermute | solution.py:365
  40.6 11.6 %collective-permute-start.22 = (bf16[2,4,240,128]{3,2,1,0:T(8,128)(2,1)S(1)}, bf16[2,4,240,128]{3,2,1,0:T(8,128)(2,1)S(1)}, u32[]{:S(2)}, u32[]{:S(2)}) collective-permute-start(bf16[2,4,240,128]{3,2,1,0:T(8,128)(2,1)S(1)} %get-tuple-element.32.refs_8_), channel_id=1, source_target_pairs={{0,8},{1,9},{2,10},{3,11},{4,12},{5,13},{6,14},{7,15},{8,0},{9,1},... | collective-permute-start | bytes 1474568 | tf_op jit(solution)/shard_map/ppermute | solution.py:365
  71.8 9.7 %collective-permute-start.24 = (bf16[4,192,128]{2,1,0:T(8,128)(2,1)S(1)}, bf16[4,192,128]{2,1,0:T(8,128)(2,1)S(1)}, u32[]{:S(2)}, u32[]{:S(2)}) collective-permute-start(bf16[4,192,128]{2,1,0:T(8,128)(2,1)S(1)} %get-tuple-element.34), channel_id=1, source_target_pairs={{0,6},{1,7},{2,4},{3,5},{4,2},{5,3},{6,0},{7,1},{8,14},{9,15},{10,... | collective-permute-start | bytes 589832 | tf_op jit(solution)/shard_map/ppermute | solution.py:365
  73.5 11.9 %collective-permute-start.28 = (bf16[4,192,128]{2,1,0:T(8,128)(2,1)S(1)}, bf16[4,192,128]{2,1,0:T(8,128)(2,1)S(1)}, u32[]{:S(2)}, u32[]{:S(2)}) collective-permute-start(bf16[4,192,128]{2,1,0:T(8,128)(2,1)S(1)} %attend.6), channel_id=1, source_target_pairs={{0,2},{1,3},{2,0},{3,1},{4,6},{5,7},{6,4},{7,5},{8,10},{9,11},{10,... | collective-permute-start | bytes 589832 | tf_op jit(solution)/shard_map/ppermute | solution.py:365
  73.6 18.5 %collective-permute-start.29 = (bf16[4,192,128]{2,1,0:T(8,128)(2,1)S(1)}, bf16[4,192,128]{2,1,0:T(8,128)(2,1)S(1)}, u32[]{:S(2)}, u32[]{:S(2)}) collective-permute-start(bf16[4,192,128]{2,1,0:T(8,128)(2,1)S(1)} %attend.7), channel_id=1, source_target_pairs={{0,4},{1,5},{2,6},{3,7},{4,0},{5,1},{6,2},{7,3},{8,12},{9,13},{10,... | collective-permute-start | bytes 589832 | tf_op jit(solution)/shard_map/ppermute | solution.py:365
  81.5 13.1 %collective-permute-start.25 = (bf16[2,192,128]{2,1,0:T(8,128)(2,1)S(1)}, bf16[2,192,128]{2,1,0:T(8,128)(2,1)S(1)}, u32[]{:S(2)}, u32[]{:S(2)}) collective-permute-start(bf16[2,192,128]{2,1,0:T(8,128)(2,1)S(1)} %pad_maximum_fusion.1), channel_id=1, source_target_pairs={{0,1},{1,0},{2,3},{3,2},{4,5},{5,4},{6,7},{7,6},{8,9},{9,8},{10,11... | collective-permute-start | bytes 294920 | tf_op jit(solution)/shard_map/ppermute | solution.py:365
  82.3 13.8 %collective-permute-start.26 = (bf16[2,192,128]{2,1,0:T(8,128)(2,1)S(1)}, bf16[2,192,128]{2,1,0:T(8,128)(2,1)S(1)}, u32[]{:S(2)}, u32[]{:S(2)}) collective-permute-start(bf16[2,192,128]{2,1,0:T(8,128)(2,1)S(1)} %pad_maximum_fusion.2), channel_id=1, source_target_pairs={{0,16},{1,17},{2,18},{3,19},{4,20},{5,21},{6,22},{7,23},{8,24},{9,... | collective-permute-start | bytes 294920 | tf_op jit(solution)/shard_map/ppermute | solution.py:365
  84.0 12.2 %collective-permute-start.27 = (bf16[2,192,128]{2,1,0:T(8,128)(2,1)S(1)}, bf16[2,192,128]{2,1,0:T(8,128)(2,1)S(1)}, u32[]{:S(2)}, u32[]{:S(2)}) collective-permute-start(bf16[2,192,128]{2,1,0:T(8,128)(2,1)S(1)} %pad_maximum_fusion.3), channel_id=1, source_target_pairs={{0,17},{1,16},{2,19},{3,18},{4,21},{5,20},{6,23},{7,22},{8,25},{9,... | collective-permute-start | bytes 294920 | tf_op jit(solution)/shard_map/ppermute | solution.py:365
  (17 other events, 319.0 us)

commit v6 on v4

--- a/solution.py
+++ b/solution.py
@@ -54,6 +54,15 @@
     same = jnp.broadcast_to(to_column(bag_row), (n, n)) == jnp.broadcast_to(bag_row, (n, n))
     rank = jnp.sum(jnp.where(same & earlier, 1.0, 0.0), axis=0, keepdims=True)
     return (bag_row * capacity + rank).astype(jnp.int32)
+
+
+def round_up(value, unit):
+    return -(-value // unit) * unit
+
+
+def window_base(start, total, wide):
+    aligned, last = start // LANE * LANE, total - wide
+    return min(aligned, last) if isinstance(start, int) else jnp.minimum(aligned, last)
 
 
 def slot_kernel(capacity, tokens_ref, seq_ref, mod_ref, *out_refs):
@@ -68,10 +77,10 @@
     rows = jnp.dot(pick.astype(BF16), tokens_ref[...], preferred_element_type=F32)
     first = lax.broadcasted_iota(jnp.int32, (capacity, width), 1) == 0
     for block, out_ref in enumerate(out_refs):
-        part = slice(block * capacity, (block + 1) * capacity)
+        rows_of = slice(block * capacity, (block + 1) * capacity)
         shift, scale = [mod_ref[column, pl.ds(block ^ me, 1)] for column in (0, 1)]
-        normed = layer_norm(rows[part]) * (1.0 + scale) + shift
-        normed = jnp.where(first & (filled[part] < 0.5), HUGE, normed)
+        normed = layer_norm(rows[rows_of]) * (1.0 + scale) + shift
+        normed = jnp.where(first & (filled[rows_of] < 0.5), HUGE, normed)
         out_ref[...] = normed.astype(BF16)
 
 
@@ -87,46 +96,46 @@
     )(tokens, seq_row, modulation)
 
 
-def weight_kernel(part, w_ref, out_ref, window, sem):
+def weight_kernel(part, chips, w_ref, out_ref, window_ref, sem):
+    _, here = coordinates()
+    depth, wide = window_ref.shape[1:]
     total = w_ref.shape[1]
-    wide = window.shape[2]
-    copies, shifts = [], []
-    _, chip = coordinates()
+    copies = []
     for kind in range(3):
-        start = kind * (total // 3) + chip * part
-        base = pl.multiple_of(jnp.minimum(start // LANE * LANE, total - wide), LANE)
-        shifts.append(start - base)
+        base = pl.multiple_of(window_base(kind * (total // 3) + here * part, total, wide), LANE)
         copies.append(
-            pltpu.make_async_copy(w_ref.at[:, pl.ds(base, wide)], window.at[kind], sem.at[kind])
+            pltpu.make_async_copy(w_ref.at[:, pl.ds(base, wide)], window_ref.at[kind], sem.at[kind])
         )
     for copy in copies:
         copy.start()
-    pieces = []
-    for kind, copy in enumerate(copies):
+    for copy in copies:
         copy.wait()
-        rolled = pltpu.roll(window[kind].astype(F32), wide - shifts[kind], axis=1)
-        pieces.append(rolled[:, :part].astype(BF16))
-    filler = out_ref.shape[1] - 3 * part
-    if filler:
-        pieces.append(jnp.zeros((w_ref.shape[0], filler), BF16))
-    out_ref[...] = jnp.concatenate(pieces, axis=1)
-
-
-def round_up(value, unit):
-    return -(-value // unit) * unit
-
-
-def chip_weights(w_qkv, head_count):
-    depth, part = w_qkv.shape[0], head_count * HD
+    for chip in range(chips):
+
+        @pl.when(here == chip)
+        def _():
+            pieces = []
+            for kind in range(3):
+                start = kind * (total // 3) + chip * part
+                shift = start - window_base(start, total, wide)
+                pieces.append(window_ref[kind][:, shift : shift + part])
+            filler = out_ref.shape[1] - 3 * part
+            if filler:
+                pieces.append(jnp.zeros((depth, filler), BF16))
+            out_ref[...] = jnp.concatenate(pieces, axis=1)
+
+
+def chip_weights(w_qkv, part):
+    depth, total = w_qkv.shape
     wide = round_up(part + LANE - math.gcd(part, LANE), LANE)
     return pl.pallas_call(
-        functools.partial(weight_kernel, part),
+        functools.partial(weight_kernel, part, total // 3 // part),
         in_specs=[hbm()],
         out_specs=vmem(),
         out_shape=jax.ShapeDtypeStruct((depth, round_up(3 * part, LANE)), BF16),
         scratch_shapes=[pltpu.VMEM((3, depth, wide), BF16), pltpu.SemaphoreType.DMA((3,))],
         cost_estimate=pl.CostEstimate(flops=10**9, bytes_accessed=10**7, transcendentals=0),
-        compiler_params=limit(20),
+        compiler_params=limit(16),
         name="chip_weights",
     )(w_qkv)
 
@@ -283,56 +292,67 @@
     return made[0], (made[1] if len(pieces) > 1 else pieces[0])
 
 
-def finish_kernel(capacity, chips, rounds, tokens_ref, seq_ref, mod_ref, w_out, w_fc1, w_fc2, *refs):
-    parts, out_ref, whole = refs[:-2], refs[-2], refs[-1]
+def finish_kernel(capacity, chips, rounds, index, tokens_ref, seq_ref, mod_ref, w_out, w_fc1, w_fc2, *refs):
+    parts, earlier, out_ref, whole = refs[:chips], refs[chips:-2], refs[-2], refs[-1]
+    members = rounds[index]
     row_count, width = tokens_ref.shape
     plane, here = coordinates()
-    for index, part in enumerate(parts):
-        for at, bag in enumerate(rounds[index // chips]):
-            whole[here ^ (index % chips), bag] = part[at]
-    bags = whole.shape[1]
-    seq_row = seq_ref[...]
-    position = slot_of_row(((seq_row // SEQ_BAG) ^ plane).astype(F32), capacity)
-    slot_ids = lax.broadcasted_iota(jnp.int32, (bags * capacity, row_count), 0)
-    pick = jnp.where(slot_ids == position, 1.0, 0.0).astype(BF16)
-    seq_column = to_column(seq_row.astype(F32))
-    slots = jnp.concatenate(
+    for chip, part in enumerate(parts):
+        whole[here ^ chip] = part[...]
+    position = slot_of_row(((seq_ref[...] // SEQ_BAG) ^ plane).astype(F32), capacity)
+
+    def picks(bags):
+        slot_ids = lax.broadcasted_iota(jnp.int32, (capacity, row_count), 0)
+        blocks = [jnp.where(slot_ids + bag * capacity == position, 1.0, 0.0) for bag in bags]
+        return jnp.concatenate(blocks, axis=0).astype(BF16)
+
+    def per_slot(column):
+        rows = [mod_ref[column, pl.ds(bag ^ plane, 1)] for bag in members]
+        return jnp.concatenate([jnp.broadcast_to(row, (capacity, width)) for row in rows], axis=0)
+
+    attended = jnp.concatenate(
         [
             jnp.concatenate(
-                [unpack(whole[chip, bag], capacity, width // chips) for chip in range(chips)], axis=1
+                [unpack(whole[chip, at], capacity, width // chips) for chip in range(chips)], axis=1
             )
-            for bag in range(bags)
+            for at in range(len(members))
         ],
         axis=0,
     )
-    tn = (((0,), (0,)), ((), ()))
-    attended = lax.dot_general(pick, slots, tn, preferred_element_type=F32).astype(BF16)
-
-    def per_row(column):
-        value = jnp.broadcast_to(mod_ref[column, 0:1], (row_count, width))
-        for seq in range(1, mod_ref.shape[1]):
-            value = jnp.where(seq_column == seq, mod_ref[column, seq : seq + 1], value)
-        return value
-
+    residual = jnp.dot(picks(members), tokens_ref[...], preferred_element_type=F32)
     branch = jnp.dot(attended, w_out[...], preferred_element_type=F32)
-    hidden = (tokens_ref[...].astype(F32) + per_row(2) * branch).astype(BF16)
-    normed = (layer_norm(hidden.astype(F32)) * (1.0 + per_row(4)) + per_row(3)).astype(BF16)
+    hidden = (residual + per_slot(2) * branch).astype(BF16)
+    normed = (layer_norm(hidden.astype(F32)) * (1.0 + per_slot(4)) + per_slot(3)).astype(BF16)
     active = jax.nn.gelu(jnp.dot(normed, w_fc1[...], preferred_element_type=F32), approximate=True)
     last = jnp.dot(active.astype(BF16), w_fc2[...], preferred_element_type=F32)
-    out_ref[...] = (hidden.astype(F32) + per_row(5) * last).astype(BF16)
-
-
-def finish(tokens, seq_row, modulation, parts, rounds, w_out, w_fc1, w_fc2, capacity, chips):
-    bags = sum(len(members) for members in rounds)
+    slots = (hidden.astype(F32) + per_slot(5) * last).astype(BF16)
+    if index < len(rounds) - 1:
+        out_ref[...] = slots
+        return
+    slots = jnp.concatenate([ref[...] for ref in earlier] + [slots], axis=0)
+    tn = (((0,), (0,)), ((), ()))
+    pick = picks([bag for bags in rounds for bag in bags])
+    out_ref[...] = lax.dot_general(pick, slots, tn, preferred_element_type=F32).astype(BF16)
+
+
+def finish(tokens, seq_row, modulation, parts, earlier, rounds, index, w_out, w_fc1, w_fc2, capacity):
+    chips, slot_count = len(parts), capacity * len(rounds[index])
+    final = index == len(rounds) - 1
+    width, depth = tokens.shape[1], w_fc1.shape[1]
     return pl.pallas_call(
-        functools.partial(finish_kernel, capacity, chips, rounds),
-        in_specs=[vmem()] * (6 + len(parts)),
+        functools.partial(finish_kernel, capacity, chips, rounds, index),
+        in_specs=[vmem()] * (6 + chips + len(earlier)),
         out_specs=vmem(),
-        out_shape=jax.ShapeDtypeStruct(tokens.shape, BF16),
-        scratch_shapes=[pltpu.VMEM((chips, bags) + parts[0].shape[1:], BF16)],
+        out_shape=jax.ShapeDtypeStruct(tokens.shape if final else (slot_count, width), BF16),
+        scratch_shapes=[pltpu.VMEM((chips,) + parts[0].shape, BF16)],
+        cost_estimate=pl.CostEstimate(
+            flops=2 * slot_count * width * (width + 2 * depth),
+            bytes_accessed=2 * width * (width + 2 * depth),
+            transcendentals=slot_count * depth,
+        ),
         compiler_params=limit(20),
         name="finish",
-    )(tokens, seq_row, modulation, w_out, w_fc1, w_fc2, *parts)
+    )(tokens, seq_row, modulation, w_out, w_fc1, w_fc2, *parts, *earlier)
 
 
 def layer(tokens, row_seq, modulation, w_qkv, w_out, w_fc1, w_fc2):
@@ -359,7 +379,7 @@
         return pltpu.with_memory_space_constraint(value, pltpu.HBM)
 
     blocks = slot_rows(in_place(tokens), in_place(seq_row), in_place(modulation), bags, capacity)
-    weights = chip_weights(in_place(w_qkv), head_count)
+    weights = chip_weights(in_place(w_qkv), head_count * HD)
     blocks = [block if k == 0 else swap(block, dz=k) for k, block in enumerate(blocks)]
     half = round_up(capacity, 32) // 2
     queries, pieces = [], []
@@ -379,29 +399,36 @@
             queries[k].append(query)
             pieces += [kv, swap(kv, core=1)]
     mixed = [None] * bags
-    rounds = [[bags - 1], [k for k in range(bags - 1) if k != 2], [2]] if bags > 3 else [list(range(bags))]
-    shares = []
+    rounds = [[bags - 1, 0], list(range(1, bags - 1))] if bags > 2 else [list(range(bags))]
 
     def exchange(index):
+        shares = []
         for j in range(chips):
             share = jnp.stack([mixed[k][j] for k in rounds[index]])
             shares.append(swap(share, dx=j // along, dy=j % along) if j else share)
+        return shares
 
     for k in reversed(range(bags)):
-        halves = 2 if k == bags - 1 and chips % 2 == 0 else 1
+        halves = 1
         mixed[k] = []
         for index in range(halves):
             part, kv = attend(queries[k], pieces, chips, capacity, index, halves)
             pieces = [kv]
             part = swap(part, dz=k) if k else part
             mixed[k] += [part[j] for j in range(part.shape[0])]
+    shares = [exchange(index) for index in range(len(rounds))]
+    done = []
     for index in range(len(rounds)):
-        exchange(index)
-    return finish(
-        tokens, seq_row, modulation, shares, rounds, w_out, w_fc1, w_fc2, capacity, chips
-    )
+        done.append(
+            finish(
+                tokens, seq_row, modulation, shares[index], done, rounds, index, w_out, w_fc1, w_fc2, capacity
+            )
+        )
+    return done[-1]
 
 
 def solution(mesh):
     placed = (P(("bag", "sp"), None), P(("bag", "sp")), P(), P(), P(), P(), P())
-    return jax.shard_map(layer, mesh=mesh, in_specs=placed, out_specs=P(("bag", "sp"), None), check_vma=False)
+    return jax.shard_map(
+        layer, mesh=mesh, in_specs=placed, out_specs=P(("bag", "sp"), None), check_vma=False
+    )

time: 105 us -> 106 us (level)
  waiting for transfers between devices: 20.8 us -> 27 us
  starting transfers between devices: 46.5 us -> 40.6 us
    ppermute x37 -> x33, waiting for transfers between devices: 20.8 us -> 27 us  [swap(): return lax.ppermute(value, AXES, pairs)]
    ppermute x37 -> x33, starting transfers between devices: 46.5 us -> 40.6 us  [swap(): return lax.ppermute(value, AXES, pairs)]
    pallas_call x2 -> x3, Pallas kernels: 9.4 us -> 10.4 us  [the longest x2 7.92 us: finish(): pl.pallas_call(functools.partial(finish_kernel, capacity, chips, rounds,...]
    pallas_call x5 -> x4, Pallas kernels: 20.7 us -> 20.3 us  [attend(): pl.pallas_call(functools.partial(attend_kernel, chips, capacity, index *...]
  transfers between devices with their start and end apart: 37 -> 33, of which waited for: 11 -> 10; matrix products, arithmetic and copies ran while one was open for 0% -> 0% of each run, Pallas kernels for 13% -> 10%
where the time goes in v6:
time: 106 us
  starting transfers between devices  40.6 us (38%)
  Pallas kernels  37.6 us (35%)
  waiting for transfers between devices  27 us (25%)
    ppermute x33, starting transfers between devices, swap(): return lax.ppermute(value, AXES, pairs)  40.6 us
    ppermute x33, waiting for transfers between devices, swap(): return lax.ppermute(value, AXES, pairs)  27 us
    pallas_call x4, Pallas kernels, attend(): pl.pallas_call(functools.partial(attend_kernel, chips, capacity, index *...  20.3 us
    pallas_call x2, Pallas kernels, finish(): pl.pallas_call(functools.partial(finish_kernel, capacity, chips, rounds,...  7.92 us
    pallas_call x5, Pallas kernels, project(): pl.pallas_call(functools.partial(project_kernel, head_count), in_specs=[v...  4.96 us
    pallas_call x1, Pallas kernels, chip_weights(): pl.pallas_call(functools.partial(weight_kernel, part, total // 3 // part)...  2.46 us
  transfers between devices with their start and end apart: 33, of which 10 were waited for; matrix products, arithmetic and copies ran while one was open for 0% of the time, Pallas kernels for 10%

profile of v6, /device:TPU:0, one launch (start us, length us, event | category | flops | bytes accessed | tf_op | source)
XLA Modules:
  0.0 106.1 jit_solution(4648768131995542285)
XLA Ops:
  0.0 2.0 %slot_rows.1 = (bf16[80,1152]{1,0:T(8,128)(2,1)S(1)}, bf16[80,1152]{1,0:T(8,128)(2,1)S(1)}, bf16[80,1152]{1,0:T(8,128)(2,1)S(1)}, bf16[80,1152]{1,0:T(8,128)(2,1)S(1)}) custom-call(bf16[256,1152]{1,0:T(8,128)(2,1)} %tokens_ref.5, s32[1,256]{1,0:T(1,128)} %bitcast.9, f32[6,4,1152]{2,1,0:T(4,128)} %bitcast.6), custom_call_target="tpu_custom_call" | custom-call | tf_op jit(solution)/shard_map/slot_rows/pallas_call | solution.py:89
  2.0 3.1 %collective-permute-start = (bf16[80,1152]{1,0:T(8,128)(2,1)S(1)}, bf16[80,1152]{1,0:T(8,128)(2,1)S(1)}, u32[]{:S(2)}, u32[]{:S(2)}) collective-permute-start(bf16[80,1152]{1,0:T(8,128)(2,1)S(1)} %get-tuple-element.21), channel_id=1, source_target_pairs={{0,2},{1,3},{2,0},{3,1},{4,6},{5,7},{6,4},{7,5},{8,10},{9,11},{10,... | collective-permute-start | bytes 552968 | tf_op jit(solution)/shard_map/ppermute | solution.py:373
  5.1 2.6 %collective-permute-start.16 = (bf16[80,1152]{1,0:T(8,128)(2,1)S(1)}, bf16[80,1152]{1,0:T(8,128)(2,1)S(1)}, u32[]{:S(2)}, u32[]{:S(2)}) collective-permute-start(bf16[80,1152]{1,0:T(8,128)(2,1)S(1)} %get-tuple-element.29), channel_id=1, source_target_pairs={{0,4},{1,5},{2,6},{3,7},{4,0},{5,1},{6,2},{7,3},{8,12},{9,13},{10,... | collective-permute-start | bytes 552968 | tf_op jit(solution)/shard_map/ppermute | solution.py:373
  9.2 1.5 %collective-permute-start.10 = (bf16[80,1152]{1,0:T(8,128)(2,1)S(1)}, bf16[80,1152]{1,0:T(8,128)(2,1)S(1)}, u32[]{:S(2)}, u32[]{:S(2)}) collective-permute-start(bf16[80,1152]{1,0:T(8,128)(2,1)S(1)} %get-tuple-element.26.refs_0_), channel_id=1, source_target_pairs={{0,1},{1,0},{2,3},{3,2},{4,5},{5,4},{6,7},{7,6},{8,9},{9,8},{10,11... | collective-permute-start | bytes 552968 | tf_op jit(solution)/shard_map/ppermute | solution.py:373
  10.7 2.9 %collective-permute-done.refs_0_ = bf16[80,1152]{1,0:T(8,128)(2,1)S(1)} collective-permute-done((bf16[80,1152]{1,0:T(8,128)(2,1)S(1)}, bf16[80,1152]{1,0:T(8,128)(2,1)S(1)}, u32[]{:S(2)}, u32[]{:S(2)}) %collective-permute-start) | collective-permute-done | bytes 184352 | tf_op jit(solution)/shard_map/ppermute | solution.py:373
  13.6 1.7 %collective-permute-start.2 = (bf16[80,1152]{1,0:T(8,128)(2,1)S(1)}, bf16[80,1152]{1,0:T(8,128)(2,1)S(1)}, u32[]{:S(2)}, u32[]{:S(2)}) collective-permute-start(bf16[80,1152]{1,0:T(8,128)(2,1)S(1)} %collective-permute-done.refs_0_), channel_id=1, source_target_pairs={{0,16},{1,17},{2,18},{3,19},{4,20},{5,21},{6,22},{7,23},{8,24},{9,... | collective-permute-start | bytes 552968 | tf_op jit(solution)/shard_map/ppermute | solution.py:373
  15.3 1.5 %collective-permute-start.1 = (bf16[80,1152]{1,0:T(8,128)(2,1)S(1)}, bf16[80,1152]{1,0:T(8,128)(2,1)S(1)}, u32[]{:S(2)}, u32[]{:S(2)}) collective-permute-start(bf16[80,1152]{1,0:T(8,128)(2,1)S(1)} %collective-permute-done.refs_0_), channel_id=1, source_target_pairs={{0,1},{1,0},{2,3},{3,2},{4,5},{5,4},{6,7},{7,6},{8,9},{9,8},{10,11... | collective-permute-start | bytes 552968 | tf_op jit(solution)/shard_map/ppermute | solution.py:373
  16.8 2.5 %collective-permute-start.5 = (bf16[80,1152]{1,0:T(8,128)(2,1)S(1)}, bf16[80,1152]{1,0:T(8,128)(2,1)S(1)}, u32[]{:S(2)}, u32[]{:S(2)}) collective-permute-start(bf16[80,1152]{1,0:T(8,128)(2,1)S(1)} %get-tuple-element.23), channel_id=1, source_target_pairs={{0,6},{1,7},{2,4},{3,5},{4,2},{5,3},{6,0},{7,1},{8,14},{9,15},{10,... | collective-permute-start | bytes 552968 | tf_op jit(solution)/shard_map/ppermute | solution.py:373
  20.1 1.5 %collective-permute-start.17 = (bf16[80,1152]{1,0:T(8,128)(2,1)S(1)}, bf16[80,1152]{1,0:T(8,128)(2,1)S(1)}, u32[]{:S(2)}, u32[]{:S(2)}) collective-permute-start(bf16[80,1152]{1,0:T(8,128)(2,1)S(1)} %collective-permute-done.16.refs_0_), channel_id=1, source_target_pairs={{0,1},{1,0},{2,3},{3,2},{4,5},{5,4},{6,7},{7,6},{8,9},{9,8},{10,11... | collective-permute-start | bytes 552968 | tf_op jit(solution)/shard_map/ppermute | solution.py:373
  25.2 1.8 %collective-permute-start.4 = (bf16[32,1152]{1,0:T(8,128)(2,1)S(1)}, bf16[32,1152]{1,0:T(8,128)(2,1)S(1)}, u32[]{:S(2)}, u32[]{:S(2)}) collective-permute-start(bf16[32,1152]{1,0:T(8,128)(2,1)S(1)} %slice.97), channel_id=1, source_target_pairs={{0,16},{1,17},{2,18},{3,19},{4,20},{5,21},{6,22},{7,23},{8,24},{9,... | collective-permute-start | bytes 221192 | tf_op jit(solution)/shard_map/ppermute | solution.py:373
  27.0 2.5 %chip_weights.1.refs_5_.refs_3_.refs_2_ = bf16[1152,896]{1,0:T(8,128)(2,1)S(1)} custom-call(bf16[1152,3456]{1,0:T(8,128)(2,1)} %w_ref.1), custom_call_target="tpu_custom_call" | custom-call | flops 1000000000 | bytes 10000000 | tf_op jit(solution)/shard_map/chip_weights/pallas_call | solution.py:131
  41.1 3.7 %collective-permute-done.9.refs_1_ = bf16[32,1152]{1,0:T(8,128)(2,1)S(1)} collective-permute-done((bf16[32,1152]{1,0:T(8,128)(2,1)S(1)}, bf16[32,1152]{1,0:T(8,128)(2,1)S(1)}, u32[]{:S(2)}, u32[]{:S(2)}) %collective-permute-start.9) | collective-permute-done | bytes 73760 | tf_op jit(solution)/shard_map/ppermute | solution.py:373
  46.2 3.3 %collective-permute-done.8.refs_0_ = bf16[48,1152]{1,0:T(8,128)(2,1)S(1)} collective-permute-done((bf16[48,1152]{1,0:T(8,128)(2,1)S(1)}, bf16[48,1152]{1,0:T(8,128)(2,1)S(1)}, u32[]{:S(2)}, u32[]{:S(2)}) %collective-permute-start.8) | collective-permute-done | bytes 110624 | tf_op jit(solution)/shard_map/ppermute | solution.py:373
  51.6 5.1 %attend.4 = (bf16[4,192,128]{2,1,0:T(8,128)(2,1)S(1)}, bf16[2,4,2560,128]{3,2,1,0:T(8,128)(2,1)S(1)}) custom-call(bf16[4,240,128]{2,1,0:T(8,128)(2,1)S(1)} %get-tuple-element.24.refs_0_, bf16[4,80,128]{2,1,0:T(8,128)(2,1)S(1)} %get-tuple-element.25.refs_1_, bf16[2,4,320,128]{3,2,1,0:T(8,128)(2,1)S(1)} %get-tuple-element.27.refs_2_, ...), custom_call_target="tpu_custom_call" | custom-call | flops 1677721600 | bytes 5242880 | tf_op jit(solution)/shard_map/attend/pallas_call | solution.py:279
  56.7 5.2 %attend.7 = bf16[4,192,128]{2,1,0:T(8,128)(2,1)S(1)} custom-call(bf16[4,320,128]{2,1,0:T(8,128)(2,1)S(1)} %get-tuple-element.36.refs_0_, bf16[2,4,2560,128]{3,2,1,0:T(8,128)(2,1)S(1)} %get-tuple-element.33.refs_1_), custom_call_target="tpu_custom_call" | custom-call | flops 1677721600 | bytes 5242880 | tf_op jit(solution)/shard_map/attend/pallas_call | solution.py:279
  61.9 5.0 %attend.6 = bf16[4,192,128]{2,1,0:T(8,128)(2,1)S(1)} custom-call(bf16[4,320,128]{2,1,0:T(8,128)(2,1)S(1)} %get-tuple-element.34.refs_0_, bf16[2,4,2560,128]{3,2,1,0:T(8,128)(2,1)S(1)} %get-tuple-element.33.refs_1_), custom_call_target="tpu_custom_call" | custom-call | flops 1677721600 | bytes 5242880 | tf_op jit(solution)/shard_map/attend/pallas_call | solution.py:279
  66.9 5.0 %attend.5 = bf16[4,192,128]{2,1,0:T(8,128)(2,1)S(1)} custom-call(bf16[4,320,128]{2,1,0:T(8,128)(2,1)S(1)} %get-tuple-element.22.refs_0_, bf16[2,4,2560,128]{3,2,1,0:T(8,128)(2,1)S(1)} %get-tuple-element.33.refs_1_), custom_call_target="tpu_custom_call" | custom-call | flops 1677721600 | bytes 5242880 | tf_op jit(solution)/shard_map/attend/pallas_call | solution.py:279
  71.9 2.0 %collective-permute-start.29 = (bf16[4,192,128]{2,1,0:T(8,128)(2,1)S(1)}, bf16[4,192,128]{2,1,0:T(8,128)(2,1)S(1)}, u32[]{:S(2)}, u32[]{:S(2)}) collective-permute-start(bf16[4,192,128]{2,1,0:T(8,128)(2,1)S(1)} %get-tuple-element.35), channel_id=1, source_target_pairs={{0,6},{1,7},{2,4},{3,5},{4,2},{5,3},{6,0},{7,1},{8,14},{9,15},{10,... | collective-permute-start | bytes 589832 | tf_op jit(solution)/shard_map/ppermute | solution.py:373
  74.4 1.9 %collective-permute-start.25 = (bf16[4,192,128]{2,1,0:T(8,128)(2,1)S(1)}, bf16[4,192,128]{2,1,0:T(8,128)(2,1)S(1)}, u32[]{:S(2)}, u32[]{:S(2)}) collective-permute-start(bf16[4,192,128]{2,1,0:T(8,128)(2,1)S(1)} %attend.6), channel_id=1, source_target_pairs={{0,4},{1,5},{2,6},{3,7},{4,0},{5,1},{6,2},{7,3},{8,12},{9,13},{10,... | collective-permute-start | bytes 589832 | tf_op jit(solution)/shard_map/ppermute | solution.py:373
  76.4 5.2 %collective-permute-done.29 = bf16[4,192,128]{2,1,0:T(8,128)(2,1)S(1)} collective-permute-done((bf16[4,192,128]{2,1,0:T(8,128)(2,1)S(1)}, bf16[4,192,128]{2,1,0:T(8,128)(2,1)S(1)}, u32[]{:S(2)}, u32[]{:S(2)}) %collective-permute-start.29) | collective-permute-done | bytes 196640 | tf_op jit(solution)/shard_map/ppermute | solution.py:373
  83.5 1.8 %collective-permute-start.32 = (bf16[2,192,128]{2,1,0:T(8,128)(2,1)S(1)}, bf16[2,192,128]{2,1,0:T(8,128)(2,1)S(1)}, u32[]{:S(2)}, u32[]{:S(2)}) collective-permute-start(bf16[2,192,128]{2,1,0:T(8,128)(2,1)S(1)} %pad_maximum_fusion.7), channel_id=1, source_target_pairs={{0,17},{1,16},{2,19},{3,18},{4,21},{5,20},{6,23},{7,22},{8,25},{9,... | collective-permute-start | bytes 294920 | tf_op jit(solution)/shard_map/ppermute | solution.py:373
  85.4 7.6 %collective-permute-done.25 = bf16[4,192,128]{2,1,0:T(8,128)(2,1)S(1)} collective-permute-done((bf16[4,192,128]{2,1,0:T(8,128)(2,1)S(1)}, bf16[4,192,128]{2,1,0:T(8,128)(2,1)S(1)}, u32[]{:S(2)}, u32[]{:S(2)}) %collective-permute-start.25) | collective-permute-done | bytes 196640 | tf_op jit(solution)/shard_map/ppermute | solution.py:373
  97.1 3.4 %finish.2.refs_4_ = bf16[160,1152]{1,0:T(8,128)(2,1)S(1)} custom-call(bf16[256,1152]{1,0:T(8,128)(2,1)S(1)} %copy-done.1, s32[1,256]{1,0:T(1,128)S(1)} %bitcast.10, f32[6,4,1152]{2,1,0:T(4,128)S(1)} %bitcast.7, bf16[1152,1152]{1,0:T(8,128)(2,1)S(1)} %copy-done, bf16[1152,2304]{1,0:T(8,128)(2,1)S(1)} %bitcast.3, bf16[2304,1152]{1,0:T(8,128)(2,1)S(1)} %bitcast.5, ...), custom_call_target="tpu_custom_call" | custom-call | flops 2123366400 | bytes 13271040 | tf_op jit(solution)/shard_map/finish/pallas_call | solution.py:342
  101.5 4.5 %finish.3 = bf16[256,1152]{1,0:T(8,128)(2,1)} custom-call(bf16[256,1152]{1,0:T(8,128)(2,1)S(1)} %copy-done.1, s32[1,256]{1,0:T(1,128)S(1)} %bitcast.11, f32[6,4,1152]{2,1,0:T(4,128)S(1)} %bitcast.8, bf16[1152,1152]{1,0:T(8,128)(2,1)S(1)} %copy-done, bf16[1152,2304]{1,0:T(8,128)(2,1)S(1)} %bitcast.3, bf16[2304,1152]{1,0:T(8,128)(2,1)S(1)} %bitcast.5, ...), custom_call_target="tpu_custom_call" | custom-call | flops 2123366400 | bytes 13271040 | tf_op jit(solution)/shard_map/finish/pallas_call | solution.py:342
  (93 shorter events, 28.4 us)
Async XLA Ops:
  2.0 11.6 %collective-permute-start = (bf16[80,1152]{1,0:T(8,128)(2,1)S(1)}, bf16[80,1152]{1,0:T(8,128)(2,1)S(1)}, u32[]{:S(2)}, u32[]{:S(2)}) collective-permute-start(bf16[80,1152]{1,0:T(8,128)(2,1)S(1)} %get-tuple-element.21), channel_id=1, source_target_pairs={{0,2},{1,3},{2,0},{3,1},{4,6},{5,7},{6,4},{7,5},{8,10},{9,11},{10,... | collective-permute-start | bytes 552968 | tf_op jit(solution)/shard_map/ppermute | solution.py:373
  5.1 11.7 %collective-permute-start.16 = (bf16[80,1152]{1,0:T(8,128)(2,1)S(1)}, bf16[80,1152]{1,0:T(8,128)(2,1)S(1)}, u32[]{:S(2)}, u32[]{:S(2)}) collective-permute-start(bf16[80,1152]{1,0:T(8,128)(2,1)S(1)} %get-tuple-element.29), channel_id=1, source_target_pairs={{0,4},{1,5},{2,6},{3,7},{4,0},{5,1},{6,2},{7,3},{8,12},{9,13},{10,... | collective-permute-start | bytes 552968 | tf_op jit(solution)/shard_map/ppermute | solution.py:373
  7.7 11.5 %collective-permute-start.11 = (bf16[80,1152]{1,0:T(8,128)(2,1)S(1)}, bf16[80,1152]{1,0:T(8,128)(2,1)S(1)}, u32[]{:S(2)}, u32[]{:S(2)}) collective-permute-start(bf16[80,1152]{1,0:T(8,128)(2,1)S(1)} %get-tuple-element.26.refs_0_), channel_id=1, source_target_pairs={{0,16},{1,17},{2,18},{3,19},{4,20},{5,21},{6,22},{7,23},{8,24},{9,... | collective-permute-start | bytes 552968 | tf_op jit(solution)/shard_map/ppermute | solution.py:373
  9.2 10.9 %collective-permute-start.10 = (bf16[80,1152]{1,0:T(8,128)(2,1)S(1)}, bf16[80,1152]{1,0:T(8,128)(2,1)S(1)}, u32[]{:S(2)}, u32[]{:S(2)}) collective-permute-start(bf16[80,1152]{1,0:T(8,128)(2,1)S(1)} %get-tuple-element.26.refs_0_), channel_id=1, source_target_pairs={{0,1},{1,0},{2,3},{3,2},{4,5},{5,4},{6,7},{7,6},{8,9},{9,8},{10,11... | collective-permute-start | bytes 552968 | tf_op jit(solution)/shard_map/ppermute | solution.py:373
  13.6 8.0 %collective-permute-start.2 = (bf16[80,1152]{1,0:T(8,128)(2,1)S(1)}, bf16[80,1152]{1,0:T(8,128)(2,1)S(1)}, u32[]{:S(2)}, u32[]{:S(2)}) collective-permute-start(bf16[80,1152]{1,0:T(8,128)(2,1)S(1)} %collective-permute-done.refs_0_), channel_id=1, source_target_pairs={{0,16},{1,17},{2,18},{3,19},{4,20},{5,21},{6,22},{7,23},{8,24},{9,... | collective-permute-start | bytes 552968 | tf_op jit(solution)/shard_map/ppermute | solution.py:373
  15.3 7.0 %collective-permute-start.1 = (bf16[80,1152]{1,0:T(8,128)(2,1)S(1)}, bf16[80,1152]{1,0:T(8,128)(2,1)S(1)}, u32[]{:S(2)}, u32[]{:S(2)}) collective-permute-start(bf16[80,1152]{1,0:T(8,128)(2,1)S(1)} %collective-permute-done.refs_0_), channel_id=1, source_target_pairs={{0,1},{1,0},{2,3},{3,2},{4,5},{5,4},{6,7},{7,6},{8,9},{9,8},{10,11... | collective-permute-start | bytes 552968 | tf_op jit(solution)/shard_map/ppermute | solution.py:373
  16.8 7.4 %collective-permute-start.5 = (bf16[80,1152]{1,0:T(8,128)(2,1)S(1)}, bf16[80,1152]{1,0:T(8,128)(2,1)S(1)}, u32[]{:S(2)}, u32[]{:S(2)}) collective-permute-start(bf16[80,1152]{1,0:T(8,128)(2,1)S(1)} %get-tuple-element.23), channel_id=1, source_target_pairs={{0,6},{1,7},{2,4},{3,5},{4,2},{5,3},{6,0},{7,1},{8,14},{9,15},{10,... | collective-permute-start | bytes 552968 | tf_op jit(solution)/shard_map/ppermute | solution.py:373
  20.1 9.4 %collective-permute-start.17 = (bf16[80,1152]{1,0:T(8,128)(2,1)S(1)}, bf16[80,1152]{1,0:T(8,128)(2,1)S(1)}, u32[]{:S(2)}, u32[]{:S(2)}) collective-permute-start(bf16[80,1152]{1,0:T(8,128)(2,1)S(1)} %collective-permute-done.16.refs_0_), channel_id=1, source_target_pairs={{0,1},{1,0},{2,3},{3,2},{4,5},{5,4},{6,7},{7,6},{8,9},{9,8},{10,11... | collective-permute-start | bytes 552968 | tf_op jit(solution)/shard_map/ppermute | solution.py:373
  21.6 9.5 %collective-permute-start.12 = (bf16[48,1152]{1,0:T(8,128)(2,1)S(1)}, bf16[48,1152]{1,0:T(8,128)(2,1)S(1)}, u32[]{:S(2)}, u32[]{:S(2)}) collective-permute-start(bf16[48,1152]{1,0:T(8,128)(2,1)S(1)} %slice.100), channel_id=1, source_target_pairs={{0,1},{1,0},{2,3},{3,2},{4,5},{5,4},{6,7},{7,6},{8,9},{9,8},{10,11... | collective-permute-start | bytes 331784 | tf_op jit(solution)/shard_map/ppermute | solution.py:373
  22.2 7.6 %collective-permute-start.13 = (bf16[32,1152]{1,0:T(8,128)(2,1)S(1)}, bf16[32,1152]{1,0:T(8,128)(2,1)S(1)}, u32[]{:S(2)}, u32[]{:S(2)}) collective-permute-start(bf16[32,1152]{1,0:T(8,128)(2,1)S(1)} %slice.101), channel_id=1, source_target_pairs={{0,16},{1,17},{2,18},{3,19},{4,20},{5,21},{6,22},{7,23},{8,24},{9,... | collective-permute-start | bytes 221192 | tf_op jit(solution)/shard_map/ppermute | solution.py:373
  24.2 10.7 %collective-permute-start.3 = (bf16[48,1152]{1,0:T(8,128)(2,1)S(1)}, bf16[48,1152]{1,0:T(8,128)(2,1)S(1)}, u32[]{:S(2)}, u32[]{:S(2)}) collective-permute-start(bf16[48,1152]{1,0:T(8,128)(2,1)S(1)} %slice.96), channel_id=1, source_target_pairs={{0,1},{1,0},{2,3},{3,2},{4,5},{5,4},{6,7},{7,6},{8,9},{9,8},{10,11... | collective-permute-start | bytes 331784 | tf_op jit(solution)/shard_map/ppermute | solution.py:373
  25.2 8.2 %collective-permute-start.4 = (bf16[32,1152]{1,0:T(8,128)(2,1)S(1)}, bf16[32,1152]{1,0:T(8,128)(2,1)S(1)}, u32[]{:S(2)}, u32[]{:S(2)}) collective-permute-start(bf16[32,1152]{1,0:T(8,128)(2,1)S(1)} %slice.97), channel_id=1, source_target_pairs={{0,16},{1,17},{2,18},{3,19},{4,20},{5,21},{6,22},{7,23},{8,24},{9,... | collective-permute-start | bytes 221192 | tf_op jit(solution)/shard_map/ppermute | solution.py:373
  29.5 8.4 %collective-permute-start.7 = (bf16[80,1152]{1,0:T(8,128)(2,1)S(1)}, bf16[80,1152]{1,0:T(8,128)(2,1)S(1)}, u32[]{:S(2)}, u32[]{:S(2)}) collective-permute-start(bf16[80,1152]{1,0:T(8,128)(2,1)S(1)} %collective-permute-done.5.refs_0_), channel_id=1, source_target_pairs={{0,16},{1,17},{2,18},{3,19},{4,20},{5,21},{6,22},{7,23},{8,24},{9,... | collective-permute-start | bytes 552968 | tf_op jit(solution)/shard_map/ppermute | solution.py:373
  34.9 16.7 %collective-permute-start.14 = (bf16[2,4,320,128]{3,2,1,0:T(8,128)(2,1)S(1)}, bf16[2,4,320,128]{3,2,1,0:T(8,128)(2,1)S(1)}, u32[]{:S(2)}, u32[]{:S(2)}) collective-permute-start(bf16[2,4,320,128]{3,2,1,0:T(8,128)(2,1)S(1)} %get-tuple-element.27.refs_2_), channel_id=1, source_target_pairs={{0,8},{1,9},{2,10},{3,11},{4,12},{5,13},{6,14},{7,15},{8,0},{9,1},... | collective-permute-start | bytes 1966088 | tf_op jit(solution)/shard_map/ppermute | solution.py:373
  36.0 15.5 %collective-permute-start.15 = (bf16[2,4,320,128]{3,2,1,0:T(8,128)(2,1)S(1)}, bf16[2,4,320,128]{3,2,1,0:T(8,128)(2,1)S(1)}, u32[]{:S(2)}, u32[]{:S(2)}) collective-permute-start(bf16[2,4,320,128]{3,2,1,0:T(8,128)(2,1)S(1)} %get-tuple-element.28.refs_4_), channel_id=1, source_target_pairs={{0,8},{1,9},{2,10},{3,11},{4,12},{5,13},{6,14},{7,15},{8,0},{9,1},... | collective-permute-start | bytes 1966088 | tf_op jit(solution)/shard_map/ppermute | solution.py:373
  37.8 13.8 %collective-permute-start.21 = (bf16[2,4,320,128]{3,2,1,0:T(8,128)(2,1)S(1)}, bf16[2,4,320,128]{3,2,1,0:T(8,128)(2,1)S(1)}, u32[]{:S(2)}, u32[]{:S(2)}) collective-permute-start(bf16[2,4,320,128]{3,2,1,0:T(8,128)(2,1)S(1)} %get-tuple-element.30.refs_6_), channel_id=1, source_target_pairs={{0,8},{1,9},{2,10},{3,11},{4,12},{5,13},{6,14},{7,15},{8,0},{9,1},... | collective-permute-start | bytes 1966088 | tf_op jit(solution)/shard_map/ppermute | solution.py:373
  40.0 11.6 %collective-permute-start.22 = (bf16[2,4,240,128]{3,2,1,0:T(8,128)(2,1)S(1)}, bf16[2,4,240,128]{3,2,1,0:T(8,128)(2,1)S(1)}, u32[]{:S(2)}, u32[]{:S(2)}) collective-permute-start(bf16[2,4,240,128]{3,2,1,0:T(8,128)(2,1)S(1)} %get-tuple-element.31.refs_8_), channel_id=1, source_target_pairs={{0,8},{1,9},{2,10},{3,11},{4,12},{5,13},{6,14},{7,15},{8,0},{9,1},... | collective-permute-start | bytes 1474568 | tf_op jit(solution)/shard_map/ppermute | solution.py:373
  71.9 9.7 %collective-permute-start.29 = (bf16[4,192,128]{2,1,0:T(8,128)(2,1)S(1)}, bf16[4,192,128]{2,1,0:T(8,128)(2,1)S(1)}, u32[]{:S(2)}, u32[]{:S(2)}) collective-permute-start(bf16[4,192,128]{2,1,0:T(8,128)(2,1)S(1)} %get-tuple-element.35), channel_id=1, source_target_pairs={{0,6},{1,7},{2,4},{3,5},{4,2},{5,3},{6,0},{7,1},{8,14},{9,15},{10,... | collective-permute-start | bytes 589832 | tf_op jit(solution)/shard_map/ppermute | solution.py:373
  74.0 11.4 %collective-permute-start.24 = (bf16[4,192,128]{2,1,0:T(8,128)(2,1)S(1)}, bf16[4,192,128]{2,1,0:T(8,128)(2,1)S(1)}, u32[]{:S(2)}, u32[]{:S(2)}) collective-permute-start(bf16[4,192,128]{2,1,0:T(8,128)(2,1)S(1)} %attend.5), channel_id=1, source_target_pairs={{0,2},{1,3},{2,0},{3,1},{4,6},{5,7},{6,4},{7,5},{8,10},{9,11},{10,... | collective-permute-start | bytes 589832 | tf_op jit(solution)/shard_map/ppermute | solution.py:373
  74.4 18.5 %collective-permute-start.25 = (bf16[4,192,128]{2,1,0:T(8,128)(2,1)S(1)}, bf16[4,192,128]{2,1,0:T(8,128)(2,1)S(1)}, u32[]{:S(2)}, u32[]{:S(2)}) collective-permute-start(bf16[4,192,128]{2,1,0:T(8,128)(2,1)S(1)} %attend.6), channel_id=1, source_target_pairs={{0,4},{1,5},{2,6},{3,7},{4,0},{5,1},{6,2},{7,3},{8,12},{9,13},{10,... | collective-permute-start | bytes 589832 | tf_op jit(solution)/shard_map/ppermute | solution.py:373
  81.6 13.9 %collective-permute-start.30 = (bf16[2,192,128]{2,1,0:T(8,128)(2,1)S(1)}, bf16[2,192,128]{2,1,0:T(8,128)(2,1)S(1)}, u32[]{:S(2)}, u32[]{:S(2)}) collective-permute-start(bf16[2,192,128]{2,1,0:T(8,128)(2,1)S(1)} %pad_maximum_fusion.5), channel_id=1, source_target_pairs={{0,1},{1,0},{2,3},{3,2},{4,5},{5,4},{6,7},{7,6},{8,9},{9,8},{10,11... | collective-permute-start | bytes 294920 | tf_op jit(solution)/shard_map/ppermute | solution.py:373
  83.2 13.8 %collective-permute-start.31 = (bf16[2,192,128]{2,1,0:T(8,128)(2,1)S(1)}, bf16[2,192,128]{2,1,0:T(8,128)(2,1)S(1)}, u32[]{:S(2)}, u32[]{:S(2)}) collective-permute-start(bf16[2,192,128]{2,1,0:T(8,128)(2,1)S(1)} %pad_maximum_fusion.6), channel_id=1, source_target_pairs={{0,16},{1,17},{2,18},{3,19},{4,20},{5,21},{6,22},{7,23},{8,24},{9,... | collective-permute-start | bytes 294920 | tf_op jit(solution)/shard_map/ppermute | solution.py:373
  83.5 13.5 %collective-permute-start.32 = (bf16[2,192,128]{2,1,0:T(8,128)(2,1)S(1)}, bf16[2,192,128]{2,1,0:T(8,128)(2,1)S(1)}, u32[]{:S(2)}, u32[]{:S(2)}) collective-permute-start(bf16[2,192,128]{2,1,0:T(8,128)(2,1)S(1)} %pad_maximum_fusion.7), channel_id=1, source_target_pairs={{0,17},{1,16},{2,19},{3,18},{4,21},{5,20},{6,23},{7,22},{8,25},{9,... | collective-permute-start | bytes 294920 | tf_op jit(solution)/shard_map/ppermute | solution.py:373
  93.2 7.2 %collective-permute-start.26 = (bf16[2,192,128]{2,1,0:T(8,128)(2,1)S(1)}, bf16[2,192,128]{2,1,0:T(8,128)(2,1)S(1)}, u32[]{:S(2)}, u32[]{:S(2)}) collective-permute-start(bf16[2,192,128]{2,1,0:T(8,128)(2,1)S(1)} %pad_maximum_fusion.1), channel_id=1, source_target_pairs={{0,1},{1,0},{2,3},{3,2},{4,5},{5,4},{6,7},{7,6},{8,9},{9,8},{10,11... | collective-permute-start | bytes 294920 | tf_op jit(solution)/shard_map/ppermute | solution.py:373
  (17 other events, 297.3 us)

commit v7 on v6

--- a/solution.py
+++ b/solution.py
@@ -237,7 +237,7 @@
     return jnp.concatenate(columns, axis=1)
 
 
-def attend_kernel(chips, capacity, first_row, query_count, piece_count, *refs):
+def attend_kernel(chips, capacity, query_count, piece_count, *refs):
     queries, pieces = refs[:query_count], refs[query_count : query_count + piece_count]
     out_ref = refs[query_count + piece_count]
     if piece_count > 1:
@@ -252,7 +252,6 @@
     results = []
     for head in range(kv_ref.shape[1]):
         query = jnp.concatenate([ref[head] for ref in queries], axis=0)
-        query = query[first_row : first_row + chips * capacity]
         score = lax.dot_general(query, kv_ref[0, head], nt, preferred_element_type=F32)
         top = jnp.max(score, axis=1, keepdims=True)
         probs = jnp.exp2(score - top).astype(BF16)
@@ -268,8 +267,7 @@
         pack(block, write)
 
 
-def attend(queries, pieces, chips, capacity, index, halves):
-    chips //= halves
+def attend(queries, pieces, chips, capacity):
     head_count, rows = queries[0].shape[0], chips * capacity
     keys = sum(piece.shape[2] for piece in pieces)
     out_rows = packed_rows(capacity, head_count * HD)[0]
@@ -277,7 +275,7 @@
     if len(pieces) > 1:
         out_shape.append(jax.ShapeDtypeStruct((2, head_count, keys, LANE), BF16))
     made = pl.pallas_call(
-        functools.partial(attend_kernel, chips, capacity, index * rows, len(queries), len(pieces)),
+        functools.partial(attend_kernel, chips, capacity, len(queries), len(pieces)),
         in_specs=[vmem()] * (len(queries) + len(pieces)),
         out_specs=[vmem()] * len(out_shape),
         out_shape=out_shape,
@@ -408,14 +406,15 @@
             shares.append(swap(share, dx=j // along, dy=j % along) if j else share)
         return shares
 
-    for k in reversed(range(bags)):
-        halves = 1
-        mixed[k] = []
-        for index in range(halves):
-            part, kv = attend(queries[k], pieces, chips, capacity, index, halves)
-            pieces = [kv]
-            part = swap(part, dz=k) if k else part
-            mixed[k] += [part[j] for j in range(part.shape[0])]
+    for k in reversed(range(1, bags)):
+        asked = queries[k] if k > 1 else queries[1] + queries[0]
+        part, kv = attend(asked, pieces, chips if k > 1 else 2 * chips, capacity)
+        pieces = [kv]
+        part = [part[j] for j in range(part.shape[0])]
+        if k == 1:
+            mixed[0] = part[chips:]
+        away = swap(jnp.stack(part[:chips]), dz=k)
+        mixed[k] = [away[j] for j in range(chips)]
     shares = [exchange(index) for index in range(len(rounds))]
     done = []
     for index in range(len(rounds)):

time: 106 us -> 105 us (level)
    pallas_call x4 -> x3, Pallas kernels: 20.3 us -> 19.6 us  [attend(): pl.pallas_call(functools.partial(attend_kernel, chips, capacity, len(quer...]
where the time goes in v7:
time: 105 us
  starting transfers between devices  40 us (38%)
  Pallas kernels  37 us (35%)
  waiting for transfers between devices  27.5 us (26%)
    ppermute x33, starting transfers between devices, swap(): return lax.ppermute(value, AXES, pairs)  40 us
    ppermute x33, waiting for transfers between devices, swap(): return lax.ppermute(value, AXES, pairs)  27.5 us
    pallas_call x3, Pallas kernels, attend(): pl.pallas_call(functools.partial(attend_kernel, chips, capacity, len(quer...  19.6 us
    pallas_call x2, Pallas kernels, finish(): pl.pallas_call(functools.partial(finish_kernel, capacity, chips, rounds,...  7.9 us
    pallas_call x5, Pallas kernels, project(): pl.pallas_call(functools.partial(project_kernel, head_count), in_specs=[v...  4.96 us
    pallas_call x1, Pallas kernels, chip_weights(): pl.pallas_call(functools.partial(weight_kernel, part, total // 3 // part)...  2.46 us
  transfers between devices with their start and end apart: 33, of which 10 were waited for; matrix products, arithmetic and copies ran while one was open for 0% of the time, Pallas kernels for 10%

profile of v7, /device:TPU:0, one launch (start us, length us, event | category | flops | bytes accessed | tf_op | source)
XLA Modules:
  0.0 105.1 jit_solution(17170859092146625070)
XLA Ops:
  0.0 2.0 %slot_rows.1 = (bf16[80,1152]{1,0:T(8,128)(2,1)S(1)}, bf16[80,1152]{1,0:T(8,128)(2,1)S(1)}, bf16[80,1152]{1,0:T(8,128)(2,1)S(1)}, bf16[80,1152]{1,0:T(8,128)(2,1)S(1)}) custom-call(bf16[256,1152]{1,0:T(8,128)(2,1)} %tokens_ref.5, s32[1,256]{1,0:T(1,128)} %bitcast.9, f32[6,4,1152]{2,1,0:T(4,128)} %bitcast.6), custom_call_target="tpu_custom_call" | custom-call | tf_op jit(solution)/shard_map/slot_rows/pallas_call | solution.py:89
  2.0 3.1 %collective-permute-start = (bf16[80,1152]{1,0:T(8,128)(2,1)S(1)}, bf16[80,1152]{1,0:T(8,128)(2,1)S(1)}, u32[]{:S(2)}, u32[]{:S(2)}) collective-permute-start(bf16[80,1152]{1,0:T(8,128)(2,1)S(1)} %get-tuple-element.21), channel_id=1, source_target_pairs={{0,2},{1,3},{2,0},{3,1},{4,6},{5,7},{6,4},{7,5},{8,10},{9,11},{10,... | collective-permute-start | bytes 552968 | tf_op jit(solution)/shard_map/ppermute | solution.py:371
  5.1 2.6 %collective-permute-start.16 = (bf16[80,1152]{1,0:T(8,128)(2,1)S(1)}, bf16[80,1152]{1,0:T(8,128)(2,1)S(1)}, u32[]{:S(2)}, u32[]{:S(2)}) collective-permute-start(bf16[80,1152]{1,0:T(8,128)(2,1)S(1)} %get-tuple-element.30), channel_id=1, source_target_pairs={{0,4},{1,5},{2,6},{3,7},{4,0},{5,1},{6,2},{7,3},{8,12},{9,13},{10,... | collective-permute-start | bytes 552968 | tf_op jit(solution)/shard_map/ppermute | solution.py:371
  9.2 1.5 %collective-permute-start.5 = (bf16[80,1152]{1,0:T(8,128)(2,1)S(1)}, bf16[80,1152]{1,0:T(8,128)(2,1)S(1)}, u32[]{:S(2)}, u32[]{:S(2)}) collective-permute-start(bf16[80,1152]{1,0:T(8,128)(2,1)S(1)} %get-tuple-element.23.refs_0_), channel_id=1, source_target_pairs={{0,1},{1,0},{2,3},{3,2},{4,5},{5,4},{6,7},{7,6},{8,9},{9,8},{10,11... | collective-permute-start | bytes 552968 | tf_op jit(solution)/shard_map/ppermute | solution.py:371
  10.7 2.9 %collective-permute-done.refs_0_ = bf16[80,1152]{1,0:T(8,128)(2,1)S(1)} collective-permute-done((bf16[80,1152]{1,0:T(8,128)(2,1)S(1)}, bf16[80,1152]{1,0:T(8,128)(2,1)S(1)}, u32[]{:S(2)}, u32[]{:S(2)}) %collective-permute-start) | collective-permute-done | bytes 184352 | tf_op jit(solution)/shard_map/ppermute | solution.py:371
  13.6 1.7 %collective-permute-start.2 = (bf16[80,1152]{1,0:T(8,128)(2,1)S(1)}, bf16[80,1152]{1,0:T(8,128)(2,1)S(1)}, u32[]{:S(2)}, u32[]{:S(2)}) collective-permute-start(bf16[80,1152]{1,0:T(8,128)(2,1)S(1)} %collective-permute-done.refs_0_), channel_id=1, source_target_pairs={{0,16},{1,17},{2,18},{3,19},{4,20},{5,21},{6,22},{7,23},{8,24},{9,... | collective-permute-start | bytes 552968 | tf_op jit(solution)/shard_map/ppermute | solution.py:371
  15.3 1.5 %collective-permute-start.1 = (bf16[80,1152]{1,0:T(8,128)(2,1)S(1)}, bf16[80,1152]{1,0:T(8,128)(2,1)S(1)}, u32[]{:S(2)}, u32[]{:S(2)}) collective-permute-start(bf16[80,1152]{1,0:T(8,128)(2,1)S(1)} %collective-permute-done.refs_0_), channel_id=1, source_target_pairs={{0,1},{1,0},{2,3},{3,2},{4,5},{5,4},{6,7},{7,6},{8,9},{9,8},{10,11... | collective-permute-start | bytes 552968 | tf_op jit(solution)/shard_map/ppermute | solution.py:371
  16.8 2.5 %collective-permute-start.9 = (bf16[80,1152]{1,0:T(8,128)(2,1)S(1)}, bf16[80,1152]{1,0:T(8,128)(2,1)S(1)}, u32[]{:S(2)}, u32[]{:S(2)}) collective-permute-start(bf16[80,1152]{1,0:T(8,128)(2,1)S(1)} %get-tuple-element.25), channel_id=1, source_target_pairs={{0,6},{1,7},{2,4},{3,5},{4,2},{5,3},{6,0},{7,1},{8,14},{9,15},{10,... | collective-permute-start | bytes 552968 | tf_op jit(solution)/shard_map/ppermute | solution.py:371
  20.1 1.5 %collective-permute-start.17 = (bf16[80,1152]{1,0:T(8,128)(2,1)S(1)}, bf16[80,1152]{1,0:T(8,128)(2,1)S(1)}, u32[]{:S(2)}, u32[]{:S(2)}) collective-permute-start(bf16[80,1152]{1,0:T(8,128)(2,1)S(1)} %collective-permute-done.16.refs_0_), channel_id=1, source_target_pairs={{0,1},{1,0},{2,3},{3,2},{4,5},{5,4},{6,7},{7,6},{8,9},{9,8},{10,11... | collective-permute-start | bytes 552968 | tf_op jit(solution)/shard_map/ppermute | solution.py:371
  25.2 1.8 %collective-permute-start.4 = (bf16[32,1152]{1,0:T(8,128)(2,1)S(1)}, bf16[32,1152]{1,0:T(8,128)(2,1)S(1)}, u32[]{:S(2)}, u32[]{:S(2)}) collective-permute-start(bf16[32,1152]{1,0:T(8,128)(2,1)S(1)} %slice.115), channel_id=1, source_target_pairs={{0,16},{1,17},{2,18},{3,19},{4,20},{5,21},{6,22},{7,23},{8,24},{9,... | collective-permute-start | bytes 221192 | tf_op jit(solution)/shard_map/ppermute | solution.py:371
  27.0 2.5 %chip_weights.1.refs_5_.refs_3_.refs_2_ = bf16[1152,896]{1,0:T(8,128)(2,1)S(1)} custom-call(bf16[1152,3456]{1,0:T(8,128)(2,1)} %w_ref.1), custom_call_target="tpu_custom_call" | custom-call | flops 1000000000 | bytes 10000000 | tf_op jit(solution)/shard_map/chip_weights/pallas_call | solution.py:131
  41.1 3.7 %collective-permute-done.13.refs_1_ = bf16[32,1152]{1,0:T(8,128)(2,1)S(1)} collective-permute-done((bf16[32,1152]{1,0:T(8,128)(2,1)S(1)}, bf16[32,1152]{1,0:T(8,128)(2,1)S(1)}, u32[]{:S(2)}, u32[]{:S(2)}) %collective-permute-start.13) | collective-permute-done | bytes 73760 | tf_op jit(solution)/shard_map/ppermute | solution.py:371
  46.2 3.3 %collective-permute-done.12.refs_0_ = bf16[48,1152]{1,0:T(8,128)(2,1)S(1)} collective-permute-done((bf16[48,1152]{1,0:T(8,128)(2,1)S(1)}, bf16[48,1152]{1,0:T(8,128)(2,1)S(1)}, u32[]{:S(2)}, u32[]{:S(2)}) %collective-permute-start.12) | collective-permute-done | bytes 110624 | tf_op jit(solution)/shard_map/ppermute | solution.py:371
  51.6 5.1 %attend.3 = (bf16[4,192,128]{2,1,0:T(8,128)(2,1)S(1)}, bf16[2,4,2560,128]{3,2,1,0:T(8,128)(2,1)S(1)}) custom-call(bf16[4,240,128]{2,1,0:T(8,128)(2,1)S(1)} %get-tuple-element.26.refs_0_, bf16[4,80,128]{2,1,0:T(8,128)(2,1)S(1)} %get-tuple-element.27.refs_1_, bf16[2,4,320,128]{3,2,1,0:T(8,128)(2,1)S(1)} %get-tuple-element.28.refs_2_, ...), custom_call_target="tpu_custom_call" | custom-call | flops 1677721600 | bytes 5242880 | tf_op jit(solution)/shard_map/attend/pallas_call | solution.py:277
  56.7 5.2 %attend.5 = bf16[4,192,128]{2,1,0:T(8,128)(2,1)S(1)} custom-call(bf16[4,320,128]{2,1,0:T(8,128)(2,1)S(1)} %get-tuple-element.35.refs_0_, bf16[2,4,2560,128]{3,2,1,0:T(8,128)(2,1)S(1)} %get-tuple-element.34.refs_2_.refs_1_), custom_call_target="tpu_custom_call" | custom-call | flops 1677721600 | bytes 5242880 | tf_op jit(solution)/shard_map/attend/pallas_call | solution.py:277
  61.9 9.3 %attend.4 = bf16[8,192,128]{2,1,0:T(8,128)(2,1)S(1)} custom-call(bf16[4,320,128]{2,1,0:T(8,128)(2,1)S(1)} %get-tuple-element.22.refs_0_, bf16[4,320,128]{2,1,0:T(8,128)(2,1)S(1)} %get-tuple-element.24.refs_1_, bf16[2,4,2560,128]{3,2,1,0:T(8,128)(2,1)S(1)} %get-tuple-element.34.refs_2_.refs_1_), custom_call_target="tpu_custom_call" | custom-call | flops 3355443200 | bytes 5242880 | tf_op jit(solution)/shard_map/attend/pallas_call | solution.py:277
  71.3 2.0 %collective-permute-start.24 = (bf16[4,192,128]{2,1,0:T(8,128)(2,1)S(1)}, bf16[4,192,128]{2,1,0:T(8,128)(2,1)S(1)}, u32[]{:S(2)}, u32[]{:S(2)}) collective-permute-start(bf16[4,192,128]{2,1,0:T(8,128)(2,1)S(1)} %slice.122), channel_id=1, source_target_pairs={{0,2},{1,3},{2,0},{3,1},{4,6},{5,7},{6,4},{7,5},{8,10},{9,11},{10,... | collective-permute-start | bytes 589832 | tf_op jit(solution)/shard_map/ppermute | solution.py:371
  74.9 9.9 %collective-permute-done.29 = bf16[4,192,128]{2,1,0:T(8,128)(2,1)S(1)} collective-permute-done((bf16[4,192,128]{2,1,0:T(8,128)(2,1)S(1)}, bf16[4,192,128]{2,1,0:T(8,128)(2,1)S(1)}, u32[]{:S(2)}, u32[]{:S(2)}) %collective-permute-start.29) | collective-permute-done | bytes 196640 | tf_op jit(solution)/shard_map/ppermute | solution.py:371
  84.8 1.5 %collective-permute-start.30 = (bf16[2,192,128]{2,1,0:T(8,128)(2,1)S(1)}, bf16[2,192,128]{2,1,0:T(8,128)(2,1)S(1)}, u32[]{:S(2)}, u32[]{:S(2)}) collective-permute-start(bf16[2,192,128]{2,1,0:T(8,128)(2,1)S(1)} %pad_maximum_fusion.5), channel_id=1, source_target_pairs={{0,1},{1,0},{2,3},{3,2},{4,5},{5,4},{6,7},{7,6},{8,9},{9,8},{10,11... | collective-permute-start | bytes 294920 | tf_op jit(solution)/shard_map/ppermute | solution.py:371
  87.0 1.5 %collective-permute-start.32 = (bf16[2,192,128]{2,1,0:T(8,128)(2,1)S(1)}, bf16[2,192,128]{2,1,0:T(8,128)(2,1)S(1)}, u32[]{:S(2)}, u32[]{:S(2)}) collective-permute-start(bf16[2,192,128]{2,1,0:T(8,128)(2,1)S(1)} %pad_maximum_fusion.7), channel_id=1, source_target_pairs={{0,17},{1,16},{2,19},{3,18},{4,21},{5,20},{6,23},{7,22},{8,25},{9,... | collective-permute-start | bytes 294920 | tf_op jit(solution)/shard_map/ppermute | solution.py:371
  88.6 3.8 %collective-permute-done.25 = bf16[4,192,128]{2,1,0:T(8,128)(2,1)S(1)} collective-permute-done((bf16[4,192,128]{2,1,0:T(8,128)(2,1)S(1)}, bf16[4,192,128]{2,1,0:T(8,128)(2,1)S(1)}, u32[]{:S(2)}, u32[]{:S(2)}) %collective-permute-start.25) | collective-permute-done | bytes 196640 | tf_op jit(solution)/shard_map/ppermute | solution.py:371
  94.7 1.7 %collective-permute-start.28 = (bf16[2,192,128]{2,1,0:T(8,128)(2,1)S(1)}, bf16[2,192,128]{2,1,0:T(8,128)(2,1)S(1)}, u32[]{:S(2)}, u32[]{:S(2)}) collective-permute-start(bf16[2,192,128]{2,1,0:T(8,128)(2,1)S(1)} %pad_maximum_fusion.3), channel_id=1, source_target_pairs={{0,17},{1,16},{2,19},{3,18},{4,21},{5,20},{6,23},{7,22},{8,25},{9,... | collective-permute-start | bytes 294920 | tf_op jit(solution)/shard_map/ppermute | solution.py:371
  96.6 3.4 %finish.2.refs_4_ = bf16[160,1152]{1,0:T(8,128)(2,1)S(1)} custom-call(bf16[256,1152]{1,0:T(8,128)(2,1)S(1)} %copy-done.1, s32[1,256]{1,0:T(1,128)S(1)} %bitcast.10, f32[6,4,1152]{2,1,0:T(4,128)S(1)} %bitcast.7, bf16[1152,1152]{1,0:T(8,128)(2,1)S(1)} %copy-done, bf16[1152,2304]{1,0:T(8,128)(2,1)S(1)} %bitcast.3, bf16[2304,1152]{1,0:T(8,128)(2,1)S(1)} %bitcast.5, ...), custom_call_target="tpu_custom_call" | custom-call | flops 2123366400 | bytes 13271040 | tf_op jit(solution)/shard_map/finish/pallas_call | solution.py:340
  100.5 4.5 %finish.3 = bf16[256,1152]{1,0:T(8,128)(2,1)} custom-call(bf16[256,1152]{1,0:T(8,128)(2,1)S(1)} %copy-done.1, s32[1,256]{1,0:T(1,128)S(1)} %bitcast.11, f32[6,4,1152]{2,1,0:T(4,128)S(1)} %bitcast.8, bf16[1152,1152]{1,0:T(8,128)(2,1)S(1)} %copy-done, bf16[1152,2304]{1,0:T(8,128)(2,1)S(1)} %bitcast.3, bf16[2304,1152]{1,0:T(8,128)(2,1)S(1)} %bitcast.5, ...), custom_call_target="tpu_custom_call" | custom-call | flops 2123366400 | bytes 13271040 | tf_op jit(solution)/shard_map/finish/pallas_call | solution.py:340
  (93 shorter events, 26.2 us)
Async XLA Ops:
  2.0 11.6 %collective-permute-start = (bf16[80,1152]{1,0:T(8,128)(2,1)S(1)}, bf16[80,1152]{1,0:T(8,128)(2,1)S(1)}, u32[]{:S(2)}, u32[]{:S(2)}) collective-permute-start(bf16[80,1152]{1,0:T(8,128)(2,1)S(1)} %get-tuple-element.21), channel_id=1, source_target_pairs={{0,2},{1,3},{2,0},{3,1},{4,6},{5,7},{6,4},{7,5},{8,10},{9,11},{10,... | collective-permute-start | bytes 552968 | tf_op jit(solution)/shard_map/ppermute | solution.py:371
  5.1 11.7 %collective-permute-start.16 = (bf16[80,1152]{1,0:T(8,128)(2,1)S(1)}, bf16[80,1152]{1,0:T(8,128)(2,1)S(1)}, u32[]{:S(2)}, u32[]{:S(2)}) collective-permute-start(bf16[80,1152]{1,0:T(8,128)(2,1)S(1)} %get-tuple-element.30), channel_id=1, source_target_pairs={{0,4},{1,5},{2,6},{3,7},{4,0},{5,1},{6,2},{7,3},{8,12},{9,13},{10,... | collective-permute-start | bytes 552968 | tf_op jit(solution)/shard_map/ppermute | solution.py:371
  7.7 11.5 %collective-permute-start.6 = (bf16[80,1152]{1,0:T(8,128)(2,1)S(1)}, bf16[80,1152]{1,0:T(8,128)(2,1)S(1)}, u32[]{:S(2)}, u32[]{:S(2)}) collective-permute-start(bf16[80,1152]{1,0:T(8,128)(2,1)S(1)} %get-tuple-element.23.refs_0_), channel_id=1, source_target_pairs={{0,16},{1,17},{2,18},{3,19},{4,20},{5,21},{6,22},{7,23},{8,24},{9,... | collective-permute-start | bytes 552968 | tf_op jit(solution)/shard_map/ppermute | solution.py:371
  9.2 10.9 %collective-permute-start.5 = (bf16[80,1152]{1,0:T(8,128)(2,1)S(1)}, bf16[80,1152]{1,0:T(8,128)(2,1)S(1)}, u32[]{:S(2)}, u32[]{:S(2)}) collective-permute-start(bf16[80,1152]{1,0:T(8,128)(2,1)S(1)} %get-tuple-element.23.refs_0_), channel_id=1, source_target_pairs={{0,1},{1,0},{2,3},{3,2},{4,5},{5,4},{6,7},{7,6},{8,9},{9,8},{10,11... | collective-permute-start | bytes 552968 | tf_op jit(solution)/shard_map/ppermute | solution.py:371
  13.6 8.0 %collective-permute-start.2 = (bf16[80,1152]{1,0:T(8,128)(2,1)S(1)}, bf16[80,1152]{1,0:T(8,128)(2,1)S(1)}, u32[]{:S(2)}, u32[]{:S(2)}) collective-permute-start(bf16[80,1152]{1,0:T(8,128)(2,1)S(1)} %collective-permute-done.refs_0_), channel_id=1, source_target_pairs={{0,16},{1,17},{2,18},{3,19},{4,20},{5,21},{6,22},{7,23},{8,24},{9,... | collective-permute-start | bytes 552968 | tf_op jit(solution)/shard_map/ppermute | solution.py:371
  15.3 7.0 %collective-permute-start.1 = (bf16[80,1152]{1,0:T(8,128)(2,1)S(1)}, bf16[80,1152]{1,0:T(8,128)(2,1)S(1)}, u32[]{:S(2)}, u32[]{:S(2)}) collective-permute-start(bf16[80,1152]{1,0:T(8,128)(2,1)S(1)} %collective-permute-done.refs_0_), channel_id=1, source_target_pairs={{0,1},{1,0},{2,3},{3,2},{4,5},{5,4},{6,7},{7,6},{8,9},{9,8},{10,11... | collective-permute-start | bytes 552968 | tf_op jit(solution)/shard_map/ppermute | solution.py:371
  16.8 7.4 %collective-permute-start.9 = (bf16[80,1152]{1,0:T(8,128)(2,1)S(1)}, bf16[80,1152]{1,0:T(8,128)(2,1)S(1)}, u32[]{:S(2)}, u32[]{:S(2)}) collective-permute-start(bf16[80,1152]{1,0:T(8,128)(2,1)S(1)} %get-tuple-element.25), channel_id=1, source_target_pairs={{0,6},{1,7},{2,4},{3,5},{4,2},{5,3},{6,0},{7,1},{8,14},{9,15},{10,... | collective-permute-start | bytes 552968 | tf_op jit(solution)/shard_map/ppermute | solution.py:371
  20.1 9.4 %collective-permute-start.17 = (bf16[80,1152]{1,0:T(8,128)(2,1)S(1)}, bf16[80,1152]{1,0:T(8,128)(2,1)S(1)}, u32[]{:S(2)}, u32[]{:S(2)}) collective-permute-start(bf16[80,1152]{1,0:T(8,128)(2,1)S(1)} %collective-permute-done.16.refs_0_), channel_id=1, source_target_pairs={{0,1},{1,0},{2,3},{3,2},{4,5},{5,4},{6,7},{7,6},{8,9},{9,8},{10,11... | collective-permute-start | bytes 552968 | tf_op jit(solution)/shard_map/ppermute | solution.py:371
  21.6 9.5 %collective-permute-start.7 = (bf16[48,1152]{1,0:T(8,128)(2,1)S(1)}, bf16[48,1152]{1,0:T(8,128)(2,1)S(1)}, u32[]{:S(2)}, u32[]{:S(2)}) collective-permute-start(bf16[48,1152]{1,0:T(8,128)(2,1)S(1)} %slice.116), channel_id=1, source_target_pairs={{0,1},{1,0},{2,3},{3,2},{4,5},{5,4},{6,7},{7,6},{8,9},{9,8},{10,11... | collective-permute-start | bytes 331784 | tf_op jit(solution)/shard_map/ppermute | solution.py:371
  22.2 7.6 %collective-permute-start.8 = (bf16[32,1152]{1,0:T(8,128)(2,1)S(1)}, bf16[32,1152]{1,0:T(8,128)(2,1)S(1)}, u32[]{:S(2)}, u32[]{:S(2)}) collective-permute-start(bf16[32,1152]{1,0:T(8,128)(2,1)S(1)} %slice.117), channel_id=1, source_target_pairs={{0,16},{1,17},{2,18},{3,19},{4,20},{5,21},{6,22},{7,23},{8,24},{9,... | collective-permute-start | bytes 221192 | tf_op jit(solution)/shard_map/ppermute | solution.py:371
  24.2 10.7 %collective-permute-start.3 = (bf16[48,1152]{1,0:T(8,128)(2,1)S(1)}, bf16[48,1152]{1,0:T(8,128)(2,1)S(1)}, u32[]{:S(2)}, u32[]{:S(2)}) collective-permute-start(bf16[48,1152]{1,0:T(8,128)(2,1)S(1)} %slice.114), channel_id=1, source_target_pairs={{0,1},{1,0},{2,3},{3,2},{4,5},{5,4},{6,7},{7,6},{8,9},{9,8},{10,11... | collective-permute-start | bytes 331784 | tf_op jit(solution)/shard_map/ppermute | solution.py:371
  25.2 8.2 %collective-permute-start.4 = (bf16[32,1152]{1,0:T(8,128)(2,1)S(1)}, bf16[32,1152]{1,0:T(8,128)(2,1)S(1)}, u32[]{:S(2)}, u32[]{:S(2)}) collective-permute-start(bf16[32,1152]{1,0:T(8,128)(2,1)S(1)} %slice.115), channel_id=1, source_target_pairs={{0,16},{1,17},{2,18},{3,19},{4,20},{5,21},{6,22},{7,23},{8,24},{9,... | collective-permute-start | bytes 221192 | tf_op jit(solution)/shard_map/ppermute | solution.py:371
  29.5 8.4 %collective-permute-start.11 = (bf16[80,1152]{1,0:T(8,128)(2,1)S(1)}, bf16[80,1152]{1,0:T(8,128)(2,1)S(1)}, u32[]{:S(2)}, u32[]{:S(2)}) collective-permute-start(bf16[80,1152]{1,0:T(8,128)(2,1)S(1)} %collective-permute-done.9.refs_0_), channel_id=1, source_target_pairs={{0,16},{1,17},{2,18},{3,19},{4,20},{5,21},{6,22},{7,23},{8,24},{9,... | collective-permute-start | bytes 552968 | tf_op jit(solution)/shard_map/ppermute | solution.py:371
  34.9 16.7 %collective-permute-start.14 = (bf16[2,4,320,128]{3,2,1,0:T(8,128)(2,1)S(1)}, bf16[2,4,320,128]{3,2,1,0:T(8,128)(2,1)S(1)}, u32[]{:S(2)}, u32[]{:S(2)}) collective-permute-start(bf16[2,4,320,128]{3,2,1,0:T(8,128)(2,1)S(1)} %get-tuple-element.28.refs_2_), channel_id=1, source_target_pairs={{0,8},{1,9},{2,10},{3,11},{4,12},{5,13},{6,14},{7,15},{8,0},{9,1},... | collective-permute-start | bytes 1966088 | tf_op jit(solution)/shard_map/ppermute | solution.py:371
  36.0 15.5 %collective-permute-start.15 = (bf16[2,4,320,128]{3,2,1,0:T(8,128)(2,1)S(1)}, bf16[2,4,320,128]{3,2,1,0:T(8,128)(2,1)S(1)}, u32[]{:S(2)}, u32[]{:S(2)}) collective-permute-start(bf16[2,4,320,128]{3,2,1,0:T(8,128)(2,1)S(1)} %get-tuple-element.29.refs_4_), channel_id=1, source_target_pairs={{0,8},{1,9},{2,10},{3,11},{4,12},{5,13},{6,14},{7,15},{8,0},{9,1},... | collective-permute-start | bytes 1966088 | tf_op jit(solution)/shard_map/ppermute | solution.py:371
  37.8 13.8 %collective-permute-start.21 = (bf16[2,4,320,128]{3,2,1,0:T(8,128)(2,1)S(1)}, bf16[2,4,320,128]{3,2,1,0:T(8,128)(2,1)S(1)}, u32[]{:S(2)}, u32[]{:S(2)}) collective-permute-start(bf16[2,4,320,128]{3,2,1,0:T(8,128)(2,1)S(1)} %get-tuple-element.31.refs_6_), channel_id=1, source_target_pairs={{0,8},{1,9},{2,10},{3,11},{4,12},{5,13},{6,14},{7,15},{8,0},{9,1},... | collective-permute-start | bytes 1966088 | tf_op jit(solution)/shard_map/ppermute | solution.py:371
  40.0 11.6 %collective-permute-start.22 = (bf16[2,4,240,128]{3,2,1,0:T(8,128)(2,1)S(1)}, bf16[2,4,240,128]{3,2,1,0:T(8,128)(2,1)S(1)}, u32[]{:S(2)}, u32[]{:S(2)}) collective-permute-start(bf16[2,4,240,128]{3,2,1,0:T(8,128)(2,1)S(1)} %get-tuple-element.32.refs_8_), channel_id=1, source_target_pairs={{0,8},{1,9},{2,10},{3,11},{4,12},{5,13},{6,14},{7,15},{8,0},{9,1},... | collective-permute-start | bytes 1474568 | tf_op jit(solution)/shard_map/ppermute | solution.py:371
  71.3 17.2 %collective-permute-start.24 = (bf16[4,192,128]{2,1,0:T(8,128)(2,1)S(1)}, bf16[4,192,128]{2,1,0:T(8,128)(2,1)S(1)}, u32[]{:S(2)}, u32[]{:S(2)}) collective-permute-start(bf16[4,192,128]{2,1,0:T(8,128)(2,1)S(1)} %slice.122), channel_id=1, source_target_pairs={{0,2},{1,3},{2,0},{3,1},{4,6},{5,7},{6,4},{7,5},{8,10},{9,11},{10,... | collective-permute-start | bytes 589832 | tf_op jit(solution)/shard_map/ppermute | solution.py:371
  73.3 11.5 %collective-permute-start.29 = (bf16[4,192,128]{2,1,0:T(8,128)(2,1)S(1)}, bf16[4,192,128]{2,1,0:T(8,128)(2,1)S(1)}, u32[]{:S(2)}, u32[]{:S(2)}) collective-permute-start(bf16[4,192,128]{2,1,0:T(8,128)(2,1)S(1)} %get-tuple-element.36), channel_id=1, source_target_pairs={{0,6},{1,7},{2,4},{3,5},{4,2},{5,3},{6,0},{7,1},{8,14},{9,15},{10,... | collective-permute-start | bytes 589832 | tf_op jit(solution)/shard_map/ppermute | solution.py:371
  74.7 17.7 %collective-permute-start.25 = (bf16[4,192,128]{2,1,0:T(8,128)(2,1)S(1)}, bf16[4,192,128]{2,1,0:T(8,128)(2,1)S(1)}, u32[]{:S(2)}, u32[]{:S(2)}) collective-permute-start(bf16[4,192,128]{2,1,0:T(8,128)(2,1)S(1)} %attend.5), channel_id=1, source_target_pairs={{0,4},{1,5},{2,6},{3,7},{4,0},{5,1},{6,2},{7,3},{8,12},{9,13},{10,... | collective-permute-start | bytes 589832 | tf_op jit(solution)/shard_map/ppermute | solution.py:371
  84.8 9.9 %collective-permute-start.30 = (bf16[2,192,128]{2,1,0:T(8,128)(2,1)S(1)}, bf16[2,192,128]{2,1,0:T(8,128)(2,1)S(1)}, u32[]{:S(2)}, u32[]{:S(2)}) collective-permute-start(bf16[2,192,128]{2,1,0:T(8,128)(2,1)S(1)} %pad_maximum_fusion.5), channel_id=1, source_target_pairs={{0,1},{1,0},{2,3},{3,2},{4,5},{5,4},{6,7},{7,6},{8,9},{9,8},{10,11... | collective-permute-start | bytes 294920 | tf_op jit(solution)/shard_map/ppermute | solution.py:371
  86.3 10.1 %collective-permute-start.31 = (bf16[2,192,128]{2,1,0:T(8,128)(2,1)S(1)}, bf16[2,192,128]{2,1,0:T(8,128)(2,1)S(1)}, u32[]{:S(2)}, u32[]{:S(2)}) collective-permute-start(bf16[2,192,128]{2,1,0:T(8,128)(2,1)S(1)} %pad_maximum_fusion.6), channel_id=1, source_target_pairs={{0,16},{1,17},{2,18},{3,19},{4,20},{5,21},{6,22},{7,23},{8,24},{9,... | collective-permute-start | bytes 294920 | tf_op jit(solution)/shard_map/ppermute | solution.py:371
  87.0 9.4 %collective-permute-start.32 = (bf16[2,192,128]{2,1,0:T(8,128)(2,1)S(1)}, bf16[2,192,128]{2,1,0:T(8,128)(2,1)S(1)}, u32[]{:S(2)}, u32[]{:S(2)}) collective-permute-start(bf16[2,192,128]{2,1,0:T(8,128)(2,1)S(1)} %pad_maximum_fusion.7), channel_id=1, source_target_pairs={{0,17},{1,16},{2,19},{3,18},{4,21},{5,20},{6,23},{7,22},{8,25},{9,... | collective-permute-start | bytes 294920 | tf_op jit(solution)/shard_map/ppermute | solution.py:371
  92.4 7.5 %collective-permute-start.26 = (bf16[2,192,128]{2,1,0:T(8,128)(2,1)S(1)}, bf16[2,192,128]{2,1,0:T(8,128)(2,1)S(1)}, u32[]{:S(2)}, u32[]{:S(2)}) collective-permute-start(bf16[2,192,128]{2,1,0:T(8,128)(2,1)S(1)} %pad_maximum_fusion.1), channel_id=1, source_target_pairs={{0,1},{1,0},{2,3},{3,2},{4,5},{5,4},{6,7},{7,6},{8,9},{9,8},{10,11... | collective-permute-start | bytes 294920 | tf_op jit(solution)/shard_map/ppermute | solution.py:371
  (17 other events, 323.1 us)

commit v8 on v7

--- a/solution.py
+++ b/solution.py
@@ -65,7 +65,7 @@
     return min(aligned, last) if isinstance(start, int) else jnp.minimum(aligned, last)
 
 
-def slot_kernel(capacity, tokens_ref, seq_ref, mod_ref, *out_refs):
+def slot_kernel(capacity, tokens_ref, seq_ref, mod_ref, raw_ref, pick_ref, *out_refs):
     me, _ = coordinates()
     row_count, width = tokens_ref.shape
     block_count = len(out_refs)
@@ -75,6 +75,8 @@
     pick = jnp.where(slot_ids == position, 1.0, 0.0)
     filled = jnp.sum(pick, axis=1, keepdims=True)
     rows = jnp.dot(pick.astype(BF16), tokens_ref[...], preferred_element_type=F32)
+    pick_ref[...] = pick.astype(BF16)
+    raw_ref[...] = rows.astype(BF16)
     first = lax.broadcasted_iota(jnp.int32, (capacity, width), 1) == 0
     for block, out_ref in enumerate(out_refs):
         rows_of = slice(block * capacity, (block + 1) * capacity)
@@ -85,15 +87,21 @@
 
 
 def slot_rows(tokens, seq_row, modulation, bag_count, capacity):
-    width = tokens.shape[1]
-    return pl.pallas_call(
+    row_count, width = tokens.shape
+    slot_count = bag_count * capacity
+    raw, pick, *blocks = pl.pallas_call(
         functools.partial(slot_kernel, capacity),
         in_specs=[vmem(), vmem(), vmem()],
-        out_specs=[vmem()] * bag_count,
-        out_shape=[jax.ShapeDtypeStruct((capacity, width), BF16)] * bag_count,
+        out_specs=[vmem()] * (2 + bag_count),
+        out_shape=[
+            jax.ShapeDtypeStruct((slot_count, width), BF16),
+            jax.ShapeDtypeStruct((slot_count, row_count), BF16),
+        ]
+        + [jax.ShapeDtypeStruct((capacity, width), BF16)] * bag_count,
         compiler_params=limit(16),
         name="slot_rows",
     )(tokens, seq_row, modulation)
+    return raw, pick, blocks
 
 
 def weight_kernel(part, chips, w_ref, out_ref, window_ref, sem):
@@ -290,19 +298,13 @@
     return made[0], (made[1] if len(pieces) > 1 else pieces[0])
 
 
-def finish_kernel(capacity, chips, rounds, index, tokens_ref, seq_ref, mod_ref, w_out, w_fc1, w_fc2, *refs):
+def finish_kernel(capacity, chips, rounds, index, raw_ref, pick_ref, mod_ref, w_out, w_fc1, w_fc2, *refs):
     parts, earlier, out_ref, whole = refs[:chips], refs[chips:-2], refs[-2], refs[-1]
     members = rounds[index]
-    row_count, width = tokens_ref.shape
+    width = raw_ref.shape[1]
     plane, here = coordinates()
     for chip, part in enumerate(parts):
         whole[here ^ chip] = part[...]
-    position = slot_of_row(((seq_ref[...] // SEQ_BAG) ^ plane).astype(F32), capacity)
-
-    def picks(bags):
-        slot_ids = lax.broadcasted_iota(jnp.int32, (capacity, row_count), 0)
-        blocks = [jnp.where(slot_ids + bag * capacity == position, 1.0, 0.0) for bag in bags]
-        return jnp.concatenate(blocks, axis=0).astype(BF16)
 
     def per_slot(column):
         rows = [mod_ref[column, pl.ds(bag ^ plane, 1)] for bag in members]
@@ -317,7 +319,9 @@
         ],
         axis=0,
     )
-    residual = jnp.dot(picks(members), tokens_ref[...], preferred_element_type=F32)
+    residual = jnp.concatenate(
+        [raw_ref[bag * capacity : (bag + 1) * capacity] for bag in members], axis=0
+    ).astype(F32)
     branch = jnp.dot(attended, w_out[...], preferred_element_type=F32)
     hidden = (residual + per_slot(2) * branch).astype(BF16)
     normed = (layer_norm(hidden.astype(F32)) * (1.0 + per_slot(4)) + per_slot(3)).astype(BF16)
@@ -327,21 +331,24 @@
     if index < len(rounds) - 1:
         out_ref[...] = slots
         return
-    slots = jnp.concatenate([ref[...] for ref in earlier] + [slots], axis=0)
+    blocks = {}
+    for bags, value in zip(rounds, [ref[...] for ref in earlier] + [slots]):
+        for at, bag in enumerate(bags):
+            blocks[bag] = value[at * capacity : (at + 1) * capacity]
+    slots = jnp.concatenate([blocks[bag] for bag in range(len(blocks))], axis=0)
     tn = (((0,), (0,)), ((), ()))
-    pick = picks([bag for bags in rounds for bag in bags])
-    out_ref[...] = lax.dot_general(pick, slots, tn, preferred_element_type=F32).astype(BF16)
-
-
-def finish(tokens, seq_row, modulation, parts, earlier, rounds, index, w_out, w_fc1, w_fc2, capacity):
+    out_ref[...] = lax.dot_general(pick_ref[...], slots, tn, preferred_element_type=F32).astype(BF16)
+
+
+def finish(raw, pick, modulation, parts, earlier, rounds, index, w_out, w_fc1, w_fc2, capacity):
     chips, slot_count = len(parts), capacity * len(rounds[index])
     final = index == len(rounds) - 1
-    width, depth = tokens.shape[1], w_fc1.shape[1]
+    width, depth, row_count = raw.shape[1], w_fc1.shape[1], pick.shape[1]
     return pl.pallas_call(
         functools.partial(finish_kernel, capacity, chips, rounds, index),
         in_specs=[vmem()] * (6 + chips + len(earlier)),
         out_specs=vmem(),
-        out_shape=jax.ShapeDtypeStruct(tokens.shape if final else (slot_count, width), BF16),
+        out_shape=jax.ShapeDtypeStruct((row_count if final else slot_count, width), BF16),
         scratch_shapes=[pltpu.VMEM((chips,) + parts[0].shape, BF16)],
         cost_estimate=pl.CostEstimate(
             flops=2 * slot_count * width * (width + 2 * depth),
@@ -350,7 +357,12 @@
         ),
         compiler_params=limit(20),
         name="finish",
-    )(tokens, seq_row, modulation, w_out, w_fc1, w_fc2, *parts, *earlier)
+    )(raw, pick, modulation, w_out, w_fc1, w_fc2, *parts, *earlier)
+
+
+def attended_together(bags):
+    middle = list(reversed(range(1, bags - 1)))
+    return [[bags - 1]] + [middle[at : at + 2] for at in range(0, len(middle), 2)] + [[0]]
 
 
 def layer(tokens, row_seq, modulation, w_qkv, w_out, w_fc1, w_fc2):
@@ -376,7 +388,8 @@
     def in_place(value):
         return pltpu.with_memory_space_constraint(value, pltpu.HBM)
 
-    blocks = slot_rows(in_place(tokens), in_place(seq_row), in_place(modulation), bags, capacity)
+    inputs = [in_place(value) for value in (tokens, seq_row, modulation)]
+    raw, pick, blocks = slot_rows(*inputs, bags, capacity)
     weights = chip_weights(in_place(w_qkv), head_count * HD)
     blocks = [block if k == 0 else swap(block, dz=k) for k, block in enumerate(blocks)]
     half = round_up(capacity, 32) // 2
@@ -406,21 +419,20 @@
             shares.append(swap(share, dx=j // along, dy=j % along) if j else share)
         return shares
 
-    for k in reversed(range(1, bags)):
-        asked = queries[k] if k > 1 else queries[1] + queries[0]
-        part, kv = attend(asked, pieces, chips if k > 1 else 2 * chips, capacity)
+    for members in attended_together(bags):
+        asked = [query for k in members for query in queries[k]]
+        part, kv = attend(asked, pieces, chips * len(members), capacity)
         pieces = [kv]
-        part = [part[j] for j in range(part.shape[0])]
-        if k == 1:
-            mixed[0] = part[chips:]
-        away = swap(jnp.stack(part[:chips]), dz=k)
-        mixed[k] = [away[j] for j in range(chips)]
+        for at, k in enumerate(members):
+            share = part[at * chips : (at + 1) * chips]
+            share = swap(share, dz=k) if k else share
+            mixed[k] = [share[j] for j in range(chips)]
     shares = [exchange(index) for index in range(len(rounds))]
     done = []
     for index in range(len(rounds)):
         done.append(
             finish(
-                tokens, seq_row, modulation, shares[index], done, rounds, index, w_out, w_fc1, w_fc2, capacity
+                raw, pick, modulation, shares[index], done, rounds, index, w_out, w_fc1, w_fc2, capacity
             )
         )
     return done[-1]

time: 105 us -> 109 us (1.038)
  waiting for transfers between devices: 27.5 us -> 30.9 us
    ppermute x33, waiting for transfers between devices: 27.5 us -> 30.9 us  [swap(): return lax.ppermute(value, AXES, pairs)]
  transfers between devices with their start and end apart: 33 -> 33, of which waited for: 10 -> 12; matrix products, arithmetic and copies ran while one was open for 0% -> 0% of each run, Pallas kernels for 10% -> 10%
where the time goes in v8:
time: 109 us
  starting transfers between devices  40.4 us (37%)
  Pallas kernels  36.6 us (34%)
  waiting for transfers between devices  30.9 us (28%)
    ppermute x33, starting transfers between devices, swap(): return lax.ppermute(value, AXES, pairs)  40.4 us
    ppermute x33, waiting for transfers between devices, swap(): return lax.ppermute(value, AXES, pairs)  30.9 us
    pallas_call x3, Pallas kernels, attend(): pl.pallas_call(functools.partial(attend_kernel, chips, capacity, len(quer...  19.6 us
    pallas_call x2, Pallas kernels, finish(): pl.pallas_call(functools.partial(finish_kernel, capacity, chips, rounds,...  7.63 us
    pallas_call x5, Pallas kernels, project(): pl.pallas_call(functools.partial(project_kernel, head_count), in_specs=[v...  4.96 us
    pallas_call x1, Pallas kernels, chip_weights(): pl.pallas_call(functools.partial(weight_kernel, part, total // 3 // part)...  2.46 us
  transfers between devices with their start and end apart: 33, of which 12 were waited for; matrix products, arithmetic and copies ran while one was open for 0% of the time, Pallas kernels for 10%

profile of v8, /device:TPU:0, one launch (start us, length us, event | category | flops | bytes accessed | tf_op | source)
XLA Modules:
  0.0 108.5 jit_solution(9427559053309906473)
XLA Ops:
  0.0 2.0 %slot_rows.1 = (bf16[320,1152]{1,0:T(8,128)(2,1)S(1)}, bf16[320,256]{1,0:T(8,128)(2,1)S(1)}, bf16[80,1152]{1,0:T(8,128)(2,1)S(1)}, bf16[80,1152]{1,0:T(8,128)(2,...) custom-call(bf16[256,1152]{1,0:T(8,128)(2,1)} %tokens_ref.1, s32[1,256]{1,0:T(1,128)} %bitcast.9, ...), custom_call_target="tpu_custom_call" | custom-call | tf_op jit(solution)/shard_map/slot_rows/pallas_call | solution.py:92
  2.0 3.1 %collective-permute-start.5 = (bf16[80,1152]{1,0:T(8,128)(2,1)S(1)}, bf16[80,1152]{1,0:T(8,128)(2,1)S(1)}, u32[]{:S(2)}, u32[]{:S(2)}) collective-permute-start(bf16[80,1152]{1,0:T(8,128)(2,1)S(1)} %get-tuple-element.27), channel_id=1, source_target_pairs={{0,2},{1,3},{2,0},{3,1},{4,6},{5,7},{6,4},{7,5},{8,10},{9,11},{10,... | collective-permute-start | bytes 552968 | tf_op jit(solution)/shard_map/ppermute | solution.py:383
  5.1 2.6 %collective-permute-start = (bf16[80,1152]{1,0:T(8,128)(2,1)S(1)}, bf16[80,1152]{1,0:T(8,128)(2,1)S(1)}, u32[]{:S(2)}, u32[]{:S(2)}) collective-permute-start(bf16[80,1152]{1,0:T(8,128)(2,1)S(1)} %get-tuple-element.25), channel_id=1, source_target_pairs={{0,4},{1,5},{2,6},{3,7},{4,0},{5,1},{6,2},{7,3},{8,12},{9,13},{10,... | collective-permute-start | bytes 552968 | tf_op jit(solution)/shard_map/ppermute | solution.py:383
  9.2 1.5 %collective-permute-start.15 = (bf16[80,1152]{1,0:T(8,128)(2,1)S(1)}, bf16[80,1152]{1,0:T(8,128)(2,1)S(1)}, u32[]{:S(2)}, u32[]{:S(2)}) collective-permute-start(bf16[80,1152]{1,0:T(8,128)(2,1)S(1)} %get-tuple-element.32.refs_0_), channel_id=1, source_target_pairs={{0,1},{1,0},{2,3},{3,2},{4,5},{5,4},{6,7},{7,6},{8,9},{9,8},{10,11... | collective-permute-start | bytes 552968 | tf_op jit(solution)/shard_map/ppermute | solution.py:383
  10.7 2.9 %collective-permute-done.5.refs_0_ = bf16[80,1152]{1,0:T(8,128)(2,1)S(1)} collective-permute-done((bf16[80,1152]{1,0:T(8,128)(2,1)S(1)}, bf16[80,1152]{1,0:T(8,128)(2,1)S(1)}, u32[]{:S(2)}, u32[]{:S(2)}) %collective-permute-start.5) | collective-permute-done | bytes 184352 | tf_op jit(solution)/shard_map/ppermute | solution.py:383
  13.6 1.6 %collective-permute-start.7 = (bf16[80,1152]{1,0:T(8,128)(2,1)S(1)}, bf16[80,1152]{1,0:T(8,128)(2,1)S(1)}, u32[]{:S(2)}, u32[]{:S(2)}) collective-permute-start(bf16[80,1152]{1,0:T(8,128)(2,1)S(1)} %collective-permute-done.5.refs_0_), channel_id=1, source_target_pairs={{0,16},{1,17},{2,18},{3,19},{4,20},{5,21},{6,22},{7,23},{8,24},{9,... | collective-permute-start | bytes 552968 | tf_op jit(solution)/shard_map/ppermute | solution.py:383
  15.3 1.5 %collective-permute-start.6 = (bf16[80,1152]{1,0:T(8,128)(2,1)S(1)}, bf16[80,1152]{1,0:T(8,128)(2,1)S(1)}, u32[]{:S(2)}, u32[]{:S(2)}) collective-permute-start(bf16[80,1152]{1,0:T(8,128)(2,1)S(1)} %collective-permute-done.5.refs_0_), channel_id=1, source_target_pairs={{0,1},{1,0},{2,3},{3,2},{4,5},{5,4},{6,7},{7,6},{8,9},{9,8},{10,11... | collective-permute-start | bytes 552968 | tf_op jit(solution)/shard_map/ppermute | solution.py:383
  16.8 2.5 %collective-permute-start.10 = (bf16[80,1152]{1,0:T(8,128)(2,1)S(1)}, bf16[80,1152]{1,0:T(8,128)(2,1)S(1)}, u32[]{:S(2)}, u32[]{:S(2)}) collective-permute-start(bf16[80,1152]{1,0:T(8,128)(2,1)S(1)} %get-tuple-element.29), channel_id=1, source_target_pairs={{0,6},{1,7},{2,4},{3,5},{4,2},{5,3},{6,0},{7,1},{8,14},{9,15},{10,... | collective-permute-start | bytes 552968 | tf_op jit(solution)/shard_map/ppermute | solution.py:383
  20.1 1.5 %collective-permute-start.1 = (bf16[80,1152]{1,0:T(8,128)(2,1)S(1)}, bf16[80,1152]{1,0:T(8,128)(2,1)S(1)}, u32[]{:S(2)}, u32[]{:S(2)}) collective-permute-start(bf16[80,1152]{1,0:T(8,128)(2,1)S(1)} %collective-permute-done.refs_0_), channel_id=1, source_target_pairs={{0,1},{1,0},{2,3},{3,2},{4,5},{5,4},{6,7},{7,6},{8,9},{9,8},{10,11... | collective-permute-start | bytes 552968 | tf_op jit(solution)/shard_map/ppermute | solution.py:383
  25.2 1.8 %collective-permute-start.9 = (bf16[32,1152]{1,0:T(8,128)(2,1)S(1)}, bf16[32,1152]{1,0:T(8,128)(2,1)S(1)}, u32[]{:S(2)}, u32[]{:S(2)}) collective-permute-start(bf16[32,1152]{1,0:T(8,128)(2,1)S(1)} %slice.107), channel_id=1, source_target_pairs={{0,16},{1,17},{2,18},{3,19},{4,20},{5,21},{6,22},{7,23},{8,24},{9,... | collective-permute-start | bytes 221192 | tf_op jit(solution)/shard_map/ppermute | solution.py:383
  27.0 2.5 %chip_weights.1.refs_5_.refs_3_.refs_2_ = bf16[1152,896]{1,0:T(8,128)(2,1)S(1)} custom-call(bf16[1152,3456]{1,0:T(8,128)(2,1)} %w_ref.1), custom_call_target="tpu_custom_call" | custom-call | flops 1000000000 | bytes 10000000 | tf_op jit(solution)/shard_map/chip_weights/pallas_call | solution.py:139
  41.1 3.7 %collective-permute-done.14.refs_1_ = bf16[32,1152]{1,0:T(8,128)(2,1)S(1)} collective-permute-done((bf16[32,1152]{1,0:T(8,128)(2,1)S(1)}, bf16[32,1152]{1,0:T(8,128)(2,1)S(1)}, u32[]{:S(2)}, u32[]{:S(2)}) %collective-permute-start.14) | collective-permute-done | bytes 73760 | tf_op jit(solution)/shard_map/ppermute | solution.py:383
  46.2 3.3 %collective-permute-done.13.refs_0_ = bf16[48,1152]{1,0:T(8,128)(2,1)S(1)} collective-permute-done((bf16[48,1152]{1,0:T(8,128)(2,1)S(1)}, bf16[48,1152]{1,0:T(8,128)(2,1)S(1)}, u32[]{:S(2)}, u32[]{:S(2)}) %collective-permute-start.13) | collective-permute-done | bytes 110624 | tf_op jit(solution)/shard_map/ppermute | solution.py:383
  51.6 5.1 %attend.3 = (bf16[4,192,128]{2,1,0:T(8,128)(2,1)S(1)}, bf16[2,4,2560,128]{3,2,1,0:T(8,128)(2,1)S(1)}) custom-call(bf16[4,240,128]{2,1,0:T(8,128)(2,1)S(1)} %get-tuple-element.30.refs_0_, bf16[4,80,128]{2,1,0:T(8,128)(2,1)S(1)} %get-tuple-element.31.refs_1_, bf16[2,4,320,128]{3,2,1,0:T(8,128)(2,1)S(1)} %get-tuple-element.33.refs_2_, ...), custom_call_target="tpu_custom_call" | custom-call | flops 1677721600 | bytes 5242880 | tf_op jit(solution)/shard_map/attend/pallas_call | solution.py:285
  56.7 5.2 %attend.5 = bf16[4,192,128]{2,1,0:T(8,128)(2,1)S(1)} custom-call(bf16[4,320,128]{2,1,0:T(8,128)(2,1)S(1)} %get-tuple-element.40.refs_0_, bf16[2,4,2560,128]{3,2,1,0:T(8,128)(2,1)S(1)} %get-tuple-element.38.refs_2_.refs_1_), custom_call_target="tpu_custom_call" | custom-call | flops 1677721600 | bytes 5242880 | tf_op jit(solution)/shard_map/attend/pallas_call | solution.py:285
  61.9 9.3 %attend.4 = bf16[8,192,128]{2,1,0:T(8,128)(2,1)S(1)} custom-call(bf16[4,320,128]{2,1,0:T(8,128)(2,1)S(1)} %get-tuple-element.26.refs_0_, bf16[4,320,128]{2,1,0:T(8,128)(2,1)S(1)} %get-tuple-element.28.refs_1_, bf16[2,4,2560,128]{3,2,1,0:T(8,128)(2,1)S(1)} %get-tuple-element.38.refs_2_.refs_1_), custom_call_target="tpu_custom_call" | custom-call | flops 3355443200 | bytes 5242880 | tf_op jit(solution)/shard_map/attend/pallas_call | solution.py:285
  71.3 2.0 %collective-permute-start.24 = (bf16[4,192,128]{2,1,0:T(8,128)(2,1)S(1)}, bf16[4,192,128]{2,1,0:T(8,128)(2,1)S(1)}, u32[]{:S(2)}, u32[]{:S(2)}) collective-permute-start(bf16[4,192,128]{2,1,0:T(8,128)(2,1)S(1)} %get-tuple-element.41), channel_id=1, source_target_pairs={{0,2},{1,3},{2,0},{3,1},{4,6},{5,7},{6,4},{7,5},{8,10},{9,11},{10,... | collective-permute-start | bytes 589832 | tf_op jit(solution)/shard_map/ppermute | solution.py:383
  73.9 1.8 %collective-permute-start.29 = (bf16[4,192,128]{2,1,0:T(8,128)(2,1)S(1)}, bf16[4,192,128]{2,1,0:T(8,128)(2,1)S(1)}, u32[]{:S(2)}, u32[]{:S(2)}) collective-permute-start(bf16[4,192,128]{2,1,0:T(8,128)(2,1)S(1)} %get-tuple-element.39), channel_id=1, source_target_pairs={{0,6},{1,7},{2,4},{3,5},{4,2},{5,3},{6,0},{7,1},{8,14},{9,15},{10,... | collective-permute-start | bytes 589832 | tf_op jit(solution)/shard_map/ppermute | solution.py:383
  75.7 5.8 %collective-permute-done.24 = bf16[4,192,128]{2,1,0:T(8,128)(2,1)S(1)} collective-permute-done((bf16[4,192,128]{2,1,0:T(8,128)(2,1)S(1)}, bf16[4,192,128]{2,1,0:T(8,128)(2,1)S(1)}, u32[]{:S(2)}, u32[]{:S(2)}) %collective-permute-start.24) | collective-permute-done | bytes 196640 | tf_op jit(solution)/shard_map/ppermute | solution.py:383
  81.5 8.8 %collective-permute-done.25 = bf16[4,192,128]{2,1,0:T(8,128)(2,1)S(1)} collective-permute-done((bf16[4,192,128]{2,1,0:T(8,128)(2,1)S(1)}, bf16[4,192,128]{2,1,0:T(8,128)(2,1)S(1)}, u32[]{:S(2)}, u32[]{:S(2)}) %collective-permute-start.25) | collective-permute-done | bytes 196640 | tf_op jit(solution)/shard_map/ppermute | solution.py:383
  94.8 1.6 %collective-permute-start.32 = (bf16[2,192,128]{2,1,0:T(8,128)(2,1)S(1)}, bf16[2,192,128]{2,1,0:T(8,128)(2,1)S(1)}, u32[]{:S(2)}, u32[]{:S(2)}) collective-permute-start(bf16[2,192,128]{2,1,0:T(8,128)(2,1)S(1)} %pad_maximum_fusion.7), channel_id=1, source_target_pairs={{0,17},{1,16},{2,19},{3,18},{4,21},{5,20},{6,23},{7,22},{8,25},{9,... | collective-permute-start | bytes 294920 | tf_op jit(solution)/shard_map/ppermute | solution.py:383
  96.4 2.1 %collective-permute-done.30.refs_1_ = bf16[2,192,128]{2,1,0:T(8,128)(2,1)S(1)} collective-permute-done((bf16[2,192,128]{2,1,0:T(8,128)(2,1)S(1)}, bf16[2,192,128]{2,1,0:T(8,128)(2,1)S(1)}, u32[]{:S(2)}, u32[]{:S(2)}) %collective-permute-start.30) | collective-permute-done | bytes 98336 | tf_op jit(solution)/shard_map/ppermute | solution.py:383
  100.5 3.2 %finish.2.refs_4_ = bf16[160,1152]{1,0:T(8,128)(2,1)S(1)} custom-call(bf16[320,1152]{1,0:T(8,128)(2,1)S(1)} %get-tuple-element.23.raw_ref, bf16[320,256]{1,0:T(8,128)(2,1)S(1)} %get-tuple-element.24.pick_ref, f32[6,4,1152]{2,1,0:T(4,128)S(1)} %bitcast.7, bf16[1152,1152]{1,0:T(8,128)(2,1)S(1)} %copy-done, bf16[1152,2304]{1,0:T(8,128)(2,1)S(1)} %bitcast.3, ...), custom_call_target="tpu_custom_call" | custom-call | flops 2123366400 | bytes 13271040 | tf_op jit(solution)/shard_map/finish/pallas_call | solution.py:347
  104.1 4.4 %finish.3 = bf16[256,1152]{1,0:T(8,128)(2,1)} custom-call(bf16[320,1152]{1,0:T(8,128)(2,1)S(1)} %get-tuple-element.23.raw_ref, bf16[320,256]{1,0:T(8,128)(2,1)S(1)} %get-tuple-element.24.pick_ref, f32[6,4,1152]{2,1,0:T(4,128)S(1)} %bitcast.8, bf16[1152,1152]{1,0:T(8,128)(2,1)S(1)} %copy-done, bf16[1152,2304]{1,0:T(8,128)(2,1)S(1)} %bitcast.3, ...), custom_call_target="tpu_custom_call" | custom-call | flops 2123366400 | bytes 13271040 | tf_op jit(solution)/shard_map/finish/pallas_call | solution.py:347
  (89 shorter events, 28.3 us)
Async XLA Ops:
  2.0 11.6 %collective-permute-start.5 = (bf16[80,1152]{1,0:T(8,128)(2,1)S(1)}, bf16[80,1152]{1,0:T(8,128)(2,1)S(1)}, u32[]{:S(2)}, u32[]{:S(2)}) collective-permute-start(bf16[80,1152]{1,0:T(8,128)(2,1)S(1)} %get-tuple-element.27), channel_id=1, source_target_pairs={{0,2},{1,3},{2,0},{3,1},{4,6},{5,7},{6,4},{7,5},{8,10},{9,11},{10,... | collective-permute-start | bytes 552968 | tf_op jit(solution)/shard_map/ppermute | solution.py:383
  5.1 11.7 %collective-permute-start = (bf16[80,1152]{1,0:T(8,128)(2,1)S(1)}, bf16[80,1152]{1,0:T(8,128)(2,1)S(1)}, u32[]{:S(2)}, u32[]{:S(2)}) collective-permute-start(bf16[80,1152]{1,0:T(8,128)(2,1)S(1)} %get-tuple-element.25), channel_id=1, source_target_pairs={{0,4},{1,5},{2,6},{3,7},{4,0},{5,1},{6,2},{7,3},{8,12},{9,13},{10,... | collective-permute-start | bytes 552968 | tf_op jit(solution)/shard_map/ppermute | solution.py:383
  7.7 11.5 %collective-permute-start.16 = (bf16[80,1152]{1,0:T(8,128)(2,1)S(1)}, bf16[80,1152]{1,0:T(8,128)(2,1)S(1)}, u32[]{:S(2)}, u32[]{:S(2)}) collective-permute-start(bf16[80,1152]{1,0:T(8,128)(2,1)S(1)} %get-tuple-element.32.refs_0_), channel_id=1, source_target_pairs={{0,16},{1,17},{2,18},{3,19},{4,20},{5,21},{6,22},{7,23},{8,24},{9,... | collective-permute-start | bytes 552968 | tf_op jit(solution)/shard_map/ppermute | solution.py:383
  9.2 10.9 %collective-permute-start.15 = (bf16[80,1152]{1,0:T(8,128)(2,1)S(1)}, bf16[80,1152]{1,0:T(8,128)(2,1)S(1)}, u32[]{:S(2)}, u32[]{:S(2)}) collective-permute-start(bf16[80,1152]{1,0:T(8,128)(2,1)S(1)} %get-tuple-element.32.refs_0_), channel_id=1, source_target_pairs={{0,1},{1,0},{2,3},{3,2},{4,5},{5,4},{6,7},{7,6},{8,9},{9,8},{10,11... | collective-permute-start | bytes 552968 | tf_op jit(solution)/shard_map/ppermute | solution.py:383
  13.6 8.0 %collective-permute-start.7 = (bf16[80,1152]{1,0:T(8,128)(2,1)S(1)}, bf16[80,1152]{1,0:T(8,128)(2,1)S(1)}, u32[]{:S(2)}, u32[]{:S(2)}) collective-permute-start(bf16[80,1152]{1,0:T(8,128)(2,1)S(1)} %collective-permute-done.5.refs_0_), channel_id=1, source_target_pairs={{0,16},{1,17},{2,18},{3,19},{4,20},{5,21},{6,22},{7,23},{8,24},{9,... | collective-permute-start | bytes 552968 | tf_op jit(solution)/shard_map/ppermute | solution.py:383
  15.3 7.0 %collective-permute-start.6 = (bf16[80,1152]{1,0:T(8,128)(2,1)S(1)}, bf16[80,1152]{1,0:T(8,128)(2,1)S(1)}, u32[]{:S(2)}, u32[]{:S(2)}) collective-permute-start(bf16[80,1152]{1,0:T(8,128)(2,1)S(1)} %collective-permute-done.5.refs_0_), channel_id=1, source_target_pairs={{0,1},{1,0},{2,3},{3,2},{4,5},{5,4},{6,7},{7,6},{8,9},{9,8},{10,11... | collective-permute-start | bytes 552968 | tf_op jit(solution)/shard_map/ppermute | solution.py:383
  16.8 7.4 %collective-permute-start.10 = (bf16[80,1152]{1,0:T(8,128)(2,1)S(1)}, bf16[80,1152]{1,0:T(8,128)(2,1)S(1)}, u32[]{:S(2)}, u32[]{:S(2)}) collective-permute-start(bf16[80,1152]{1,0:T(8,128)(2,1)S(1)} %get-tuple-element.29), channel_id=1, source_target_pairs={{0,6},{1,7},{2,4},{3,5},{4,2},{5,3},{6,0},{7,1},{8,14},{9,15},{10,... | collective-permute-start | bytes 552968 | tf_op jit(solution)/shard_map/ppermute | solution.py:383
  20.1 9.4 %collective-permute-start.1 = (bf16[80,1152]{1,0:T(8,128)(2,1)S(1)}, bf16[80,1152]{1,0:T(8,128)(2,1)S(1)}, u32[]{:S(2)}, u32[]{:S(2)}) collective-permute-start(bf16[80,1152]{1,0:T(8,128)(2,1)S(1)} %collective-permute-done.refs_0_), channel_id=1, source_target_pairs={{0,1},{1,0},{2,3},{3,2},{4,5},{5,4},{6,7},{7,6},{8,9},{9,8},{10,11... | collective-permute-start | bytes 552968 | tf_op jit(solution)/shard_map/ppermute | solution.py:383
  21.6 9.5 %collective-permute-start.17 = (bf16[48,1152]{1,0:T(8,128)(2,1)S(1)}, bf16[48,1152]{1,0:T(8,128)(2,1)S(1)}, u32[]{:S(2)}, u32[]{:S(2)}) collective-permute-start(bf16[48,1152]{1,0:T(8,128)(2,1)S(1)} %slice.110), channel_id=1, source_target_pairs={{0,1},{1,0},{2,3},{3,2},{4,5},{5,4},{6,7},{7,6},{8,9},{9,8},{10,11... | collective-permute-start | bytes 331784 | tf_op jit(solution)/shard_map/ppermute | solution.py:383
  22.3 7.6 %collective-permute-start.18 = (bf16[32,1152]{1,0:T(8,128)(2,1)S(1)}, bf16[32,1152]{1,0:T(8,128)(2,1)S(1)}, u32[]{:S(2)}, u32[]{:S(2)}) collective-permute-start(bf16[32,1152]{1,0:T(8,128)(2,1)S(1)} %slice.111), channel_id=1, source_target_pairs={{0,16},{1,17},{2,18},{3,19},{4,20},{5,21},{6,22},{7,23},{8,24},{9,... | collective-permute-start | bytes 221192 | tf_op jit(solution)/shard_map/ppermute | solution.py:383
  24.2 10.7 %collective-permute-start.8 = (bf16[48,1152]{1,0:T(8,128)(2,1)S(1)}, bf16[48,1152]{1,0:T(8,128)(2,1)S(1)}, u32[]{:S(2)}, u32[]{:S(2)}) collective-permute-start(bf16[48,1152]{1,0:T(8,128)(2,1)S(1)} %slice.106), channel_id=1, source_target_pairs={{0,1},{1,0},{2,3},{3,2},{4,5},{5,4},{6,7},{7,6},{8,9},{9,8},{10,11... | collective-permute-start | bytes 331784 | tf_op jit(solution)/shard_map/ppermute | solution.py:383
  25.2 8.2 %collective-permute-start.9 = (bf16[32,1152]{1,0:T(8,128)(2,1)S(1)}, bf16[32,1152]{1,0:T(8,128)(2,1)S(1)}, u32[]{:S(2)}, u32[]{:S(2)}) collective-permute-start(bf16[32,1152]{1,0:T(8,128)(2,1)S(1)} %slice.107), channel_id=1, source_target_pairs={{0,16},{1,17},{2,18},{3,19},{4,20},{5,21},{6,22},{7,23},{8,24},{9,... | collective-permute-start | bytes 221192 | tf_op jit(solution)/shard_map/ppermute | solution.py:383
  29.5 8.4 %collective-permute-start.12 = (bf16[80,1152]{1,0:T(8,128)(2,1)S(1)}, bf16[80,1152]{1,0:T(8,128)(2,1)S(1)}, u32[]{:S(2)}, u32[]{:S(2)}) collective-permute-start(bf16[80,1152]{1,0:T(8,128)(2,1)S(1)} %collective-permute-done.10.refs_0_), channel_id=1, source_target_pairs={{0,16},{1,17},{2,18},{3,19},{4,20},{5,21},{6,22},{7,23},{8,24},{9,... | collective-permute-start | bytes 552968 | tf_op jit(solution)/shard_map/ppermute | solution.py:383
  29.8 6.8 %collective-permute-start.3 = (bf16[48,1152]{1,0:T(8,128)(2,1)S(1)}, bf16[48,1152]{1,0:T(8,128)(2,1)S(1)}, u32[]{:S(2)}, u32[]{:S(2)}) collective-permute-start(bf16[48,1152]{1,0:T(8,128)(2,1)S(1)} %slice.104), channel_id=1, source_target_pairs={{0,1},{1,0},{2,3},{3,2},{4,5},{5,4},{6,7},{7,6},{8,9},{9,8},{10,11... | collective-permute-start | bytes 331784 | tf_op jit(solution)/shard_map/ppermute | solution.py:383
  34.9 16.7 %collective-permute-start.19 = (bf16[2,4,320,128]{3,2,1,0:T(8,128)(2,1)S(1)}, bf16[2,4,320,128]{3,2,1,0:T(8,128)(2,1)S(1)}, u32[]{:S(2)}, u32[]{:S(2)}) collective-permute-start(bf16[2,4,320,128]{3,2,1,0:T(8,128)(2,1)S(1)} %get-tuple-element.33.refs_2_), channel_id=1, source_target_pairs={{0,8},{1,9},{2,10},{3,11},{4,12},{5,13},{6,14},{7,15},{8,0},{9,1},... | collective-permute-start | bytes 1966088 | tf_op jit(solution)/shard_map/ppermute | solution.py:383
  36.0 15.5 %collective-permute-start.20 = (bf16[2,4,320,128]{3,2,1,0:T(8,128)(2,1)S(1)}, bf16[2,4,320,128]{3,2,1,0:T(8,128)(2,1)S(1)}, u32[]{:S(2)}, u32[]{:S(2)}) collective-permute-start(bf16[2,4,320,128]{3,2,1,0:T(8,128)(2,1)S(1)} %get-tuple-element.34.refs_4_), channel_id=1, source_target_pairs={{0,8},{1,9},{2,10},{3,11},{4,12},{5,13},{6,14},{7,15},{8,0},{9,1},... | collective-permute-start | bytes 1966088 | tf_op jit(solution)/shard_map/ppermute | solution.py:383
  37.8 13.8 %collective-permute-start.21 = (bf16[2,4,320,128]{3,2,1,0:T(8,128)(2,1)S(1)}, bf16[2,4,320,128]{3,2,1,0:T(8,128)(2,1)S(1)}, u32[]{:S(2)}, u32[]{:S(2)}) collective-permute-start(bf16[2,4,320,128]{3,2,1,0:T(8,128)(2,1)S(1)} %get-tuple-element.35.refs_6_), channel_id=1, source_target_pairs={{0,8},{1,9},{2,10},{3,11},{4,12},{5,13},{6,14},{7,15},{8,0},{9,1},... | collective-permute-start | bytes 1966088 | tf_op jit(solution)/shard_map/ppermute | solution.py:383
  40.0 11.6 %collective-permute-start.22 = (bf16[2,4,240,128]{3,2,1,0:T(8,128)(2,1)S(1)}, bf16[2,4,240,128]{3,2,1,0:T(8,128)(2,1)S(1)}, u32[]{:S(2)}, u32[]{:S(2)}) collective-permute-start(bf16[2,4,240,128]{3,2,1,0:T(8,128)(2,1)S(1)} %get-tuple-element.36.refs_8_), channel_id=1, source_target_pairs={{0,8},{1,9},{2,10},{3,11},{4,12},{5,13},{6,14},{7,15},{8,0},{9,1},... | collective-permute-start | bytes 1474568 | tf_op jit(solution)/shard_map/ppermute | solution.py:383
  71.3 10.2 %collective-permute-start.24 = (bf16[4,192,128]{2,1,0:T(8,128)(2,1)S(1)}, bf16[4,192,128]{2,1,0:T(8,128)(2,1)S(1)}, u32[]{:S(2)}, u32[]{:S(2)}) collective-permute-start(bf16[4,192,128]{2,1,0:T(8,128)(2,1)S(1)} %get-tuple-element.41), channel_id=1, source_target_pairs={{0,2},{1,3},{2,0},{3,1},{4,6},{5,7},{6,4},{7,5},{8,10},{9,11},{10,... | collective-permute-start | bytes 589832 | tf_op jit(solution)/shard_map/ppermute | solution.py:383
  73.2 17.1 %collective-permute-start.25 = (bf16[4,192,128]{2,1,0:T(8,128)(2,1)S(1)}, bf16[4,192,128]{2,1,0:T(8,128)(2,1)S(1)}, u32[]{:S(2)}, u32[]{:S(2)}) collective-permute-start(bf16[4,192,128]{2,1,0:T(8,128)(2,1)S(1)} %get-tuple-element.42), channel_id=1, source_target_pairs={{0,4},{1,5},{2,6},{3,7},{4,0},{5,1},{6,2},{7,3},{8,12},{9,13},{10,... | collective-permute-start | bytes 589832 | tf_op jit(solution)/shard_map/ppermute | solution.py:383
  73.9 18.7 %collective-permute-start.29 = (bf16[4,192,128]{2,1,0:T(8,128)(2,1)S(1)}, bf16[4,192,128]{2,1,0:T(8,128)(2,1)S(1)}, u32[]{:S(2)}, u32[]{:S(2)}) collective-permute-start(bf16[4,192,128]{2,1,0:T(8,128)(2,1)S(1)} %get-tuple-element.39), channel_id=1, source_target_pairs={{0,6},{1,7},{2,4},{3,5},{4,2},{5,3},{6,0},{7,1},{8,14},{9,15},{10,... | collective-permute-start | bytes 589832 | tf_op jit(solution)/shard_map/ppermute | solution.py:383
  90.4 13.4 %collective-permute-start.26 = (bf16[2,192,128]{2,1,0:T(8,128)(2,1)S(1)}, bf16[2,192,128]{2,1,0:T(8,128)(2,1)S(1)}, u32[]{:S(2)}, u32[]{:S(2)}) collective-permute-start(bf16[2,192,128]{2,1,0:T(8,128)(2,1)S(1)} %pad_maximum_fusion.1), channel_id=1, source_target_pairs={{0,1},{1,0},{2,3},{3,2},{4,5},{5,4},{6,7},{7,6},{8,9},{9,8},{10,11... | collective-permute-start | bytes 294920 | tf_op jit(solution)/shard_map/ppermute | solution.py:383
  91.7 12.1 %collective-permute-start.27 = (bf16[2,192,128]{2,1,0:T(8,128)(2,1)S(1)}, bf16[2,192,128]{2,1,0:T(8,128)(2,1)S(1)}, u32[]{:S(2)}, u32[]{:S(2)}) collective-permute-start(bf16[2,192,128]{2,1,0:T(8,128)(2,1)S(1)} %pad_maximum_fusion.2), channel_id=1, source_target_pairs={{0,16},{1,17},{2,18},{3,19},{4,20},{5,21},{6,22},{7,23},{8,24},{9,... | collective-permute-start | bytes 294920 | tf_op jit(solution)/shard_map/ppermute | solution.py:383
  93.7 6.1 %collective-permute-start.31 = (bf16[2,192,128]{2,1,0:T(8,128)(2,1)S(1)}, bf16[2,192,128]{2,1,0:T(8,128)(2,1)S(1)}, u32[]{:S(2)}, u32[]{:S(2)}) collective-permute-start(bf16[2,192,128]{2,1,0:T(8,128)(2,1)S(1)} %pad_maximum_fusion.6), channel_id=1, source_target_pairs={{0,16},{1,17},{2,18},{3,19},{4,20},{5,21},{6,22},{7,23},{8,24},{9,... | collective-permute-start | bytes 294920 | tf_op jit(solution)/shard_map/ppermute | solution.py:383
  (15 other events, 276.2 us)

commit v9 on v8

--- a/solution.py
+++ b/solution.py
@@ -392,10 +392,11 @@
     raw, pick, blocks = slot_rows(*inputs, bags, capacity)
     weights = chip_weights(in_place(w_qkv), head_count * HD)
     blocks = [block if k == 0 else swap(block, dz=k) for k, block in enumerate(blocks)]
-    half = round_up(capacity, 32) // 2
+    halves = round_up(capacity, 32) // 2, capacity - round_up(capacity, 32) // 2
     queries, pieces = [], []
     for k, block in enumerate(blocks):
         if across == 2 and along == 2:
+            half = halves[k % 2]
             from_x, from_y = swap(block, dx=1), swap(block, dy=1)
             upper, lower = swap(from_x[:half], dy=1), swap(from_y[half:], dx=1)
             parts = [block, from_y, from_x, upper, lower]
@@ -413,11 +414,11 @@
     rounds = [[bags - 1, 0], list(range(1, bags - 1))] if bags > 2 else [list(range(bags))]
 
     def exchange(index):
-        shares = []
-        for j in range(chips):
+        shares = {}
+        for j in reversed(range(chips)):
             share = jnp.stack([mixed[k][j] for k in rounds[index]])
-            shares.append(swap(share, dx=j // along, dy=j % along) if j else share)
-        return shares
+            shares[j] = swap(share, dx=j // along, dy=j % along) if j else share
+        return [shares[j] for j in range(chips)]
 
     for members in attended_together(bags):
         asked = [query for k in members for query in queries[k]]
@@ -440,6 +441,4 @@
 
 def solution(mesh):
     placed = (P(("bag", "sp"), None), P(("bag", "sp")), P(), P(), P(), P(), P())
-    return jax.shard_map(
-        layer, mesh=mesh, in_specs=placed, out_specs=P(("bag", "sp"), None), check_vma=False
-    )
+    return jax.shard_map(layer, mesh=mesh, in_specs=placed, out_specs=P(("bag", "sp"), None), check_vma=False)

time: 109 us -> 109 us (level)
  no operation moved by 1% of the time
where the time goes in v9:
time: 109 us; the launch traced here: 108 us
  starting transfers between devices  40.8 us (37%)
  Pallas kernels  36.7 us (34%)
  waiting for transfers between devices  30.4 us (28%)
    ppermute x33, starting transfers between devices, swap(): return lax.ppermute(value, AXES, pairs)  40.8 us
    ppermute x33, waiting for transfers between devices, swap(): return lax.ppermute(value, AXES, pairs)  30.4 us
    pallas_call x3, Pallas kernels, attend(): pl.pallas_call(functools.partial(attend_kernel, chips, capacity, len(quer...  19.6 us
    pallas_call x2, Pallas kernels, finish(): pl.pallas_call(functools.partial(finish_kernel, capacity, chips, rounds,...  7.65 us
    pallas_call x5, Pallas kernels, project(): pl.pallas_call(functools.partial(project_kernel, head_count), in_specs=[v...  4.95 us
    pallas_call x1, Pallas kernels, chip_weights(): pl.pallas_call(functools.partial(weight_kernel, part, total // 3 // part)...  2.46 us
  transfers between devices with their start and end apart: 33, of which 12 were waited for; matrix products, arithmetic and copies ran while one was open for 0% of the time, Pallas kernels for 10%

profile of v9, /device:TPU:0, one launch (start us, length us, event | category | flops | bytes accessed | tf_op | source)
XLA Modules:
  0.0 108.5 jit_solution(9813920630042086036)
XLA Ops:
  0.0 2.0 %slot_rows.1 = (bf16[320,1152]{1,0:T(8,128)(2,1)S(1)}, bf16[320,256]{1,0:T(8,128)(2,1)S(1)}, bf16[80,1152]{1,0:T(8,128)(2,1)S(1)}, bf16[80,1152]{1,0:T(8,128)(2,...) custom-call(bf16[256,1152]{1,0:T(8,128)(2,1)} %tokens_ref.1, s32[1,256]{1,0:T(1,128)} %bitcast.9, ...), custom_call_target="tpu_custom_call" | custom-call | tf_op jit(solution)/shard_map/slot_rows/pallas_call | solution.py:92
  2.0 3.1 %collective-permute-start.5 = (bf16[80,1152]{1,0:T(8,128)(2,1)S(1)}, bf16[80,1152]{1,0:T(8,128)(2,1)S(1)}, u32[]{:S(2)}, u32[]{:S(2)}) collective-permute-start(bf16[80,1152]{1,0:T(8,128)(2,1)S(1)} %get-tuple-element.27), channel_id=1, source_target_pairs={{0,2},{1,3},{2,0},{3,1},{4,6},{5,7},{6,4},{7,5},{8,10},{9,11},{10,... | collective-permute-start | bytes 552968 | tf_op jit(solution)/shard_map/ppermute | solution.py:383
  5.1 2.6 %collective-permute-start = (bf16[80,1152]{1,0:T(8,128)(2,1)S(1)}, bf16[80,1152]{1,0:T(8,128)(2,1)S(1)}, u32[]{:S(2)}, u32[]{:S(2)}) collective-permute-start(bf16[80,1152]{1,0:T(8,128)(2,1)S(1)} %get-tuple-element.25), channel_id=1, source_target_pairs={{0,4},{1,5},{2,6},{3,7},{4,0},{5,1},{6,2},{7,3},{8,12},{9,13},{10,... | collective-permute-start | bytes 552968 | tf_op jit(solution)/shard_map/ppermute | solution.py:383
  10.7 2.9 %collective-permute-done.5.refs_0_ = bf16[80,1152]{1,0:T(8,128)(2,1)S(1)} collective-permute-done((bf16[80,1152]{1,0:T(8,128)(2,1)S(1)}, bf16[80,1152]{1,0:T(8,128)(2,1)S(1)}, u32[]{:S(2)}, u32[]{:S(2)}) %collective-permute-start.5) | collective-permute-done | bytes 184352 | tf_op jit(solution)/shard_map/ppermute | solution.py:383
  13.6 1.6 %collective-permute-start.7 = (bf16[80,1152]{1,0:T(8,128)(2,1)S(1)}, bf16[80,1152]{1,0:T(8,128)(2,1)S(1)}, u32[]{:S(2)}, u32[]{:S(2)}) collective-permute-start(bf16[80,1152]{1,0:T(8,128)(2,1)S(1)} %collective-permute-done.5.refs_0_), channel_id=1, source_target_pairs={{0,16},{1,17},{2,18},{3,19},{4,20},{5,21},{6,22},{7,23},{8,24},{9,... | collective-permute-start | bytes 552968 | tf_op jit(solution)/shard_map/ppermute | solution.py:383
  15.3 1.5 %collective-permute-start.6 = (bf16[80,1152]{1,0:T(8,128)(2,1)S(1)}, bf16[80,1152]{1,0:T(8,128)(2,1)S(1)}, u32[]{:S(2)}, u32[]{:S(2)}) collective-permute-start(bf16[80,1152]{1,0:T(8,128)(2,1)S(1)} %collective-permute-done.5.refs_0_), channel_id=1, source_target_pairs={{0,1},{1,0},{2,3},{3,2},{4,5},{5,4},{6,7},{7,6},{8,9},{9,8},{10,11... | collective-permute-start | bytes 552968 | tf_op jit(solution)/shard_map/ppermute | solution.py:383
  16.8 2.5 %collective-permute-start.10 = (bf16[80,1152]{1,0:T(8,128)(2,1)S(1)}, bf16[80,1152]{1,0:T(8,128)(2,1)S(1)}, u32[]{:S(2)}, u32[]{:S(2)}) collective-permute-start(bf16[80,1152]{1,0:T(8,128)(2,1)S(1)} %get-tuple-element.29), channel_id=1, source_target_pairs={{0,6},{1,7},{2,4},{3,5},{4,2},{5,3},{6,0},{7,1},{8,14},{9,15},{10,... | collective-permute-start | bytes 552968 | tf_op jit(solution)/shard_map/ppermute | solution.py:383
  25.2 1.9 %collective-permute-start.9 = (bf16[48,1152]{1,0:T(8,128)(2,1)S(1)}, bf16[48,1152]{1,0:T(8,128)(2,1)S(1)}, u32[]{:S(2)}, u32[]{:S(2)}) collective-permute-start(bf16[48,1152]{1,0:T(8,128)(2,1)S(1)} %slice.107), channel_id=1, source_target_pairs={{0,16},{1,17},{2,18},{3,19},{4,20},{5,21},{6,22},{7,23},{8,24},{9,... | collective-permute-start | bytes 331784 | tf_op jit(solution)/shard_map/ppermute | solution.py:383
  27.2 2.5 %chip_weights.1.refs_5_.refs_3_.refs_2_ = bf16[1152,896]{1,0:T(8,128)(2,1)S(1)} custom-call(bf16[1152,3456]{1,0:T(8,128)(2,1)} %w_ref.1), custom_call_target="tpu_custom_call" | custom-call | flops 1000000000 | bytes 10000000 | tf_op jit(solution)/shard_map/chip_weights/pallas_call | solution.py:139
  33.4 1.7 %collective-permute-start.11 = (bf16[80,1152]{1,0:T(8,128)(2,1)S(1)}, bf16[80,1152]{1,0:T(8,128)(2,1)S(1)}, u32[]{:S(2)}, u32[]{:S(2)}) collective-permute-start(bf16[80,1152]{1,0:T(8,128)(2,1)S(1)} %collective-permute-done.10.refs_0_), channel_id=1, source_target_pairs={{0,1},{1,0},{2,3},{3,2},{4,5},{5,4},{6,7},{7,6},{8,9},{9,8},{10,11... | collective-permute-start | bytes 552968 | tf_op jit(solution)/shard_map/ppermute | solution.py:383
  40.1 1.7 %collective-permute-start.13 = (bf16[32,1152]{1,0:T(8,128)(2,1)S(1)}, bf16[32,1152]{1,0:T(8,128)(2,1)S(1)}, u32[]{:S(2)}, u32[]{:S(2)}) collective-permute-start(bf16[32,1152]{1,0:T(8,128)(2,1)S(1)} %slice.108), channel_id=1, source_target_pairs={{0,1},{1,0},{2,3},{3,2},{4,5},{5,4},{6,7},{7,6},{8,9},{9,8},{10,11... | collective-permute-start | bytes 221192 | tf_op jit(solution)/shard_map/ppermute | solution.py:383
  41.8 3.0 %collective-permute-done.13.refs_0_ = bf16[32,1152]{1,0:T(8,128)(2,1)S(1)} collective-permute-done((bf16[32,1152]{1,0:T(8,128)(2,1)S(1)}, bf16[32,1152]{1,0:T(8,128)(2,1)S(1)}, u32[]{:S(2)}, u32[]{:S(2)}) %collective-permute-start.13) | collective-permute-done | bytes 73760 | tf_op jit(solution)/shard_map/ppermute | solution.py:383
  45.7 3.8 %collective-permute-done.14.refs_1_ = bf16[48,1152]{1,0:T(8,128)(2,1)S(1)} collective-permute-done((bf16[48,1152]{1,0:T(8,128)(2,1)S(1)}, bf16[48,1152]{1,0:T(8,128)(2,1)S(1)}, u32[]{:S(2)}, u32[]{:S(2)}) %collective-permute-start.14) | collective-permute-done | bytes 110624 | tf_op jit(solution)/shard_map/ppermute | solution.py:383
  51.6 5.1 %attend.3 = (bf16[4,192,128]{2,1,0:T(8,128)(2,1)S(1)}, bf16[2,4,2560,128]{3,2,1,0:T(8,128)(2,1)S(1)}) custom-call(bf16[4,240,128]{2,1,0:T(8,128)(2,1)S(1)} %get-tuple-element.30.refs_0_, bf16[4,80,128]{2,1,0:T(8,128)(2,1)S(1)} %get-tuple-element.31.refs_1_, bf16[2,4,320,128]{3,2,1,0:T(8,128)(2,1)S(1)} %get-tuple-element.33.refs_2_, ...), custom_call_target="tpu_custom_call" | custom-call | flops 1677721600 | bytes 5242880 | tf_op jit(solution)/shard_map/attend/pallas_call | solution.py:285
  56.7 5.2 %attend.5 = bf16[4,192,128]{2,1,0:T(8,128)(2,1)S(1)} custom-call(bf16[4,320,128]{2,1,0:T(8,128)(2,1)S(1)} %get-tuple-element.40.refs_0_, bf16[2,4,2560,128]{3,2,1,0:T(8,128)(2,1)S(1)} %get-tuple-element.38.refs_2_.refs_1_), custom_call_target="tpu_custom_call" | custom-call | flops 1677721600 | bytes 5242880 | tf_op jit(solution)/shard_map/attend/pallas_call | solution.py:285
  61.9 9.3 %attend.4 = bf16[8,192,128]{2,1,0:T(8,128)(2,1)S(1)} custom-call(bf16[4,320,128]{2,1,0:T(8,128)(2,1)S(1)} %get-tuple-element.26.refs_0_, bf16[4,320,128]{2,1,0:T(8,128)(2,1)S(1)} %get-tuple-element.28.refs_1_, bf16[2,4,2560,128]{3,2,1,0:T(8,128)(2,1)S(1)} %get-tuple-element.38.refs_2_.refs_1_), custom_call_target="tpu_custom_call" | custom-call | flops 3355443200 | bytes 5242880 | tf_op jit(solution)/shard_map/attend/pallas_call | solution.py:285
  71.3 2.0 %collective-permute-start.24 = (bf16[4,192,128]{2,1,0:T(8,128)(2,1)S(1)}, bf16[4,192,128]{2,1,0:T(8,128)(2,1)S(1)}, u32[]{:S(2)}, u32[]{:S(2)}) collective-permute-start(bf16[4,192,128]{2,1,0:T(8,128)(2,1)S(1)} %get-tuple-element.41), channel_id=1, source_target_pairs={{0,2},{1,3},{2,0},{3,1},{4,6},{5,7},{6,4},{7,5},{8,10},{9,11},{10,... | collective-permute-start | bytes 589832 | tf_op jit(solution)/shard_map/ppermute | solution.py:383
  73.9 1.8 %collective-permute-start.29 = (bf16[4,192,128]{2,1,0:T(8,128)(2,1)S(1)}, bf16[4,192,128]{2,1,0:T(8,128)(2,1)S(1)}, u32[]{:S(2)}, u32[]{:S(2)}) collective-permute-start(bf16[4,192,128]{2,1,0:T(8,128)(2,1)S(1)} %get-tuple-element.39), channel_id=1, source_target_pairs={{0,6},{1,7},{2,4},{3,5},{4,2},{5,3},{6,0},{7,1},{8,14},{9,15},{10,... | collective-permute-start | bytes 589832 | tf_op jit(solution)/shard_map/ppermute | solution.py:383
  75.7 5.8 %collective-permute-done.24 = bf16[4,192,128]{2,1,0:T(8,128)(2,1)S(1)} collective-permute-done((bf16[4,192,128]{2,1,0:T(8,128)(2,1)S(1)}, bf16[4,192,128]{2,1,0:T(8,128)(2,1)S(1)}, u32[]{:S(2)}, u32[]{:S(2)}) %collective-permute-start.24) | collective-permute-done | bytes 196640 | tf_op jit(solution)/shard_map/ppermute | solution.py:383
  81.5 8.8 %collective-permute-done.25 = bf16[4,192,128]{2,1,0:T(8,128)(2,1)S(1)} collective-permute-done((bf16[4,192,128]{2,1,0:T(8,128)(2,1)S(1)}, bf16[4,192,128]{2,1,0:T(8,128)(2,1)S(1)}, u32[]{:S(2)}, u32[]{:S(2)}) %collective-permute-start.25) | collective-permute-done | bytes 196640 | tf_op jit(solution)/shard_map/ppermute | solution.py:383
  94.8 1.6 %collective-permute-start.32 = (bf16[2,192,128]{2,1,0:T(8,128)(2,1)S(1)}, bf16[2,192,128]{2,1,0:T(8,128)(2,1)S(1)}, u32[]{:S(2)}, u32[]{:S(2)}) collective-permute-start(bf16[2,192,128]{2,1,0:T(8,128)(2,1)S(1)} %pad_maximum_fusion.7), channel_id=1, source_target_pairs={{0,17},{1,16},{2,19},{3,18},{4,21},{5,20},{6,23},{7,22},{8,25},{9,... | collective-permute-start | bytes 294920 | tf_op jit(solution)/shard_map/ppermute | solution.py:383
  96.4 2.1 %collective-permute-done.30.refs_1_ = bf16[2,192,128]{2,1,0:T(8,128)(2,1)S(1)} collective-permute-done((bf16[2,192,128]{2,1,0:T(8,128)(2,1)S(1)}, bf16[2,192,128]{2,1,0:T(8,128)(2,1)S(1)}, u32[]{:S(2)}, u32[]{:S(2)}) %collective-permute-start.30) | collective-permute-done | bytes 98336 | tf_op jit(solution)/shard_map/ppermute | solution.py:383
  100.5 3.2 %finish.2.refs_4_ = bf16[160,1152]{1,0:T(8,128)(2,1)S(1)} custom-call(bf16[320,1152]{1,0:T(8,128)(2,1)S(1)} %get-tuple-element.23.raw_ref, bf16[320,256]{1,0:T(8,128)(2,1)S(1)} %get-tuple-element.24.pick_ref, f32[6,4,1152]{2,1,0:T(4,128)S(1)} %bitcast.7, bf16[1152,1152]{1,0:T(8,128)(2,1)S(1)} %copy-done, bf16[1152,2304]{1,0:T(8,128)(2,1)S(1)} %bitcast.3, ...), custom_call_target="tpu_custom_call" | custom-call | flops 2123366400 | bytes 13271040 | tf_op jit(solution)/shard_map/finish/pallas_call | solution.py:347
  104.1 4.4 %finish.3 = bf16[256,1152]{1,0:T(8,128)(2,1)} custom-call(bf16[320,1152]{1,0:T(8,128)(2,1)S(1)} %get-tuple-element.23.raw_ref, bf16[320,256]{1,0:T(8,128)(2,1)S(1)} %get-tuple-element.24.pick_ref, f32[6,4,1152]{2,1,0:T(4,128)S(1)} %bitcast.8, bf16[1152,1152]{1,0:T(8,128)(2,1)S(1)} %copy-done, bf16[1152,2304]{1,0:T(8,128)(2,1)S(1)} %bitcast.3, ...), custom_call_target="tpu_custom_call" | custom-call | flops 2123366400 | bytes 13271040 | tf_op jit(solution)/shard_map/finish/pallas_call | solution.py:347
  (89 shorter events, 28.0 us)
Async XLA Ops:
  2.0 11.6 %collective-permute-start.5 = (bf16[80,1152]{1,0:T(8,128)(2,1)S(1)}, bf16[80,1152]{1,0:T(8,128)(2,1)S(1)}, u32[]{:S(2)}, u32[]{:S(2)}) collective-permute-start(bf16[80,1152]{1,0:T(8,128)(2,1)S(1)} %get-tuple-element.27), channel_id=1, source_target_pairs={{0,2},{1,3},{2,0},{3,1},{4,6},{5,7},{6,4},{7,5},{8,10},{9,11},{10,... | collective-permute-start | bytes 552968 | tf_op jit(solution)/shard_map/ppermute | solution.py:383
  5.1 11.7 %collective-permute-start = (bf16[80,1152]{1,0:T(8,128)(2,1)S(1)}, bf16[80,1152]{1,0:T(8,128)(2,1)S(1)}, u32[]{:S(2)}, u32[]{:S(2)}) collective-permute-start(bf16[80,1152]{1,0:T(8,128)(2,1)S(1)} %get-tuple-element.25), channel_id=1, source_target_pairs={{0,4},{1,5},{2,6},{3,7},{4,0},{5,1},{6,2},{7,3},{8,12},{9,13},{10,... | collective-permute-start | bytes 552968 | tf_op jit(solution)/shard_map/ppermute | solution.py:383
  7.7 11.5 %collective-permute-start.16 = (bf16[80,1152]{1,0:T(8,128)(2,1)S(1)}, bf16[80,1152]{1,0:T(8,128)(2,1)S(1)}, u32[]{:S(2)}, u32[]{:S(2)}) collective-permute-start(bf16[80,1152]{1,0:T(8,128)(2,1)S(1)} %get-tuple-element.32.refs_0_), channel_id=1, source_target_pairs={{0,16},{1,17},{2,18},{3,19},{4,20},{5,21},{6,22},{7,23},{8,24},{9,... | collective-permute-start | bytes 552968 | tf_op jit(solution)/shard_map/ppermute | solution.py:383
  9.2 10.9 %collective-permute-start.15 = (bf16[80,1152]{1,0:T(8,128)(2,1)S(1)}, bf16[80,1152]{1,0:T(8,128)(2,1)S(1)}, u32[]{:S(2)}, u32[]{:S(2)}) collective-permute-start(bf16[80,1152]{1,0:T(8,128)(2,1)S(1)} %get-tuple-element.32.refs_0_), channel_id=1, source_target_pairs={{0,1},{1,0},{2,3},{3,2},{4,5},{5,4},{6,7},{7,6},{8,9},{9,8},{10,11... | collective-permute-start | bytes 552968 | tf_op jit(solution)/shard_map/ppermute | solution.py:383
  13.6 8.0 %collective-permute-start.7 = (bf16[80,1152]{1,0:T(8,128)(2,1)S(1)}, bf16[80,1152]{1,0:T(8,128)(2,1)S(1)}, u32[]{:S(2)}, u32[]{:S(2)}) collective-permute-start(bf16[80,1152]{1,0:T(8,128)(2,1)S(1)} %collective-permute-done.5.refs_0_), channel_id=1, source_target_pairs={{0,16},{1,17},{2,18},{3,19},{4,20},{5,21},{6,22},{7,23},{8,24},{9,... | collective-permute-start | bytes 552968 | tf_op jit(solution)/shard_map/ppermute | solution.py:383
  15.3 7.0 %collective-permute-start.6 = (bf16[80,1152]{1,0:T(8,128)(2,1)S(1)}, bf16[80,1152]{1,0:T(8,128)(2,1)S(1)}, u32[]{:S(2)}, u32[]{:S(2)}) collective-permute-start(bf16[80,1152]{1,0:T(8,128)(2,1)S(1)} %collective-permute-done.5.refs_0_), channel_id=1, source_target_pairs={{0,1},{1,0},{2,3},{3,2},{4,5},{5,4},{6,7},{7,6},{8,9},{9,8},{10,11... | collective-permute-start | bytes 552968 | tf_op jit(solution)/shard_map/ppermute | solution.py:383
  16.8 7.4 %collective-permute-start.10 = (bf16[80,1152]{1,0:T(8,128)(2,1)S(1)}, bf16[80,1152]{1,0:T(8,128)(2,1)S(1)}, u32[]{:S(2)}, u32[]{:S(2)}) collective-permute-start(bf16[80,1152]{1,0:T(8,128)(2,1)S(1)} %get-tuple-element.29), channel_id=1, source_target_pairs={{0,6},{1,7},{2,4},{3,5},{4,2},{5,3},{6,0},{7,1},{8,14},{9,15},{10,... | collective-permute-start | bytes 552968 | tf_op jit(solution)/shard_map/ppermute | solution.py:383
  20.1 9.5 %collective-permute-start.1 = (bf16[80,1152]{1,0:T(8,128)(2,1)S(1)}, bf16[80,1152]{1,0:T(8,128)(2,1)S(1)}, u32[]{:S(2)}, u32[]{:S(2)}) collective-permute-start(bf16[80,1152]{1,0:T(8,128)(2,1)S(1)} %collective-permute-done.refs_0_), channel_id=1, source_target_pairs={{0,1},{1,0},{2,3},{3,2},{4,5},{5,4},{6,7},{7,6},{8,9},{9,8},{10,11... | collective-permute-start | bytes 552968 | tf_op jit(solution)/shard_map/ppermute | solution.py:383
  21.6 9.5 %collective-permute-start.17 = (bf16[48,1152]{1,0:T(8,128)(2,1)S(1)}, bf16[48,1152]{1,0:T(8,128)(2,1)S(1)}, u32[]{:S(2)}, u32[]{:S(2)}) collective-permute-start(bf16[48,1152]{1,0:T(8,128)(2,1)S(1)} %slice.110), channel_id=1, source_target_pairs={{0,1},{1,0},{2,3},{3,2},{4,5},{5,4},{6,7},{7,6},{8,9},{9,8},{10,11... | collective-permute-start | bytes 331784 | tf_op jit(solution)/shard_map/ppermute | solution.py:383
  22.2 7.6 %collective-permute-start.18 = (bf16[32,1152]{1,0:T(8,128)(2,1)S(1)}, bf16[32,1152]{1,0:T(8,128)(2,1)S(1)}, u32[]{:S(2)}, u32[]{:S(2)}) collective-permute-start(bf16[32,1152]{1,0:T(8,128)(2,1)S(1)} %slice.111), channel_id=1, source_target_pairs={{0,16},{1,17},{2,18},{3,19},{4,20},{5,21},{6,22},{7,23},{8,24},{9,... | collective-permute-start | bytes 221192 | tf_op jit(solution)/shard_map/ppermute | solution.py:383
  24.2 9.2 %collective-permute-start.8 = (bf16[32,1152]{1,0:T(8,128)(2,1)S(1)}, bf16[32,1152]{1,0:T(8,128)(2,1)S(1)}, u32[]{:S(2)}, u32[]{:S(2)}) collective-permute-start(bf16[32,1152]{1,0:T(8,128)(2,1)S(1)} %slice.106), channel_id=1, source_target_pairs={{0,1},{1,0},{2,3},{3,2},{4,5},{5,4},{6,7},{7,6},{8,9},{9,8},{10,11... | collective-permute-start | bytes 221192 | tf_op jit(solution)/shard_map/ppermute | solution.py:383
  25.2 9.9 %collective-permute-start.9 = (bf16[48,1152]{1,0:T(8,128)(2,1)S(1)}, bf16[48,1152]{1,0:T(8,128)(2,1)S(1)}, u32[]{:S(2)}, u32[]{:S(2)}) collective-permute-start(bf16[48,1152]{1,0:T(8,128)(2,1)S(1)} %slice.107), channel_id=1, source_target_pairs={{0,16},{1,17},{2,18},{3,19},{4,20},{5,21},{6,22},{7,23},{8,24},{9,... | collective-permute-start | bytes 331784 | tf_op jit(solution)/shard_map/ppermute | solution.py:383
  29.7 8.4 %collective-permute-start.12 = (bf16[80,1152]{1,0:T(8,128)(2,1)S(1)}, bf16[80,1152]{1,0:T(8,128)(2,1)S(1)}, u32[]{:S(2)}, u32[]{:S(2)}) collective-permute-start(bf16[80,1152]{1,0:T(8,128)(2,1)S(1)} %collective-permute-done.10.refs_0_), channel_id=1, source_target_pairs={{0,16},{1,17},{2,18},{3,19},{4,20},{5,21},{6,22},{7,23},{8,24},{9,... | collective-permute-start | bytes 552968 | tf_op jit(solution)/shard_map/ppermute | solution.py:383
  29.8 7.0 %collective-permute-start.3 = (bf16[48,1152]{1,0:T(8,128)(2,1)S(1)}, bf16[48,1152]{1,0:T(8,128)(2,1)S(1)}, u32[]{:S(2)}, u32[]{:S(2)}) collective-permute-start(bf16[48,1152]{1,0:T(8,128)(2,1)S(1)} %slice.104), channel_id=1, source_target_pairs={{0,1},{1,0},{2,3},{3,2},{4,5},{5,4},{6,7},{7,6},{8,9},{9,8},{10,11... | collective-permute-start | bytes 331784 | tf_op jit(solution)/shard_map/ppermute | solution.py:383
  35.1 16.5 %collective-permute-start.19 = (bf16[2,4,320,128]{3,2,1,0:T(8,128)(2,1)S(1)}, bf16[2,4,320,128]{3,2,1,0:T(8,128)(2,1)S(1)}, u32[]{:S(2)}, u32[]{:S(2)}) collective-permute-start(bf16[2,4,320,128]{3,2,1,0:T(8,128)(2,1)S(1)} %get-tuple-element.33.refs_2_), channel_id=1, source_target_pairs={{0,8},{1,9},{2,10},{3,11},{4,12},{5,13},{6,14},{7,15},{8,0},{9,1},... | collective-permute-start | bytes 1966088 | tf_op jit(solution)/shard_map/ppermute | solution.py:383
  36.2 15.3 %collective-permute-start.20 = (bf16[2,4,320,128]{3,2,1,0:T(8,128)(2,1)S(1)}, bf16[2,4,320,128]{3,2,1,0:T(8,128)(2,1)S(1)}, u32[]{:S(2)}, u32[]{:S(2)}) collective-permute-start(bf16[2,4,320,128]{3,2,1,0:T(8,128)(2,1)S(1)} %get-tuple-element.34.refs_4_), channel_id=1, source_target_pairs={{0,8},{1,9},{2,10},{3,11},{4,12},{5,13},{6,14},{7,15},{8,0},{9,1},... | collective-permute-start | bytes 1966088 | tf_op jit(solution)/shard_map/ppermute | solution.py:383
  37.9 13.6 %collective-permute-start.21 = (bf16[2,4,320,128]{3,2,1,0:T(8,128)(2,1)S(1)}, bf16[2,4,320,128]{3,2,1,0:T(8,128)(2,1)S(1)}, u32[]{:S(2)}, u32[]{:S(2)}) collective-permute-start(bf16[2,4,320,128]{3,2,1,0:T(8,128)(2,1)S(1)} %get-tuple-element.35.refs_6_), channel_id=1, source_target_pairs={{0,8},{1,9},{2,10},{3,11},{4,12},{5,13},{6,14},{7,15},{8,0},{9,1},... | collective-permute-start | bytes 1966088 | tf_op jit(solution)/shard_map/ppermute | solution.py:383
  40.0 11.6 %collective-permute-start.22 = (bf16[2,4,240,128]{3,2,1,0:T(8,128)(2,1)S(1)}, bf16[2,4,240,128]{3,2,1,0:T(8,128)(2,1)S(1)}, u32[]{:S(2)}, u32[]{:S(2)}) collective-permute-start(bf16[2,4,240,128]{3,2,1,0:T(8,128)(2,1)S(1)} %get-tuple-element.36.refs_8_), channel_id=1, source_target_pairs={{0,8},{1,9},{2,10},{3,11},{4,12},{5,13},{6,14},{7,15},{8,0},{9,1},... | collective-permute-start | bytes 1474568 | tf_op jit(solution)/shard_map/ppermute | solution.py:383
  71.3 10.2 %collective-permute-start.24 = (bf16[4,192,128]{2,1,0:T(8,128)(2,1)S(1)}, bf16[4,192,128]{2,1,0:T(8,128)(2,1)S(1)}, u32[]{:S(2)}, u32[]{:S(2)}) collective-permute-start(bf16[4,192,128]{2,1,0:T(8,128)(2,1)S(1)} %get-tuple-element.41), channel_id=1, source_target_pairs={{0,2},{1,3},{2,0},{3,1},{4,6},{5,7},{6,4},{7,5},{8,10},{9,11},{10,... | collective-permute-start | bytes 589832 | tf_op jit(solution)/shard_map/ppermute | solution.py:383
  73.2 17.1 %collective-permute-start.25 = (bf16[4,192,128]{2,1,0:T(8,128)(2,1)S(1)}, bf16[4,192,128]{2,1,0:T(8,128)(2,1)S(1)}, u32[]{:S(2)}, u32[]{:S(2)}) collective-permute-start(bf16[4,192,128]{2,1,0:T(8,128)(2,1)S(1)} %get-tuple-element.42), channel_id=1, source_target_pairs={{0,4},{1,5},{2,6},{3,7},{4,0},{5,1},{6,2},{7,3},{8,12},{9,13},{10,... | collective-permute-start | bytes 589832 | tf_op jit(solution)/shard_map/ppermute | solution.py:383
  73.9 18.7 %collective-permute-start.29 = (bf16[4,192,128]{2,1,0:T(8,128)(2,1)S(1)}, bf16[4,192,128]{2,1,0:T(8,128)(2,1)S(1)}, u32[]{:S(2)}, u32[]{:S(2)}) collective-permute-start(bf16[4,192,128]{2,1,0:T(8,128)(2,1)S(1)} %get-tuple-element.39), channel_id=1, source_target_pairs={{0,6},{1,7},{2,4},{3,5},{4,2},{5,3},{6,0},{7,1},{8,14},{9,15},{10,... | collective-permute-start | bytes 589832 | tf_op jit(solution)/shard_map/ppermute | solution.py:383
  90.4 13.4 %collective-permute-start.26 = (bf16[2,192,128]{2,1,0:T(8,128)(2,1)S(1)}, bf16[2,192,128]{2,1,0:T(8,128)(2,1)S(1)}, u32[]{:S(2)}, u32[]{:S(2)}) collective-permute-start(bf16[2,192,128]{2,1,0:T(8,128)(2,1)S(1)} %pad_maximum_fusion.1), channel_id=1, source_target_pairs={{0,1},{1,0},{2,3},{3,2},{4,5},{5,4},{6,7},{7,6},{8,9},{9,8},{10,11... | collective-permute-start | bytes 294920 | tf_op jit(solution)/shard_map/ppermute | solution.py:383
  91.7 12.1 %collective-permute-start.27 = (bf16[2,192,128]{2,1,0:T(8,128)(2,1)S(1)}, bf16[2,192,128]{2,1,0:T(8,128)(2,1)S(1)}, u32[]{:S(2)}, u32[]{:S(2)}) collective-permute-start(bf16[2,192,128]{2,1,0:T(8,128)(2,1)S(1)} %pad_maximum_fusion.2), channel_id=1, source_target_pairs={{0,16},{1,17},{2,18},{3,19},{4,20},{5,21},{6,22},{7,23},{8,24},{9,... | collective-permute-start | bytes 294920 | tf_op jit(solution)/shard_map/ppermute | solution.py:383
  93.7 6.1 %collective-permute-start.31 = (bf16[2,192,128]{2,1,0:T(8,128)(2,1)S(1)}, bf16[2,192,128]{2,1,0:T(8,128)(2,1)S(1)}, u32[]{:S(2)}, u32[]{:S(2)}) collective-permute-start(bf16[2,192,128]{2,1,0:T(8,128)(2,1)S(1)} %pad_maximum_fusion.6), channel_id=1, source_target_pairs={{0,16},{1,17},{2,18},{3,19},{4,20},{5,21},{6,22},{7,23},{8,24},{9,... | collective-permute-start | bytes 294920 | tf_op jit(solution)/shard_map/ppermute | solution.py:383
  (15 other events, 276.4 us)
